TPU v7x, 256 devices: a whole 4x4x8 slice. The times are simulated.
256 devices in a mesh: row: 32 (over z_lo, x, core), col: 8 (over z_hi, y).
Axes of the slice: x: 4, y: 4, z: 8 (z_hi: 2, z_lo: 4; z = z_hi * 4 + z_lo), core: 2. Of those that a mesh axis runs over, the one named last changes fastest.
Arguments:
- ancestors: bfloat16 [128, 128, 256, 256], P('row', 'col'), may hold values from -6 to 6
- panel_one: bfloat16 [2, 128, 256, 256], P(None, 'row'), may hold values from -0.0625 to 0.0625
- present_one: int32 [2, 128], replicated, may hold values from 0 to 1, as said below
- dinv_one: bfloat16 [2, 256, 256], replicated, may hold values from -6 to 6
- panel_two: bfloat16 [2, 128, 256, 256], P(None, 'row'), may hold values from -0.0625 to 0.0625
- present_two: int32 [2, 128], replicated, may hold values from 0 to 1, as said below
- dinv_two: bfloat16 [2, 256, 256], replicated, may hold values from -6 to 6
Outputs:
- update_one: float32 [256, 256, 256], P(('row', 'col'))
- diag_one: float32 [2, 256, 256], replicated
- update_two: float32 [256, 256, 256], P(('row', 'col'))
- diag_two: float32 [2, 256, 256], replicated
Inputs may be any that keep to these rules, and one draw needn't show every extreme that they name: `present_one`: each supernode's row has 16 to 64 ones, block row 0 among them; the first supernode of each level has exactly 64. `present_two`: each supernode's row has 16 to 64 ones, block row 0 among them; the first supernode of each level has exactly 64.
All inputs are finite; a program needn't handle non-finite values.
Results may differ from a plain program's by a relative error of at most 0.0003.
Values may be sent and summed in bfloat16 or wider, within the bound.
No kernel may reach another device: no remote copies, remote signals or barrier semaphores. Data moves between devices by JAX's collectives and lax.ppermute only.
A program may use at most 128 MiB of HBM per device.

v0:
```python
import jax
import jax.numpy as jnp
from jax import lax
from jax.sharding import PartitionSpec as P


def spread(block, axis, holder):
    block = jnp.where(lax.axis_index(axis) == holder, block, jnp.zeros_like(block))
    return lax.psum(block, axis)


def one_level(ancestors, panel_part, present, inv_diag):
    a_row = ancestors.shape[0]
    a_col = ancestors.shape[1]
    block_size = ancestors.shape[2]
    count_s = panel_part.shape[0]
    row_at = lax.axis_index("row")
    col_at = lax.axis_index("col")
    root_count = a_col // a_row
    pieces = []
    for offset in range(root_count):
        pieces.append(spread(panel_part, "row", col_at * root_count + offset))
    column_panel = jnp.concatenate(pieces, axis=1)
    col_mask = lax.dynamic_slice_in_dim(present, col_at * a_col, a_col, 1)
    row_mask = lax.dynamic_slice_in_dim(present, row_at * a_row, a_row, 1)
    masked = column_panel * col_mask[:, :, None, None].astype(jnp.bfloat16)
    partial_sums = jnp.einsum(
        "ijab,kjbc->ikac", ancestors, masked, preferred_element_type=jnp.float32
    )
    term_blocks = -partial_sums * jnp.transpose(row_mask).astype(jnp.float32)[:, :, None, None]
    flat_terms = term_blocks.reshape(a_row * count_s, block_size, block_size)
    owned_blocks = lax.psum_scatter(flat_terms, "col", scatter_dimension=0, tiled=True)
    panel_flat = jnp.transpose(panel_part, (1, 0, 2, 3)).reshape(
        a_row * count_s, block_size, block_size
    )
    owned_count = owned_blocks.shape[0]
    first_row = col_at * owned_count
    panel_own = lax.dynamic_slice_in_dim(panel_flat, first_row, owned_count, 0)
    products = jnp.einsum(
        "nba,nbc->nac", panel_own.astype(jnp.float32), owned_blocks, precision=lax.Precision.HIGHEST
    )
    sup_index = (first_row + jnp.arange(owned_count, dtype=jnp.int32)) % count_s
    one_hot_rows = (sup_index[:, None] == jnp.arange(count_s, dtype=jnp.int32)[None, :]).astype(
        jnp.float32
    )
    diag_terms = jnp.einsum("nk,nac->kac", one_hot_rows, products, precision=lax.Precision.HIGHEST)
    diag_total = lax.psum(diag_terms, ("row", "col"))
    return (owned_blocks, inv_diag.astype(jnp.float32) - diag_total)


def body(ancestors, panel_one, present_one, dinv_one, panel_two, present_two, dinv_two):
    update_one, diag_one = one_level(ancestors, panel_one, present_one, dinv_one)
    update_two, diag_two = one_level(ancestors, panel_two, present_two, dinv_two)
    return (update_one, diag_one, update_two, diag_two)


def solution(mesh):
    in_specs = (
        P("row", "col", None, None),
        P(None, "row", None, None),
        P(),
        P(),
        P(None, "row", None, None),
        P(),
        P(),
    )
    out_specs = (P(("row", "col"), None, None), P(), P(("row", "col"), None, None), P())
    return jax.shard_map(body, mesh=mesh, in_specs=in_specs, out_specs=out_specs, check_vma=False)
```

profile of v0, /device:TPU:1, one launch (start us, length us, event | category | flops | bytes accessed | tf_op | source)
XLA Modules:
  0.0 787.0 jit_solution(2082607152326001342)
XLA Ops:
  7.2 0.0 all-reduce.7.cloned.1.call-start
  7.2 4.8 broadcast_select_fusion.6
  12.1 0.0 all-reduce.7.cloned.1.call-update
  12.1 0.0 reduce-scatter.5.cloned.1.call-start
  12.1 0.6 copy-done.4
  12.7 0.1 fusion.40
  12.8 0.1 fusion.42
  12.9 304.8 %all-reduce.7.cloned.1.call-done = (bf16[2,4,256,256]{3,2,1,0:T(8,128)(2,1)}, bf16[2,4,256,256]{3,2,1,0:T(8,128)(2,1)}, bf16[2,4,256,256]{3,2,1,0:T(8,128)(2,1)}...) async-done(((bf16[2,4,256,256]{3,2,1,0:T(8,128)(2,1)}, ...) | async-done | bytes 8388624 | tf_op jit(solution)/shard_map/psum | solution.py:9
  317.7 10.0 %bitcast_multiply_fusion = f32[4,2,256,256]{2,3,0,1:T(8,128)S(1)} fusion(bf16[4,16,256,256]{3,2,1,0:T(8,128)(2,1)} %param.7, bf16[2,4,256,256]{3,2,1,0:T(8,128)(2,1)} %get-tuple-element.10, bf16[2,4,256,256]{3,2,1,0:T(8,128)(2,1)} %get-tuple-element.11, bf16[2,4,256,256]{3,2,1,0:T(8,128)(2,1)} %get-tuple-element.12, ...), kind=kOutput, calls=%fused_computation.20 | convolution fusion | flops 4316987392 | bytes 14680160 | tf_op jit(solution)/shard_map/ijab,kjbc->ikac/dot_general | solution.py:27
  327.7 1.8 copy.17
  329.6 0.0 reduce-scatter.3.cloned.1.call-start
  329.6 11.3 %bitcast_multiply_fusion.1 = f32[4,2,256,256]{2,3,0,1:T(8,128)} fusion(bf16[4,16,256,256]{3,2,1,0:T(8,128)(2,1)} %param.7, bf16[2,4,256,256]{3,2,1,0:T(8,128)(2,1)S(1)} %copy-done.6, bf16[2,4,256,256]{3,2,1,0:T(8,128)(2,1)} %get-tuple-element.7, bf16[2,4,256,256]{3,2,1,0:T(8,128)(2,1)} %get-tuple-element.8, bf16[2,4,256,256]{3,2,1,0:T(8,128)(2,1)} %get-tuple-element.9, ...), kind=kOutput, calls=%fused_computation.22 | convolution fusion | flops 4316987392 | bytes 14680160 | tf_op jit(solution)/shard_map/ijab,kjbc->ikac/dot_general | solution.py:27
  341.0 3.1 copy.14
  344.1 0.0 all-reduce.5.cloned.1.call-start
  344.2 0.1 copy.18
  344.2 0.1 copy.15
  344.4 78.4 %reduce-scatter.5.cloned.1.call-done = f32[1,256,256]{2,1,0:T(8,128)} async-done(((f32[8,256,256]{2,1,0:T(8,128)}), f32[1,256,256]{2,1,0:T(8,128)}) %reduce-scatter.5.cloned.1.call-update) | async-done | bytes 262160 | tf_op jit(solution)/shard_map/reduce_scatter | solution.py:32
  422.8 1.3 fusion.30
  424.0 94.8 %reduce-scatter.3.cloned.1.call-done = f32[1,256,256]{2,1,0:T(8,128)} async-done(((f32[8,256,256]{2,1,0:T(8,128)}), f32[1,256,256]{2,1,0:T(8,128)}) %reduce-scatter.3.cloned.1.call-update) | async-done | bytes 262160 | tf_op jit(solution)/shard_map/reduce_scatter | solution.py:32
  518.8 1.3 fusion.32
  520.1 1.1 broadcast_multiply_fusion
  521.2 255.5 %all-reduce.5.cloned.1.call-done = (f32[2,256,256]{2,1,0:T(8,128)}, f32[2,256,256]{2,1,0:T(8,128)}) async-done(((f32[2,256,256]{2,1,0:T(8,128)}, f32[2,256,256]{2,1,0:T(8,128)}), (f32[2,256,256]{2,1,0:T(8,128)}, f32[2,256,256]{2,1,0:T(8,128)})) %all-reduce.5.cloned.1.call-update) | async-done | bytes 1048592 | tf_op jit(solution)/shard_map/psum | solution.py:47
  776.7 1.9 convert_subtract_fusion
  778.6 1.9 convert_subtract_fusion.1
  (17 shorter events, 0.1 us)
Async XLA Ops:
  7.2 310.6 %all-reduce.7.cloned.1.call-start = ((), (), s32[]{:S(2)}) async-start(), calls=%async_computation.5 | async-start | bytes 16777216 | tf_op jit(solution)/shard_map/psum | solution.py:9
  12.0 0.7 copy-start.4
  12.0 0.7 copy-start.5
  12.1 410.7 %reduce-scatter.5.cloned.1.call-start = ((), (), s32[]{:S(2)}) async-start(), calls=%async_computation.3 | async-start | bytes 2359296 | tf_op jit(solution)/shard_map/reduce_scatter | solution.py:32
  327.7 1.9 copy-start.6
  329.6 189.2 %reduce-scatter.3.cloned.1.call-start = ((), (), s32[]{:S(2)}) async-start(), calls=%async_computation.2 | async-start | bytes 2359296 | tf_op jit(solution)/shard_map/reduce_scatter | solution.py:32
  341.0 3.2 copy-start
  341.0 3.3 copy-start.1
  344.1 432.6 %copy-start.2 = (bf16[2,256,256]{2,1,0:T(8,128)(2,1)S(1)}, bf16[2,256,256]{2,1,0:T(8,128)(2,1)}, u32[]{:S(2)}) copy-start(bf16[2,256,256]{2,1,0:T(8,128)(2,1)} %param.13) | copy-start | bytes 786436
  344.1 432.6 %all-reduce.5.cloned.1.call-start = ((), (), s32[]{:S(2)}) async-start(), calls=%async_computation.4 | async-start | bytes 2097152 | tf_op jit(solution)/shard_map/psum | solution.py:47
  344.3 434.3 %copy-start.3 = (bf16[2,256,256]{2,1,0:T(8,128)(2,1)S(1)}, bf16[2,256,256]{2,1,0:T(8,128)(2,1)}, u32[]{:S(2)}) copy-start(bf16[2,256,256]{2,1,0:T(8,128)(2,1)} %param.10) | copy-start | bytes 786436
Sparse Core Ops, SparseCore 0:
  12.2 305.4 all-reduce.6
  329.7 93.0 reduce-scatter.4
  427.9 90.8 reduce-scatter.2
  524.9 251.7 all-reduce.4
where the time goes:
time: 788 us; the launch traced here: 787 us
  waiting for transfers between devices  734 us (93%)
  matrix products  23.8 us (3%)
  between operations  13.9 us (2%)
  other arithmetic  9.86 us (1%)
    psum x1, waiting for transfers between devices, spread(): return lax.psum(block, axis)  305 us
    psum x1, waiting for transfers between devices, one_level(): diag_total = lax.psum(diag_terms, ('row', 'col'))  255 us
    reduce_scatter x2, waiting for transfers between devices, one_level(): lax.psum_scatter(flat_terms, 'col', scatter_dimension=0, tiled=True)  173 us
    dot_general x2, matrix products, one_level(): jnp.einsum('ijab,kjbc->ikac', ancestors, masked, preferred_element_type=j...  21.3 us
  transfers between devices with their start and end apart: 4, of which 4 were waited for; matrix products, arithmetic and copies ran while one was open for 2% of the time, Pallas kernels for 0%

commit v1 on v0

v1 whole, which is shorter than its diff:
```python
import functools

import jax
import jax.numpy as jnp
from jax import lax
from jax.experimental import pallas as pl
from jax.experimental.pallas import tpu as pltpu
from jax.sharding import PartitionSpec as P

F32 = jnp.float32
BF16 = jnp.bfloat16
SEND = jnp.float16
AXES = ("row", "col")


def split_id(dev):
    row, col = dev // 8, dev % 8
    return row // 8, (row // 2) % 4, row % 2, col // 4, col % 4


def join_id(zl, x, core, zh, y):
    return ((zl * 4 + x) * 2 + core) * 8 + zh * 4 + y


def send(value, where):
    pairs = [(dev, join_id(*where(*split_id(dev)))) for dev in range(256)]
    return lax.ppermute(value, AXES, pairs)


def to_core(value):
    return send(value, lambda zl, x, core, zh, y: (zl, x, core ^ 1, zh, y))


def to_x(value, k):
    return send(value, lambda zl, x, core, zh, y: (zl, x ^ k, core, zh, y))


def to_zl(value, k):
    return send(value, lambda zl, x, core, zh, y: (zl ^ k, x, core, zh, y))


def to_y(value, k):
    return send(value, lambda zl, x, core, zh, y: (zl, x, core, zh, y ^ k))


def to_zh(value):
    return send(value, lambda zl, x, core, zh, y: (zl, x, core, zh ^ 1, y))


def to_plane(value):
    return send(
        value,
        lambda zl, x, core, zh, y: (y, 2 * (x % 2) + zh, core, zl // 2, 2 * (zl % 2) + x // 2),
    )


def product_kernel(scal, a_ref, p0, p1, p2, p3, d_ref, out_ref, diag_ref):
    step = pl.program_id(0)
    pieces = (p0, p1, p2, p3)
    low = scal[24] & 1

    @pl.when(step == 0)
    def _():
        diag_ref[...] = jnp.zeros_like(diag_ref)

    for k in range(2):
        acc = jnp.zeros((256, 256), F32)
        for pos in range(16):
            block = a_ref[0, scal[pos]]
            acc += jnp.dot(block, pieces[pos // 4][pos % 4, k], preferred_element_type=F32)
        term = acc * (-scal[16 + 2 * step + k]).astype(F32)
        out_ref[k ^ low, 0] = term
        high = term.astype(BF16)
        rest = (term - high.astype(F32)).astype(BF16)
        left = d_ref[k, 0]
        dims = (((0,), (0,)), ((), ()))
        diag_ref[k] += lax.dot_general(left, high, dims, preferred_element_type=F32)
        diag_ref[k] += lax.dot_general(left, rest, dims, preferred_element_type=F32)


def products(scal, blocks, pieces, left):
    whole = lambda i, s: (0, 0, 0, 0)
    return pl.pallas_call(
        product_kernel,
        grid_spec=pltpu.PrefetchScalarGridSpec(
            num_scalar_prefetch=1,
            grid=(4,),
            in_specs=[
                pl.BlockSpec((1, 16, 256, 256), lambda i, s: (i, 0, 0, 0)),
                pl.BlockSpec((4, 2, 256, 256), whole),
                pl.BlockSpec((4, 2, 256, 256), whole),
                pl.BlockSpec((4, 2, 256, 256), whole),
                pl.BlockSpec((4, 2, 256, 256), whole),
                pl.BlockSpec((2, 1, 256, 256), lambda i, s: (0, i, 0, 0)),
            ],
            out_specs=[
                pl.BlockSpec(
                    (2, 1, 256, 256),
                    lambda i, s: ((i % 2) ^ (s[24] // 2), (i // 2) ^ s[25], 0, 0),
                ),
                pl.BlockSpec((2, 256, 256), lambda i, s: (0, 0, 0)),
            ],
        ),
        out_shape=[
            jax.ShapeDtypeStruct((4, 2, 256, 256), F32),
            jax.ShapeDtypeStruct((2, 256, 256), F32),
        ],
        compiler_params=pltpu.CompilerParams(
            dimension_semantics=("arbitrary",), vmem_limit_bytes=48 * 2**20
        ),
    )(scal, blocks, *pieces, left)


def body(ancestors, panel_one, present_one, dinv_one, panel_two, present_two, dinv_two):
    row = lax.axis_index("row")
    col = lax.axis_index("col")
    zl, x, core = row // 8, (row // 2) % 4, row % 2
    zh, y = col // 4, col % 4
    first = core == 0

    with jax.named_scope("swap"):
        other_blocks = to_core(ancestors)
        rows_one = lax.dynamic_slice_in_dim(present_one, 4 * row, 4, 1)
        rows_two = lax.dynamic_slice_in_dim(present_two, 4 * row, 4, 1)
        masked_one = panel_one * rows_one[:, :, None, None].astype(BF16)
        masked_two = panel_two * rows_two[:, :, None, None].astype(BF16)
        mine = jnp.where(first, masked_one, masked_two)
        theirs = to_core(jnp.where(first, masked_two, masked_one))

    with jax.named_scope("gather"):
        pick = jnp.where(zh == core, mine, theirs)
        own = lax.dynamic_slice_in_dim(pick, y, 1, 1)[:, 0]
        own = to_plane(own)
        line = jnp.stack([own] + [to_zl(own, k) for k in (1, 2, 3)])
        pieces = [line] + [to_x(line, k) for k in (1, 2, 3)]

    present = jnp.where(first, present_one, present_two)
    order = jnp.array([[m, k] for m in range(4) for k in range(4)], jnp.int32)
    where = 4 * (x ^ order[:, 0]) + (zl ^ order[:, 1])

    def table(rows_of):
        live = lax.dynamic_slice_in_dim(present, 4 * rows_of, 4, 1)
        return jnp.concatenate(
            [where, jnp.transpose(live).reshape(8), jnp.stack([y, zh])]
        ).astype(jnp.int32)

    with jax.named_scope("product"):
        near, diag_near = products(table(row), ancestors, pieces, mine)
        far, diag_far = products(table(row ^ 1), other_blocks, pieces, theirs)

    def column(terms):
        total = terms[0]
        got = [to_y(terms[k].astype(SEND), k) for k in (1, 2, 3)]
        for value in got:
            total = total + value.astype(F32)
        return total[0] + to_zh(total[1])

    with jax.named_scope("near"):
        near = column(near)
    with jax.named_scope("far"):
        far = to_core(column(far))
    update_one = jnp.where(first, near, far)[None]
    update_two = jnp.where(first, far, near)[None]

    with jax.named_scope("diag"):
        diag = (diag_near + diag_far).reshape(4, 2, 64, 256)
        at = lambda k: lax.dynamic_index_in_dim(diag, y ^ k, 0, keepdims=False)
        part = at(0)
        for value in [to_y(at(k), k) for k in (1, 2, 3)]:
            part = part + value
        half = lambda k: lax.dynamic_index_in_dim(part, zh ^ k, 0, keepdims=False)
        piece = half(0) + to_zh(half(1))
        one, two, three = [to_x(piece, k) for k in (1, 2, 3)]
        piece = (piece + one) + (two + three)
        one, two, three = [to_zl(piece, k) for k in (1, 2, 3)]
        total = (piece + one) + (two + three)
        back = to_zh(total)
        pair = jnp.where(zh == 0, jnp.stack([total, back]), jnp.stack([back, total]))
        quarters = [pair] + [to_y(pair, k) for k in (1, 2, 3)]
        stack = jnp.stack(quarters)
        ordered = jnp.stack(
            [lax.dynamic_index_in_dim(stack, y ^ k, 0, keepdims=False) for k in range(4)]
        )
        whole = ordered.reshape(2, 256, 256)
        partner = to_core(whole)
        total_one = jnp.where(first, whole, partner)
        total_two = jnp.where(first, partner, whole)

    return (
        update_one,
        dinv_one.astype(F32) - total_one,
        update_two,
        dinv_two.astype(F32) - total_two,
    )


def solution(mesh):
    in_specs = (
        P("row", "col", None, None),
        P(None, "row", None, None),
        P(),
        P(),
        P(None, "row", None, None),
        P(),
        P(),
    )
    out_specs = (P(("row", "col"), None, None), P(), P(("row", "col"), None, None), P())
    return jax.shard_map(body, mesh=mesh, in_specs=in_specs, out_specs=out_specs, check_vma=False)
```

time: 788 us -> 227 us (0.29)
  waiting for transfers between devices: 734 us -> 98.3 us
  starting transfers between devices: 0.16 us -> 83 us
  Pallas kernels: 0 us -> 30.3 us
  matrix products: 23.8 us -> 0 us
  between operations: 13.9 us -> 0.95 us
    psum x2 -> x0, waiting for transfers between devices: 560 us -> none  [the longest x1 305 us: spread(): return lax.psum(block, axis)]
    reduce_scatter x2 -> x0, waiting for transfers between devices: 173 us -> none  [one_level(): lax.psum_scatter(flat_terms, 'col', scatter_dimension=0, tiled=True)]
    ppermute x0 -> x33, waiting for transfers between devices: none -> 98.3 us  [send(): return lax.ppermute(value, AXES, pairs)]
    ppermute x0 -> x33, starting transfers between devices: none -> 83 us  [send(): return lax.ppermute(value, AXES, pairs)]
    pallas_call x0 -> x2, Pallas kernels: none -> 30.3 us  [products(): pl.pallas_call(product_kernel, grid_spec=pltpu.PrefetchScalarGridSpec(num...]
    dot_general x4 -> x0, matrix products: 23.8 us -> none  [the longest x2 21.3 us: one_level(): jnp.einsum('ijab,kjbc->ikac', ancestors, masked, preferred_element_type=j...]
  transfers between devices with their start and end apart: 4 -> 33, of which waited for: 4 -> 16; matrix products, arithmetic and copies ran while one was open for 2% -> 3% of each run, Pallas kernels for 0% -> 7%
where the time goes in v1:
time: 227 us; the launch traced here: 223 us
  waiting for transfers between devices  98.3 us (43%)
  starting transfers between devices  83 us (37%)
  Pallas kernels  30.3 us (13%)
  other arithmetic  7.47 us (3%)
  local copies, waits for them, and re-layouts  3.25 us (1%)
    ppermute x33, waiting for transfers between devices, send(): return lax.ppermute(value, AXES, pairs)  98.3 us
    ppermute x33, starting transfers between devices, send(): return lax.ppermute(value, AXES, pairs)  83 us
    pallas_call x2, Pallas kernels, products(): pl.pallas_call(product_kernel, grid_spec=pltpu.PrefetchScalarGridSpec(num...  30.3 us
  transfers between devices with their start and end apart: 33, of which 16 were waited for; matrix products, arithmetic and copies ran while one was open for 3% of the time, Pallas kernels for 7%

profile of v1, /device:TPU:1, one launch (start us, length us, event | category | flops | bytes accessed | tf_op | source)
XLA Modules:
  0.0 223.3 jit_solution(2687173072927544972)
XLA Ops:
  0.6 3.3 %collective-permute-start.12 = (bf16[4,16,256,256]{3,2,1,0:T(8,128)(2,1)}, bf16[4,16,256,256]{3,2,1,0:T(8,128)(2,1)}, u32[]{:S(2)}, u32[]{:S(2)}) collective-permute-start(bf16[4,16,256,256]{3,2,1,0:T(8,128)(2,1)} %a_ref.1), channel_id=1, source_target_pairs={{0,8},{1,9},{2,10},{3,11},{4,12},{5,13},{6,14},{7,15},{8,0},{9,1},... | collective-permute-start | bytes 25165832 | tf_op jit(solution)/shard_map/swap/ppermute | solution.py:27
  6.7 11.5 %collective-permute-done.d_ref = bf16[2,4,256,256]{3,2,1,0:T(8,128)(2,1)S(1)} collective-permute-done((bf16[2,4,256,256]{3,2,1,0:T(8,128)(2,1)S(1)}, bf16[2,4,256,256]{3,2,1,0:T(8,128)(2,1)S(1)}, u32[]{:S(2)}, u32[]{:S(2)}) %collective-permute-start) | collective-permute-done | bytes 1048608 | tf_op jit(solution)/shard_map/swap/ppermute | solution.py:27
  19.9 22.6 %collective-permute-start.4 = (bf16[2,256,256]{2,1,0:T(8,128)(2,1)S(1)}, bf16[2,256,256]{2,1,0:T(8,128)(2,1)S(1)}, u32[]{:S(2)}, u32[]{:S(2)}) collective-permute-start(bf16[2,256,256]{2,1,0:T(8,128)(2,1)S(1)} %collective-permute-done.1), channel_id=1, source_target_pairs={{0,192},{1,193},{2,194},{3,195},{4,196},{5,197},{6,198},{7,199},{8... | collective-permute-start | bytes 786440 | tf_op jit(solution)/shard_map/gather/ppermute | solution.py:27
  42.8 6.1 %collective-permute-done.4 = bf16[2,256,256]{2,1,0:T(8,128)(2,1)S(1)} collective-permute-done((bf16[2,256,256]{2,1,0:T(8,128)(2,1)S(1)}, bf16[2,256,256]{2,1,0:T(8,128)(2,1)S(1)}, u32[]{:S(2)}, u32[]{:S(2)}) %collective-permute-start.4) | collective-permute-done | bytes 262176 | tf_op jit(solution)/shard_map/gather/ppermute | solution.py:27
  49.0 11.6 %collective-permute-done.3 = bf16[2,256,256]{2,1,0:T(8,128)(2,1)S(1)} collective-permute-done((bf16[2,256,256]{2,1,0:T(8,128)(2,1)S(1)}, bf16[2,256,256]{2,1,0:T(8,128)(2,1)S(1)}, u32[]{:S(2)}, u32[]{:S(2)}) %collective-permute-start.3) | collective-permute-done | bytes 262176 | tf_op jit(solution)/shard_map/gather/ppermute | solution.py:27
  60.7 5.4 %collective-permute-start.5 = (bf16[4,2,256,256]{3,2,1,0:T(8,128)(2,1)S(1)}, bf16[4,2,256,256]{3,2,1,0:T(8,128)(2,1)S(1)}, u32[]{:S(2)}, u32[]{:S(2)}) collective-permute-start(bf16[4,2,256,256]{3,2,1,0:T(8,128)(2,1)S(1)} %pad_maximum_fusion.p0), channel_id=1, source_target_pairs={{0,16},{1,17},{2,18},{3,19},{4,20},{5,21},{6,22},{7,23},{8,24},{9,... | collective-permute-start | bytes 3145736 | tf_op jit(solution)/shard_map/gather/ppermute | solution.py:27
  66.1 3.9 %collective-permute-start.6 = (bf16[4,2,256,256]{3,2,1,0:T(8,128)(2,1)S(1)}, bf16[4,2,256,256]{3,2,1,0:T(8,128)(2,1)}, u32[]{:S(2)}, u32[]{:S(2)}) collective-permute-start(bf16[4,2,256,256]{3,2,1,0:T(8,128)(2,1)S(1)} %pad_maximum_fusion.p0), channel_id=1, source_target_pairs={{0,32},{1,33},{2,34},{3,35},{4,36},{5,37},{6,38},{7,39},{8,40},{9,... | collective-permute-start | bytes 3145736 | tf_op jit(solution)/shard_map/gather/ppermute | solution.py:27
  70.6 18.7 %collective-permute-done.5.p1 = bf16[4,2,256,256]{3,2,1,0:T(8,128)(2,1)S(1)} collective-permute-done((bf16[4,2,256,256]{3,2,1,0:T(8,128)(2,1)S(1)}, bf16[4,2,256,256]{3,2,1,0:T(8,128)(2,1)S(1)}, u32[]{:S(2)}, u32[]{:S(2)}) %collective-permute-start.5) | collective-permute-done | bytes 1048608 | tf_op jit(solution)/shard_map/gather/ppermute | solution.py:27
  89.3 25.9 %collective-permute-done.6.p2 = bf16[4,2,256,256]{3,2,1,0:T(8,128)(2,1)} collective-permute-done((bf16[4,2,256,256]{3,2,1,0:T(8,128)(2,1)S(1)}, bf16[4,2,256,256]{3,2,1,0:T(8,128)(2,1)}, u32[]{:S(2)}, u32[]{:S(2)}) %collective-permute-start.6) | collective-permute-done | bytes 1048608 | tf_op jit(solution)/shard_map/gather/ppermute | solution.py:27
  115.3 2.0 collective-permute-done.7.p3
  117.3 15.1 %product.2 = (f32[4,2,256,256]{3,2,1,0:T(8,128)}, f32[2,256,256]{2,1,0:T(8,128)S(1)}) custom-call(s32[26]{0:T(128)S(1)} %get-tuple-element.33.scal, bf16[4,16,256,256]{3,2,1,0:T(8,128)(2,1)} %a_ref.1, bf16[4,2,256,256]{3,2,1,0:T(8,128)(2,1)S(1)} %pad_maximum_fusion.p0, bf16[4,2,256,256]{3,2,1,0:T(8,128)(2,1)S(1)} %collective-permute-done.5.p1, ...), custom_call_target="tpu_custom_call" | custom-call | tf_op jit(solution)/shard_map/product/pallas_call | solution.py:83
  132.4 15.2 %product.3 = (f32[4,2,256,256]{3,2,1,0:T(8,128)}, f32[2,256,256]{2,1,0:T(8,128)S(1)}) custom-call(s32[26]{0:T(128)S(1)} %get-tuple-element.34.scal, bf16[4,16,256,256]{3,2,1,0:T(8,128)(2,1)} %collective-permute-done.12.a_ref, bf16[4,2,256,256]{3,2,1,0:T(8,128)(2,1)S(1)} %pad_maximum_fusion.p0, bf16[4,2,256,256]{3,2,1,0:T(8,128)(2,1)S(1)} %collective-permute-done.5.p1, ...), custom_call_target="tpu_custom_call" | custom-call | tf_op jit(solution)/shard_map/product/pallas_call | solution.py:83
  147.9 3.1 %collective-permute-start.18 = (f32[2,64,256]{2,1,0:T(8,128)S(1)}, f32[2,64,256]{2,1,0:T(8,128)S(1)}, u32[]{:S(2)}, u32[]{:S(2)}) collective-permute-start(f32[2,64,256]{2,1,0:T(8,128)S(1)} %get-tuple-element.28), channel_id=1, source_target_pairs={{0,1},{1,0},{2,3},{3,2},{4,5},{5,4},{6,7},{7,6},{8,9},{9,8},{10,11... | collective-permute-start | bytes 393224 | tf_op jit(solution)/shard_map/diag/ppermute | solution.py:27
  151.2 3.5 %collective-permute-done.20 = f32[2,64,256]{2,1,0:T(8,128)S(1)} collective-permute-done((f32[2,64,256]{2,1,0:T(8,128)S(1)}, f32[2,64,256]{2,1,0:T(8,128)S(1)}, u32[]{:S(2)}, u32[]{:S(2)}) %collective-permute-start.20) | collective-permute-done | bytes 131104 | tf_op jit(solution)/shard_map/diag/ppermute | solution.py:27
  155.8 3.6 %collective-permute-start.21 = (f32[64,256]{1,0:T(8,128)}, f32[64,256]{1,0:T(8,128)}, u32[]{:S(2)}, u32[]{:S(2)}) collective-permute-start(f32[64,256]{1,0:T(8,128)} %dynamic-slice_bitcast_fusion.3), channel_id=1, source_target_pairs={{0,4},{1,5},{2,6},{3,7},{4,0},{5,1},{6,2},{7,3},{8,12},{9,13},{10,... | collective-permute-start | bytes 196616 | tf_op jit(solution)/shard_map/diag/ppermute | solution.py:27
  160.3 1.9 collective-permute-start.10
  166.2 6.7 %collective-permute-done.10 = f16[2,256,256]{2,1,0:T(8,128)(2,1)S(1)} collective-permute-done((f16[2,256,256]{2,1,0:T(8,128)(2,1)}, f16[2,256,256]{2,1,0:T(8,128)(2,1)S(1)}, u32[]{:S(2)}, u32[]{:S(2)}) %collective-permute-start.10) | collective-permute-done | bytes 262176 | tf_op jit(solution)/shard_map/near/ppermute | solution.py:27
  176.4 3.4 %collective-permute-start.15 = (f16[2,256,256]{2,1,0:T(8,128)(2,1)S(1)}, f16[2,256,256]{2,1,0:T(8,128)(2,1)S(1)}, u32[]{:S(2)}, u32[]{:S(2)}) collective-permute-start(f16[2,256,256]{2,1,0:T(8,128)(2,1)S(1)} %get-tuple-element.22), channel_id=1, source_target_pairs={{0,3},{1,2},{2,1},{3,0},{4,7},{5,6},{6,5},{7,4},{8,11},{9,10},{10,... | collective-permute-start | bytes 786440 | tf_op jit(solution)/shard_map/far/ppermute | solution.py:27
  180.6 4.7 %collective-permute-start.27 = (f32[64,256]{1,0:T(8,128)S(1)}, f32[64,256]{1,0:T(8,128)S(1)}, u32[]{:S(2)}, u32[]{:S(2)}) collective-permute-start(f32[64,256]{1,0:T(8,128)S(1)} %add_add_fusion.1), channel_id=1, source_target_pairs={{0,192},{1,193},{2,194},{3,195},{4,196},{5,197},{6,198},{7,199},{8... | collective-permute-start | bytes 196616 | tf_op jit(solution)/shard_map/diag/ppermute | solution.py:27
  188.7 3.7 %collective-permute-start.28 = (f32[64,256]{1,0:T(8,128)S(1)}, f32[64,256]{1,0:T(8,128)S(1)}, u32[]{:S(2)}, u32[]{:S(2)}) collective-permute-start(f32[64,256]{1,0:T(8,128)S(1)} %add_add_fusion), channel_id=1, source_target_pairs={{0,4},{1,5},{2,6},{3,7},{4,0},{5,1},{6,2},{7,3},{8,12},{9,13},{10,... | collective-permute-start | bytes 196616 | tf_op jit(solution)/shard_map/diag/ppermute | solution.py:27
  192.5 5.7 %collective-permute-done.28 = f32[64,256]{1,0:T(8,128)S(1)} collective-permute-done((f32[64,256]{1,0:T(8,128)S(1)}, f32[64,256]{1,0:T(8,128)S(1)}, u32[]{:S(2)}, u32[]{:S(2)}) %collective-permute-start.28) | collective-permute-done | bytes 65568 | tf_op jit(solution)/shard_map/diag/ppermute | solution.py:27
  201.6 3.3 %collective-permute-start.16 = (f32[256,256]{1,0:T(8,128)S(1)}, f32[256,256]{1,0:T(8,128)S(1)}, u32[]{:S(2)}, u32[]{:S(2)}) collective-permute-start(f32[256,256]{1,0:T(8,128)S(1)} %slice_bitcast_fusion), channel_id=1, source_target_pairs={{0,4},{1,5},{2,6},{3,7},{4,0},{5,1},{6,2},{7,3},{8,12},{9,13},{10,... | collective-permute-start | bytes 786440 | tf_op jit(solution)/shard_map/far/ppermute | solution.py:27
  205.6 9.0 %collective-permute-start.32 = (f32[2,256,256]{2,1,0:T(8,128)S(1)}, f32[2,256,256]{2,1,0:T(8,128)S(1)}, u32[]{:S(2)}, u32[]{:S(2)}) collective-permute-start(f32[2,256,256]{2,1,0:T(8,128)S(1)} %bitcast.85), channel_id=1, source_target_pairs={{0,8},{1,9},{2,10},{3,11},{4,12},{5,13},{6,14},{7,15},{8,0},{9,1},... | collective-permute-start | bytes 1572872 | tf_op jit(solution)/shard_map/diag/ppermute | solution.py:27
  214.6 5.5 %collective-permute-start.17 = (f32[256,256]{1,0:T(8,128)S(1)}, f32[256,256]{1,0:T(8,128)S(1)}, u32[]{:S(2)}, u32[]{:S(2)}) collective-permute-start(f32[256,256]{1,0:T(8,128)S(1)} %fusion.4), channel_id=1, source_target_pairs={{0,8},{1,9},{2,10},{3,11},{4,12},{5,13},{6,14},{7,15},{8,0},{9,1},... | collective-permute-start | bytes 786440 | tf_op jit(solution)/shard_map/far/ppermute | solution.py:27
  (99 shorter events, 26.6 us)
Async XLA Ops:
  0.6 131.8 %collective-permute-start.12 = (bf16[4,16,256,256]{3,2,1,0:T(8,128)(2,1)}, bf16[4,16,256,256]{3,2,1,0:T(8,128)(2,1)}, u32[]{:S(2)}, u32[]{:S(2)}) collective-permute-start(bf16[4,16,256,256]{3,2,1,0:T(8,128)(2,1)} %a_ref.1), channel_id=1, source_target_pairs={{0,8},{1,9},{2,10},{3,11},{4,12},{5,13},{6,14},{7,15},{8,0},{9,1},... | collective-permute-start | bytes 25165832 | tf_op jit(solution)/shard_map/swap/ppermute | solution.py:27
  6.6 11.7 %collective-permute-start = (bf16[2,4,256,256]{3,2,1,0:T(8,128)(2,1)S(1)}, bf16[2,4,256,256]{3,2,1,0:T(8,128)(2,1)S(1)}, u32[]{:S(2)}, u32[]{:S(2)}) collective-permute-start(bf16[2,4,256,256]{3,2,1,0:T(8,128)(2,1)S(1)} %get-tuple-element.13), channel_id=1, source_target_pairs={{0,8},{1,9},{2,10},{3,11},{4,12},{5,13},{6,14},{7,15},{8,0},{9,1},... | collective-permute-start | bytes 3145736 | tf_op jit(solution)/shard_map/swap/ppermute | solution.py:27
  19.9 29.0 %collective-permute-start.4 = (bf16[2,256,256]{2,1,0:T(8,128)(2,1)S(1)}, bf16[2,256,256]{2,1,0:T(8,128)(2,1)S(1)}, u32[]{:S(2)}, u32[]{:S(2)}) collective-permute-start(bf16[2,256,256]{2,1,0:T(8,128)(2,1)S(1)} %collective-permute-done.1), channel_id=1, source_target_pairs={{0,192},{1,193},{2,194},{3,195},{4,196},{5,197},{6,198},{7,199},{8... | collective-permute-start | bytes 786440 | tf_op jit(solution)/shard_map/gather/ppermute | solution.py:27
  42.6 18.0 %collective-permute-start.3 = (bf16[2,256,256]{2,1,0:T(8,128)(2,1)S(1)}, bf16[2,256,256]{2,1,0:T(8,128)(2,1)S(1)}, u32[]{:S(2)}, u32[]{:S(2)}) collective-permute-start(bf16[2,256,256]{2,1,0:T(8,128)(2,1)S(1)} %collective-permute-done.1), channel_id=1, source_target_pairs={{0,128},{1,129},{2,130},{3,131},{4,132},{5,133},{6,134},{7,135},{8... | collective-permute-start | bytes 786440 | tf_op jit(solution)/shard_map/gather/ppermute | solution.py:27
  42.6 18.0 %collective-permute-start.2 = (bf16[2,256,256]{2,1,0:T(8,128)(2,1)S(1)}, bf16[2,256,256]{2,1,0:T(8,128)(2,1)S(1)}, u32[]{:S(2)}, u32[]{:S(2)}) collective-permute-start(bf16[2,256,256]{2,1,0:T(8,128)(2,1)S(1)} %collective-permute-done.1), channel_id=1, source_target_pairs={{0,64},{1,65},{2,66},{3,67},{4,68},{5,69},{6,70},{7,71},{8,72},{9,... | collective-permute-start | bytes 786440 | tf_op jit(solution)/shard_map/gather/ppermute | solution.py:27
  60.7 28.6 %collective-permute-start.5 = (bf16[4,2,256,256]{3,2,1,0:T(8,128)(2,1)S(1)}, bf16[4,2,256,256]{3,2,1,0:T(8,128)(2,1)S(1)}, u32[]{:S(2)}, u32[]{:S(2)}) collective-permute-start(bf16[4,2,256,256]{3,2,1,0:T(8,128)(2,1)S(1)} %pad_maximum_fusion.p0), channel_id=1, source_target_pairs={{0,16},{1,17},{2,18},{3,19},{4,20},{5,21},{6,22},{7,23},{8,24},{9,... | collective-permute-start | bytes 3145736 | tf_op jit(solution)/shard_map/gather/ppermute | solution.py:27
  66.1 49.1 %collective-permute-start.6 = (bf16[4,2,256,256]{3,2,1,0:T(8,128)(2,1)S(1)}, bf16[4,2,256,256]{3,2,1,0:T(8,128)(2,1)}, u32[]{:S(2)}, u32[]{:S(2)}) collective-permute-start(bf16[4,2,256,256]{3,2,1,0:T(8,128)(2,1)S(1)} %pad_maximum_fusion.p0), channel_id=1, source_target_pairs={{0,32},{1,33},{2,34},{3,35},{4,36},{5,37},{6,38},{7,39},{8,40},{9,... | collective-permute-start | bytes 3145736 | tf_op jit(solution)/shard_map/gather/ppermute | solution.py:27
  70.0 47.3 %collective-permute-start.7 = (bf16[4,2,256,256]{3,2,1,0:T(8,128)(2,1)S(1)}, bf16[4,2,256,256]{3,2,1,0:T(8,128)(2,1)}, u32[]{:S(2)}, u32[]{:S(2)}) collective-permute-start(bf16[4,2,256,256]{3,2,1,0:T(8,128)(2,1)S(1)} %pad_maximum_fusion.p0), channel_id=1, source_target_pairs={{0,48},{1,49},{2,50},{3,51},{4,52},{5,53},{6,54},{7,55},{8,56},{9,... | collective-permute-start | bytes 3145736 | tf_op jit(solution)/shard_map/gather/ppermute | solution.py:27
  147.7 7.0 %collective-permute-start.20 = (f32[2,64,256]{2,1,0:T(8,128)S(1)}, f32[2,64,256]{2,1,0:T(8,128)S(1)}, u32[]{:S(2)}, u32[]{:S(2)}) collective-permute-start(f32[2,64,256]{2,1,0:T(8,128)S(1)} %get-tuple-element.29), channel_id=1, source_target_pairs={{0,3},{1,2},{2,1},{3,0},{4,7},{5,6},{6,5},{7,4},{8,11},{9,10},{10,... | collective-permute-start | bytes 393224 | tf_op jit(solution)/shard_map/diag/ppermute | solution.py:27
  147.9 7.2 %collective-permute-start.18 = (f32[2,64,256]{2,1,0:T(8,128)S(1)}, f32[2,64,256]{2,1,0:T(8,128)S(1)}, u32[]{:S(2)}, u32[]{:S(2)}) collective-permute-start(f32[2,64,256]{2,1,0:T(8,128)S(1)} %get-tuple-element.28), channel_id=1, source_target_pairs={{0,1},{1,0},{2,3},{3,2},{4,5},{5,4},{6,7},{7,6},{8,9},{9,8},{10,11... | collective-permute-start | bytes 393224 | tf_op jit(solution)/shard_map/diag/ppermute | solution.py:27
  155.8 8.1 %collective-permute-start.21 = (f32[64,256]{1,0:T(8,128)}, f32[64,256]{1,0:T(8,128)}, u32[]{:S(2)}, u32[]{:S(2)}) collective-permute-start(f32[64,256]{1,0:T(8,128)} %dynamic-slice_bitcast_fusion.3), channel_id=1, source_target_pairs={{0,4},{1,5},{2,6},{3,7},{4,0},{5,1},{6,2},{7,3},{8,12},{9,13},{10,... | collective-permute-start | bytes 196616 | tf_op jit(solution)/shard_map/diag/ppermute | solution.py:27
  160.3 12.6 %collective-permute-start.10 = (f16[2,256,256]{2,1,0:T(8,128)(2,1)}, f16[2,256,256]{2,1,0:T(8,128)(2,1)S(1)}, u32[]{:S(2)}, u32[]{:S(2)}) collective-permute-start(f16[2,256,256]{2,1,0:T(8,128)(2,1)} %get-tuple-element.19), channel_id=1, source_target_pairs={{0,3},{1,2},{2,1},{3,0},{4,7},{5,6},{6,5},{7,4},{8,11},{9,10},{10,... | collective-permute-start | bytes 786440 | tf_op jit(solution)/shard_map/near/ppermute | solution.py:27
  162.2 10.7 %collective-permute-start.9 = (f16[2,256,256]{2,1,0:T(8,128)(2,1)S(1)}, f16[2,256,256]{2,1,0:T(8,128)(2,1)S(1)}, u32[]{:S(2)}, u32[]{:S(2)}) collective-permute-start(f16[2,256,256]{2,1,0:T(8,128)(2,1)S(1)} %get-tuple-element.20), channel_id=1, source_target_pairs={{0,2},{1,3},{2,0},{3,1},{4,6},{5,7},{6,4},{7,5},{8,10},{9,11},{10,... | collective-permute-start | bytes 786440 | tf_op jit(solution)/shard_map/near/ppermute | solution.py:27
  162.9 10.1 %collective-permute-start.8 = (f16[2,256,256]{2,1,0:T(8,128)(2,1)S(1)}, f16[2,256,256]{2,1,0:T(8,128)(2,1)S(1)}, u32[]{:S(2)}, u32[]{:S(2)}) collective-permute-start(f16[2,256,256]{2,1,0:T(8,128)(2,1)S(1)} %get-tuple-element.18), channel_id=1, source_target_pairs={{0,1},{1,0},{2,3},{3,2},{4,5},{5,4},{6,7},{7,6},{8,9},{9,8},{10,11... | collective-permute-start | bytes 786440 | tf_op jit(solution)/shard_map/near/ppermute | solution.py:27
  164.8 9.5 %collective-permute-start.23 = (f32[64,256]{1,0:T(8,128)S(1)}, f32[64,256]{1,0:T(8,128)S(1)}, u32[]{:S(2)}, u32[]{:S(2)}) collective-permute-start(f32[64,256]{1,0:T(8,128)S(1)} %bitcast_add_fusion.3), channel_id=1, source_target_pairs={{0,32},{1,33},{2,34},{3,35},{4,36},{5,37},{6,38},{7,39},{8,40},{9,... | collective-permute-start | bytes 196616 | tf_op jit(solution)/shard_map/diag/ppermute | solution.py:27
  164.9 9.4 %collective-permute-start.24 = (f32[64,256]{1,0:T(8,128)S(1)}, f32[64,256]{1,0:T(8,128)S(1)}, u32[]{:S(2)}, u32[]{:S(2)}) collective-permute-start(f32[64,256]{1,0:T(8,128)S(1)} %bitcast_add_fusion.3), channel_id=1, source_target_pairs={{0,48},{1,49},{2,50},{3,51},{4,52},{5,53},{6,54},{7,55},{8,56},{9,... | collective-permute-start | bytes 196616 | tf_op jit(solution)/shard_map/diag/ppermute | solution.py:27
  176.2 9.1 %collective-permute-start.26 = (f32[64,256]{1,0:T(8,128)S(1)}, f32[64,256]{1,0:T(8,128)S(1)}, u32[]{:S(2)}, u32[]{:S(2)}) collective-permute-start(f32[64,256]{1,0:T(8,128)S(1)} %add_add_fusion.1), channel_id=1, source_target_pairs={{0,128},{1,129},{2,130},{3,131},{4,132},{5,133},{6,134},{7,135},{8... | collective-permute-start | bytes 196616 | tf_op jit(solution)/shard_map/diag/ppermute | solution.py:27
  176.4 16.0 %collective-permute-start.15 = (f16[2,256,256]{2,1,0:T(8,128)(2,1)S(1)}, f16[2,256,256]{2,1,0:T(8,128)(2,1)S(1)}, u32[]{:S(2)}, u32[]{:S(2)}) collective-permute-start(f16[2,256,256]{2,1,0:T(8,128)(2,1)S(1)} %get-tuple-element.22), channel_id=1, source_target_pairs={{0,3},{1,2},{2,1},{3,0},{4,7},{5,6},{6,5},{7,4},{8,11},{9,10},{10,... | collective-permute-start | bytes 786440 | tf_op jit(solution)/shard_map/far/ppermute | solution.py:27
  179.9 12.5 %collective-permute-start.14 = (f16[2,256,256]{2,1,0:T(8,128)(2,1)S(1)}, f16[2,256,256]{2,1,0:T(8,128)(2,1)S(1)}, u32[]{:S(2)}, u32[]{:S(2)}) collective-permute-start(f16[2,256,256]{2,1,0:T(8,128)(2,1)S(1)} %get-tuple-element.23), channel_id=1, source_target_pairs={{0,2},{1,3},{2,0},{3,1},{4,6},{5,7},{6,4},{7,5},{8,10},{9,11},{10,... | collective-permute-start | bytes 786440 | tf_op jit(solution)/shard_map/far/ppermute | solution.py:27
  179.9 12.5 %collective-permute-start.13 = (f16[2,256,256]{2,1,0:T(8,128)(2,1)S(1)}, f16[2,256,256]{2,1,0:T(8,128)(2,1)S(1)}, u32[]{:S(2)}, u32[]{:S(2)}) collective-permute-start(f16[2,256,256]{2,1,0:T(8,128)(2,1)S(1)} %get-tuple-element.21), channel_id=1, source_target_pairs={{0,1},{1,0},{2,3},{3,2},{4,5},{5,4},{6,7},{7,6},{8,9},{9,8},{10,11... | collective-permute-start | bytes 786440 | tf_op jit(solution)/shard_map/far/ppermute | solution.py:27
  186.9 33.2 %collective-permute-start.11 = (f32[256,256]{1,0:T(8,128)S(1)}, f32[256,256]{1,0:T(8,128)S(1)}, u32[]{:S(2)}, u32[]{:S(2)}) collective-permute-start(f32[256,256]{1,0:T(8,128)S(1)} %slice_bitcast_fusion.5), channel_id=1, source_target_pairs={{0,4},{1,5},{2,6},{3,7},{4,0},{5,1},{6,2},{7,3},{8,12},{9,13},{10,... | collective-permute-start | bytes 786440 | tf_op jit(solution)/shard_map/near/ppermute | solution.py:27
  188.7 9.5 %collective-permute-start.28 = (f32[64,256]{1,0:T(8,128)S(1)}, f32[64,256]{1,0:T(8,128)S(1)}, u32[]{:S(2)}, u32[]{:S(2)}) collective-permute-start(f32[64,256]{1,0:T(8,128)S(1)} %add_add_fusion), channel_id=1, source_target_pairs={{0,4},{1,5},{2,6},{3,7},{4,0},{5,1},{6,2},{7,3},{8,12},{9,13},{10,... | collective-permute-start | bytes 196616 | tf_op jit(solution)/shard_map/diag/ppermute | solution.py:27
  201.6 13.0 %collective-permute-start.16 = (f32[256,256]{1,0:T(8,128)S(1)}, f32[256,256]{1,0:T(8,128)S(1)}, u32[]{:S(2)}, u32[]{:S(2)}) collective-permute-start(f32[256,256]{1,0:T(8,128)S(1)} %slice_bitcast_fusion), channel_id=1, source_target_pairs={{0,4},{1,5},{2,6},{3,7},{4,0},{5,1},{6,2},{7,3},{8,12},{9,13},{10,... | collective-permute-start | bytes 786440 | tf_op jit(solution)/shard_map/far/ppermute | solution.py:27
  205.6 16.6 %collective-permute-start.32 = (f32[2,256,256]{2,1,0:T(8,128)S(1)}, f32[2,256,256]{2,1,0:T(8,128)S(1)}, u32[]{:S(2)}, u32[]{:S(2)}) collective-permute-start(f32[2,256,256]{2,1,0:T(8,128)S(1)} %bitcast.85), channel_id=1, source_target_pairs={{0,8},{1,9},{2,10},{3,11},{4,12},{5,13},{6,14},{7,15},{8,0},{9,1},... | collective-permute-start | bytes 1572872 | tf_op jit(solution)/shard_map/diag/ppermute | solution.py:27
  (19 other events, 375.3 us)

commit v2 on v0

v2 whole, which is shorter than its diff:
```python
import jax
import jax.numpy as jnp
from jax import lax
from jax.experimental import pallas as pl
from jax.experimental.pallas import tpu as pltpu
from jax.sharding import PartitionSpec as P

F32 = jnp.float32
BF16 = jnp.bfloat16
CODE = jnp.int16
AXES = ("row", "col")
PARTS = 2
WIDE = 256 // PARTS


def split_id(dev):
    row, col = dev // 8, dev % 8
    return row // 8, (row // 2) % 4, row % 2, col // 4, col % 4


def join_id(zl, x, core, zh, y):
    return ((zl * 4 + x) * 2 + core) * 8 + zh * 4 + y


def send(value, where):
    pairs = [(dev, join_id(*where(*split_id(dev)))) for dev in range(256)]
    return lax.ppermute(value, AXES, pairs)


def to_core(value):
    return send(value, lambda zl, x, core, zh, y: (zl, x, core ^ 1, zh, y))


def to_x(value, k):
    return send(value, lambda zl, x, core, zh, y: (zl, x ^ k, core, zh, y))


def along_x(value, k):
    return send(value, lambda zl, x, core, zh, y: (zl, (x + k) % 4, core, zh, y))


def to_zl(value, k):
    return send(value, lambda zl, x, core, zh, y: (zl ^ k, x, core, zh, y))


def to_y(value, k):
    return send(value, lambda zl, x, core, zh, y: (zl, x, core, zh, y ^ k))


def to_zh(value):
    return send(value, lambda zl, x, core, zh, y: (zl, x, core, zh ^ 1, y))


def plane_spot(zl, x, core, zh, y):
    h, bit = x % 2, y // 2
    x_to = (x + (2 * h - 1) * bit) % 4
    return 2 * zh + core, x_to, core ^ (y % 2), zl // 2, 2 * (zl % 2) + x // 2


def to_plane(value):
    return send(value, plane_spot)


def chunk_spot(zl, x, y):
    u = (x - 2 * (y % 2)) % 4
    h = jnp.where((u == 1) | (u == 2), 1, 0)
    bit = jnp.where(u >= 2, 1, 0)
    return 8 * h + 4 * (zl % 2) + 2 * (zl // 2) + bit


def encode(value):
    peak = jnp.max(jnp.abs(value), axis=0, keepdims=True)
    power = jnp.floor(jnp.log2(jnp.maximum(peak, 1e-30))) + 1.0
    scaled = jnp.round(value * jnp.exp2(15.0 - power))
    code = jnp.clip(scaled, -32767.0, 32767.0).astype(jnp.int32).astype(CODE)
    mark = jnp.broadcast_to(power, (16, value.shape[1])).astype(jnp.int32).astype(CODE)
    return code, mark


def decode(code, mark):
    return code.astype(jnp.int32).astype(F32) * jnp.exp2(mark.astype(jnp.int32).astype(F32) - 15.0)


def product_kernel(
    scal, near, far, p0, p1, p2, p3, p4, left_near, left_far, own, q1, q2, q3, diag_ref, wide
):
    step = pl.program_id(0)

    @pl.when(step == 0)
    def _():
        diag_ref[...] = jnp.zeros_like(diag_ref)
        for m, piece in enumerate((p0, p1, p2)):
            for z in range(4):
                at = pl.multiple_of(scal[4 * m + z] * 256, 256)
                for k in range(2):
                    wide[pl.ds(at, 256), k * WIDE : (k + 1) * WIDE] = piece[k, z]
        for k, piece in enumerate((p3, p4)):
            for z in range(4):
                at = pl.multiple_of(scal[12 + z] * 256, 256)
                wide[pl.ds(at, 256), k * WIDE : (k + 1) * WIDE] = piece[z]

    half = lax.rem(step, 4) // 2
    zrel = half ^ scal[33]
    side = step // 4

    def work(blocks, left):
        acc = jnp.zeros((256, 2 * WIDE), F32)
        for j in range(16):
            acc += jnp.dot(
                blocks[0, j], wide[j * 256 : (j + 1) * 256, :], preferred_element_type=F32
            )
        for k in range(2):
            live = (-scal[16 + 2 * step + k]).astype(F32)
            term = acc[:, k * WIDE : (k + 1) * WIDE] * live
            high = term.astype(BF16)
            rest = (term - high.astype(F32)).astype(BF16)
            both = jnp.dot(
                left[k, 0], jnp.concatenate([high, rest], axis=1), preferred_element_type=F32
            )
            diag_ref[k] += both[:, :WIDE] + both[:, WIDE:]
            to = (2 * lax.rem(step, 2) + k) ^ scal[32]

            @pl.when(to == 0)
            def _():
                own[zrel, side] = term

            @pl.when(to != 0)
            def _():
                code, mark = encode(term)
                for m, ref in ((1, q1), (2, q2), (3, q3)):

                    @pl.when(to == m)
                    def _():
                        ref[zrel, side, 0:256] = code
                        ref[zrel, side, 256:272] = mark

    @pl.when(step < 4)
    def _():
        work(near, left_near)

    @pl.when(step >= 4)
    def _():
        work(far, left_far)


def total_kernel(own, q1, q2, q3, keep, give):
    for z in range(2):
        for side in range(2):
            value = own[z, side]
            for ref in (q1, q2, q3):
                value += decode(ref[z, side, 0:256], ref[z, side, 256:257])
            if z == 0:
                keep[side] = value
            else:
                code, mark = encode(value)
                give[side, 0:256] = code
                give[side, 256:272] = mark


def totals(own, others):
    return pl.pallas_call(
        total_kernel,
        out_shape=[
            jax.ShapeDtypeStruct((2, 256, WIDE), F32),
            jax.ShapeDtypeStruct((2, 272, WIDE), CODE),
        ],
        compiler_params=pltpu.CompilerParams(vmem_limit_bytes=32 * 2**20),
    )(own, *others)


def products(scal, near, far, pieces, left_near, left_far):
    early = lambda i: jnp.minimum(i, 3)
    late = lambda i: jnp.maximum(i - 4, 0)
    full = lambda shape: pl.BlockSpec(shape, lambda i, s: (0,) * len(shape))
    return pl.pallas_call(
        product_kernel,
        grid_spec=pltpu.PrefetchScalarGridSpec(
            num_scalar_prefetch=1,
            grid=(8,),
            in_specs=[
                pl.BlockSpec((1, 16, 256, 256), lambda i, s: (early(i), 0, 0, 0)),
                pl.BlockSpec((1, 16, 256, 256), lambda i, s: (late(i), 0, 0, 0)),
            ]
            + [full(p.shape) for p in pieces]
            + [
                pl.BlockSpec((2, 1, 256, 256), lambda i, s: (0, early(i), 0, 0)),
                pl.BlockSpec((2, 1, 256, 256), lambda i, s: (0, late(i), 0, 0)),
            ],
            out_specs=[
                full((2, 2, 256, WIDE)),
                full((2, 2, 272, WIDE)),
                full((2, 2, 272, WIDE)),
                full((2, 2, 272, WIDE)),
                full((2, 256, WIDE)),
            ],
            scratch_shapes=[pltpu.VMEM((4096, 2 * WIDE), BF16)],
        ),
        out_shape=[jax.ShapeDtypeStruct((2, 2, 256, WIDE), F32)]
        + [jax.ShapeDtypeStruct((2, 2, 272, WIDE), CODE)] * 3
        + [jax.ShapeDtypeStruct((2, 256, WIDE), F32)],
        cost_estimate=pl.CostEstimate(
            flops=2 * 2048 * 4096 * 2 * WIDE, transcendentals=0, bytes_accessed=24 * 2**20
        ),
        compiler_params=pltpu.CompilerParams(
            dimension_semantics=("arbitrary",), vmem_limit_bytes=48 * 2**20
        ),
    )(scal, near, far, *pieces, left_near, left_far)


def body(ancestors, panel_one, present_one, dinv_one, panel_two, present_two, dinv_two):
    row = lax.axis_index("row")
    col = lax.axis_index("col")
    zl, x, core = row // 8, (row // 2) % 4, row % 2
    zh, y = col // 4, col % 4
    first = core == 0
    rows_one = lax.dynamic_slice_in_dim(present_one, 4 * row, 4, 1)
    rows_two = lax.dynamic_slice_in_dim(present_two, 4 * row, 4, 1)

    with jax.named_scope("spread"):
        take = lambda value: lax.dynamic_slice_in_dim(value, 2 * zh + y // 2, 1, 1)
        one, two = take(panel_one)[:, 0], take(panel_two)[:, 0]
        live_one, live_two = take(rows_one), take(rows_two)
        chosen = core == y % 2
        live = jnp.where(chosen, live_one, live_two).astype(BF16)
        own = jnp.where(chosen, one, two) * live[:, :, None]
        shares = [to_plane(own[:, :, h * WIDE : (h + 1) * WIDE]) for h in range(PARTS)]

    with jax.named_scope("swap"):
        masked_one = panel_one * rows_one[:, :, None, None].astype(BF16)
        masked_two = panel_two * rows_two[:, :, None, None].astype(BF16)
        mine = jnp.swapaxes(jnp.where(first, masked_one, masked_two), 2, 3)
        theirs = to_core(jnp.swapaxes(jnp.where(first, masked_two, masked_one), 2, 3))
        other_blocks = to_core(ancestors)

    present = jnp.where(first, present_one, present_two)
    x_from = ((x + jnp.array([0, 3, 1, 2], jnp.int32)) % 4)[:, None]
    z_from = (zl ^ jnp.arange(4, dtype=jnp.int32))[None, :]
    spots = chunk_spot(z_from, x_from, y)
    live_near = lax.dynamic_slice_in_dim(present, 4 * row, 4, 1)
    live_far = lax.dynamic_slice_in_dim(present, 4 * (row ^ 1), 4, 1)
    scal = jnp.concatenate(
        [
            spots.reshape(16),
            jnp.transpose(live_near).reshape(8),
            jnp.transpose(live_far).reshape(8),
            jnp.stack([y, zh]),
        ]
    ).astype(jnp.int32)

    def tie(value, *others):
        return lax.optimization_barrier((value, *others))[0]

    def line_of(share):
        return jnp.stack([share] + [to_zl(share, k) for k in (1, 2, 3)], axis=1)

    def over_y(out):
        return out[0], [to_y(out[m], m) for m in (1, 2, 3)]

    with jax.named_scope("gather0"):
        line = line_of(shares[0])
        before, after = along_x(line, 1), along_x(line, -1)
        low, high = before[0], after[1]
        pieces = [line, before, after, along_x(low, 1), along_x(high, -1)]
    with jax.named_scope("product0"):
        out_a = products(scal, ancestors, other_blocks, pieces, mine, theirs)
    with jax.named_scope("column0"):
        sent_a = over_y(out_a)
    with jax.named_scope("gather1"):
        line = tie(line_of(shares[1]), low, high)
        before, after = along_x(line, 1), along_x(line, -1)
        pieces = [line, before, after, along_x(before[0], 1), along_x(after[1], -1)]
    with jax.named_scope("product1"):
        pieces[0] = tie(pieces[0], out_a[4])
        out_b = products(scal, ancestors, other_blocks, pieces, mine, theirs)
    with jax.named_scope("total0"):
        keep_a, give_a = totals(sent_a[0], [tie(v, out_b[4]) for v in sent_a[1]])
    with jax.named_scope("diag_y"):
        diag = jnp.concatenate([out_a[4], tie(out_b[4], keep_a)], axis=2).reshape(4, 128, 256)
        at = lambda k: lax.dynamic_index_in_dim(diag, y ^ k, 0, keepdims=False)
        got = [to_y(at(k), k) for k in (1, 2, 3)]
        part = (at(0) + got[0]) + (got[1] + got[2])
    with jax.named_scope("column1"):
        sent_b = over_y(out_b)
    with jax.named_scope("diag_z"):
        one, two, three = [to_zl(part, k) for k in (1, 2, 3)]
        part = (part + one) + (two + three)
        part = part + to_zh(part)
    with jax.named_scope("total1"):
        keep_b, give_b = totals(*sent_b)
        got = to_zh(jnp.concatenate([give_a, give_b], axis=2))
        keep = jnp.concatenate([keep_a, keep_b], axis=2)
        block = keep + decode(got[:, :256], got[:, 256:257])
    with jax.named_scope("diag_x"):
        part = tie(part, keep_b)
        one, two, three = [to_x(part, k) for k in (1, 2, 3)]
        part = (part + one) + (two + three)
    with jax.named_scope("diag_back"):
        stack = jnp.stack([part] + [to_y(part, k) for k in (1, 2, 3)])
        ordered = [lax.dynamic_index_in_dim(stack, y ^ k, 0, keepdims=False) for k in range(4)]
        whole = jnp.stack(ordered).reshape(2, 256, 256)
        partner = to_core(jnp.concatenate([whole, block[1:]]))
    near, far = block[0], partner[2]
    return (
        jnp.where(first, near, far)[None],
        dinv_one.astype(F32) - jnp.where(first, whole, partner[:2]),
        jnp.where(first, far, near)[None],
        dinv_two.astype(F32) - jnp.where(first, partner[:2], whole),
    )


def solution(mesh):
    in_specs = (
        P("row", "col", None, None),
        P(None, "row", None, None),
        P(),
        P(),
        P(None, "row", None, None),
        P(),
        P(),
    )
    out_specs = (P(("row", "col"), None, None), P(), P(("row", "col"), None, None), P())
    return jax.shard_map(body, mesh=mesh, in_specs=in_specs, out_specs=out_specs, check_vma=False)
```

time: 788 us -> 189 us (0.24)
  waiting for transfers between devices: 734 us -> 45.8 us
  starting transfers between devices: 0.16 us -> 86.3 us
  Pallas kernels: 0 us -> 30.9 us
  matrix products: 23.8 us -> 0 us
  between operations: 13.9 us -> 0.95 us
  local copies, waits for them, and re-layouts: 5.69 us -> 13.8 us
    psum x2 -> x0, waiting for transfers between devices: 560 us -> none  [the longest x1 305 us: spread(): return lax.psum(block, axis)]
    reduce_scatter x2 -> x0, waiting for transfers between devices: 173 us -> none  [one_level(): lax.psum_scatter(flat_terms, 'col', scatter_dimension=0, tiled=True)]
    ppermute x0 -> x39, starting transfers between devices: none -> 86.3 us  [send(): return lax.ppermute(value, AXES, pairs)]
    ppermute x0 -> x39, waiting for transfers between devices: none -> 45.8 us  [send(): return lax.ppermute(value, AXES, pairs)]
    pallas_call x0 -> x4, Pallas kernels: none -> 30.9 us  [the longest x2 30.3 us: products(): pl.pallas_call(product_kernel, grid_spec=pltpu.PrefetchScalarGridSpec(num...]
    dot_general x4 -> x0, matrix products: 23.8 us -> none  [the longest x2 21.3 us: one_level(): jnp.einsum('ijab,kjbc->ikac', ancestors, masked, preferred_element_type=j...]
  transfers between devices with their start and end apart: 4 -> 39, of which waited for: 4 -> 16; matrix products, arithmetic and copies ran while one was open for 2% -> 10% of each run, Pallas kernels for 0% -> 16%
where the time goes in v2:
time: 189 us; the launch traced here: 187 us
  starting transfers between devices  86.3 us (46%)
  waiting for transfers between devices  45.8 us (24%)
  Pallas kernels  30.9 us (16%)
  local copies, waits for them, and re-layouts  13.8 us (7%)
  other arithmetic  9.73 us (5%)
    ppermute x39, starting transfers between devices, send(): return lax.ppermute(value, AXES, pairs)  86.3 us
    ppermute x39, waiting for transfers between devices, send(): return lax.ppermute(value, AXES, pairs)  45.8 us
    pallas_call x2, Pallas kernels, products(): pl.pallas_call(product_kernel, grid_spec=pltpu.PrefetchScalarGridSpec(num...  30.3 us
    unnamed x21, local copies, waits for them, and re-layouts  5.48 us
  transfers between devices with their start and end apart: 39, of which 16 were waited for; matrix products, arithmetic and copies ran while one was open for 10% of the time, Pallas kernels for 16%

profile of v2, /device:TPU:1, one launch (start us, length us, event | category | flops | bytes accessed | tf_op | source)
XLA Modules:
  0.0 187.5 jit_solution(7815614338597027590)
XLA Ops:
  0.7 3.3 %collective-permute-start = (bf16[4,16,256,256]{3,2,1,0:T(8,128)(2,1)}, bf16[4,16,256,256]{3,2,1,0:T(8,128)(2,1)}, u32[]{:S(2)}, u32[]{:S(2)}) collective-permute-start(bf16[4,16,256,256]{3,2,1,0:T(8,128)(2,1)} %near.3), channel_id=1, source_target_pairs={{0,8},{1,9},{2,10},{3,11},{4,12},{5,13},{6,14},{7,15},{8,0},{9,1},... | collective-permute-start | bytes 25165832 | tf_op jit(solution)/shard_map/swap/ppermute | solution.py:27
  8.0 4.7 %collective-permute-start.11 = (bf16[2,256,128]{2,1,0:T(8,128)(2,1)S(1)}, bf16[2,256,128]{2,1,0:T(8,128)(2,1)S(1)}, u32[]{:S(2)}, u32[]{:S(2)}) collective-permute-start(bf16[2,256,128]{2,1,0:T(8,128)(2,1)S(1)} %get-tuple-element.62), channel_id=1, source_target_pairs={{0,0},{1,8},{2,48},{3,56},{4,128},{5,136},{6,176},{7,184},{8,72},{... | collective-permute-start | bytes 393224 | tf_op jit(solution)/shard_map/spread/ppermute | solution.py:27
  16.5 2.5 %collective-permute-start.2 = (bf16[2,256,128]{2,1,0:T(8,128)(2,1)S(1)}, bf16[2,256,128]{2,1,0:T(8,128)(2,1)}, u32[]{:S(2)}, u32[]{:S(2)}) collective-permute-start(bf16[2,256,128]{2,1,0:T(8,128)(2,1)S(1)} %collective-permute-done.1), channel_id=1, source_target_pairs={{0,64},{1,65},{2,66},{3,67},{4,68},{5,69},{6,70},{7,71},{8,72},{9,... | collective-permute-start | bytes 393224 | tf_op jit(solution)/shard_map/gather0/ppermute | solution.py:27
  19.0 6.0 %collective-permute-start.3 = (bf16[2,256,128]{2,1,0:T(8,128)(2,1)S(1)}, bf16[2,256,128]{2,1,0:T(8,128)(2,1)}, u32[]{:S(2)}, u32[]{:S(2)}) collective-permute-start(bf16[2,256,128]{2,1,0:T(8,128)(2,1)S(1)} %collective-permute-done.1), channel_id=1, source_target_pairs={{0,128},{1,129},{2,130},{3,131},{4,132},{5,133},{6,134},{7,135},{8... | collective-permute-start | bytes 393224 | tf_op jit(solution)/shard_map/gather0/ppermute | solution.py:27
  26.5 2.4 %collective-permute-done.3 = bf16[2,256,128]{2,1,0:T(8,128)(2,1)} collective-permute-done((bf16[2,256,128]{2,1,0:T(8,128)(2,1)S(1)}, bf16[2,256,128]{2,1,0:T(8,128)(2,1)}, u32[]{:S(2)}, u32[]{:S(2)}) %collective-permute-start.3) | collective-permute-done | bytes 131104 | tf_op jit(solution)/shard_map/gather0/ppermute | solution.py:27
  28.9 6.7 %collective-permute-done.4 = bf16[2,256,128]{2,1,0:T(8,128)(2,1)} collective-permute-done((bf16[2,256,128]{2,1,0:T(8,128)(2,1)S(1)}, bf16[2,256,128]{2,1,0:T(8,128)(2,1)}, u32[]{:S(2)}, u32[]{:S(2)}) %collective-permute-start.4) | collective-permute-done | bytes 131104 | tf_op jit(solution)/shard_map/gather0/ppermute | solution.py:27
  37.1 2.7 %collective-permute-start.13 = (bf16[2,256,128]{2,1,0:T(8,128)(2,1)S(1)}, bf16[2,256,128]{2,1,0:T(8,128)(2,1)S(1)}, u32[]{:S(2)}, u32[]{:S(2)}) collective-permute-start(bf16[2,256,128]{2,1,0:T(8,128)(2,1)S(1)} %collective-permute-done.11), channel_id=1, source_target_pairs={{0,128},{1,129},{2,130},{3,131},{4,132},{5,133},{6,134},{7,135},{8... | collective-permute-start | bytes 393224 | tf_op jit(solution)/shard_map/gather1/ppermute | solution.py:27
  41.0 2.6 %collective-permute-start.6 = (bf16[2,4,256,128]{3,2,0,1:T(8,128)(2,1)S(1)}, bf16[2,4,256,128]{3,2,0,1:T(8,128)(2,1)}, u32[]{:S(2)}, u32[]{:S(2)}) collective-permute-start(bf16[2,4,256,128]{3,2,0,1:T(8,128)(2,1)S(1)} %pad_maximum_fusion.1), channel_id=1, source_target_pairs={{0,48},{1,49},{2,50},{3,51},{4,52},{5,53},{6,54},{7,55},{8,56},{9,... | collective-permute-start | bytes 1572872 | tf_op jit(solution)/shard_map/gather0/ppermute | solution.py:27
  44.2 4.1 %collective-permute-done.13 = bf16[2,256,128]{2,1,0:T(8,128)(2,1)S(1)} collective-permute-done((bf16[2,256,128]{2,1,0:T(8,128)(2,1)S(1)}, bf16[2,256,128]{2,1,0:T(8,128)(2,1)S(1)}, u32[]{:S(2)}, u32[]{:S(2)}) %collective-permute-start.13) | collective-permute-done | bytes 131104 | tf_op jit(solution)/shard_map/gather1/ppermute | solution.py:27
  48.2 3.0 %collective-permute-start.9 = (bf16[2,4,256,256]{3,2,1,0:T(8,128)(2,1)}, bf16[2,4,256,256]{3,2,1,0:T(8,128)(2,1)S(1)}, u32[]{:S(2)}, u32[]{:S(2)}) collective-permute-start(bf16[2,4,256,256]{3,2,1,0:T(8,128)(2,1)} %get-tuple-element.48), channel_id=1, source_target_pairs={{0,8},{1,9},{2,10},{3,11},{4,12},{5,13},{6,14},{7,15},{8,0},{9,1},... | collective-permute-start | bytes 3145736 | tf_op jit(solution)/shard_map/swap/ppermute | solution.py:27
  64.2 4.8 %collective-permute-done.15.p1 = bf16[2,4,256,128]{3,2,1,0:T(8,128)(2,1)S(1)} collective-permute-done((bf16[2,4,256,128]{3,2,1,0:T(8,128)(2,1)S(1)}, bf16[2,4,256,128]{3,2,1,0:T(8,128)(2,1)S(1)}, u32[]{:S(2)}, u32[]{:S(2)}) %collective-permute-start.15) | collective-permute-done | bytes 524320 | tf_op jit(solution)/shard_map/gather1/ppermute | solution.py:27
  75.7 14.7 %product0.1 = (f32[2,2,256,128]{3,2,1,0:T(8,128)S(1)}, s16[2,2,272,128]{3,2,1,0:T(8,128)(2,1)S(1)}, s16[2,2,272,128]{3,2,1,0:T(8,128)(2,1)S(1)}, s16[2,2,272,128]{3,2,1,0:T(8,128)(2,1)S(1)}, f32[2,256,128]{2,1,0:T(8,128)S(1)}) custom-call(s32[34]{0:T(128)S(1)} %concatenate.15.scal, bf16[4,16,256,256]{3,2,1,0:T(8,128)(2,1)} %near.3, ...), custom_call_target="tpu_custom_call" | custom-call | flops 4294967296 | bytes 25165824 | tf_op jit(solution)/shard_map/product0/pallas_call | solution.py:175
  90.4 2.2 %collective-permute-start.20 = (s16[2,2,272,128]{3,2,1,0:T(8,128)(2,1)S(1)}, s16[2,2,272,128]{3,2,1,0:T(8,128)(2,1)S(1)}, u32[]{:S(2)}, u32[]{:S(2)}) collective-permute-start(s16[2,2,272,128]{3,2,1,0:T(8,128)(2,1)S(1)} %get-tuple-element.34), channel_id=1, source_target_pairs={{0,3},{1,2},{2,1},{3,0},{4,7},{5,6},{6,5},{7,4},{8,11},{9,10},{10,... | collective-permute-start | bytes 835592 | tf_op jit(solution)/shard_map/column0/ppermute | solution.py:27
  93.8 15.6 %product1.1 = (f32[2,2,256,128]{3,2,1,0:T(8,128)S(1)}, s16[2,2,272,128]{3,2,1,0:T(8,128)(2,1)}, s16[2,2,272,128]{3,2,1,0:T(8,128)(2,1)}, s16[2,2,272,128]{3,2,1,0:T(8,128)(2,1)S(1)}, f32[2,256,128]{2,1,0:T(8,128)S(1)}) custom-call(s32[34]{0:T(128)S(1)} %concatenate.15.scal, bf16[4,16,256,256]{3,2,1,0:T(8,128)(2,1)} %near.3, ...), custom_call_target="tpu_custom_call" | custom-call | flops 4294967296 | bytes 25165824 | tf_op jit(solution)/shard_map/product1/pallas_call | solution.py:175
  111.6 2.2 %collective-permute-start.26 = (f32[128,256]{1,0:T(8,128)S(1)}, f32[128,256]{1,0:T(8,128)S(1)}, u32[]{:S(2)}, u32[]{:S(2)}) collective-permute-start(f32[128,256]{1,0:T(8,128)S(1)} %get-tuple-element.59), channel_id=1, source_target_pairs={{0,2},{1,3},{2,0},{3,1},{4,6},{5,7},{6,4},{7,5},{8,10},{9,11},{10,... | collective-permute-start | bytes 393224 | tf_op jit(solution)/shard_map/diag_y/ppermute | solution.py:27
  114.5 3.2 %collective-permute-start.22 = (s16[2,2,272,128]{3,2,1,0:T(8,128)(2,1)}, s16[2,2,272,128]{3,2,1,0:T(8,128)(2,1)S(1)}, u32[]{:S(2)}, u32[]{:S(2)}) collective-permute-start(s16[2,2,272,128]{3,2,1,0:T(8,128)(2,1)} %get-tuple-element.39), channel_id=1, source_target_pairs={{0,2},{1,3},{2,0},{3,1},{4,6},{5,7},{6,4},{7,5},{8,10},{9,11},{10,... | collective-permute-start | bytes 835592 | tf_op jit(solution)/shard_map/column1/ppermute | solution.py:27
  119.0 3.8 %collective-permute-start.28 = (f32[128,256]{1,0:T(8,128)S(1)}, f32[128,256]{1,0:T(8,128)S(1)}, u32[]{:S(2)}, u32[]{:S(2)}) collective-permute-start(f32[128,256]{1,0:T(8,128)S(1)} %fusion.2), channel_id=1, source_target_pairs={{0,64},{1,65},{2,66},{3,67},{4,68},{5,69},{6,70},{7,71},{8,72},{9,... | collective-permute-start | bytes 393224 | tf_op jit(solution)/shard_map/diag_z/ppermute | solution.py:27
  122.8 2.2 %collective-permute-start.30 = (f32[128,256]{1,0:T(8,128)S(1)}, f32[128,256]{1,0:T(8,128)S(1)}, u32[]{:S(2)}, u32[]{:S(2)}) collective-permute-start(f32[128,256]{1,0:T(8,128)S(1)} %fusion.2), channel_id=1, source_target_pairs={{0,192},{1,193},{2,194},{3,195},{4,196},{5,197},{6,198},{7,199},{8... | collective-permute-start | bytes 393224 | tf_op jit(solution)/shard_map/diag_z/ppermute | solution.py:27
  126.0 3.9 %collective-permute-done.23.q3 = s16[2,2,272,128]{3,2,1,0:T(8,128)(2,1)S(1)} collective-permute-done((s16[2,2,272,128]{3,2,1,0:T(8,128)(2,1)S(1)}, s16[2,2,272,128]{3,2,1,0:T(8,128)(2,1)S(1)}, u32[]{:S(2)}, u32[]{:S(2)}) %collective-permute-start.23) | collective-permute-done | bytes 278560 | tf_op jit(solution)/shard_map/column1/ppermute | solution.py:27
  131.3 7.8 %collective-permute-start.24 = (s16[2,272,256]{2,1,0:T(8,128)(2,1)S(1)}, s16[2,272,256]{2,1,0:T(8,128)(2,1)S(1)}, u32[]{:S(2)}, u32[]{:S(2)}) collective-permute-start(s16[2,272,256]{2,1,0:T(8,128)(2,1)S(1)} %pad_add_fusion), channel_id=1, source_target_pairs={{0,4},{1,5},{2,6},{3,7},{4,0},{5,1},{6,2},{7,3},{8,12},{9,13},{10,... | collective-permute-start | bytes 835592 | tf_op jit(solution)/shard_map/total1/ppermute | solution.py:27
  139.2 9.4 %collective-permute-done.31 = f32[128,256]{1,0:T(8,128)S(1)} collective-permute-done((f32[128,256]{1,0:T(8,128)S(1)}, f32[128,256]{1,0:T(8,128)S(1)}, u32[]{:S(2)}, u32[]{:S(2)}) %collective-permute-start.31) | collective-permute-done | bytes 131104 | tf_op jit(solution)/shard_map/diag_z/ppermute | solution.py:27
  149.0 4.2 %collective-permute-start.33 = (f32[128,256]{1,0:T(8,128)S(1)}, f32[128,256]{1,0:T(8,128)S(1)}, u32[]{:S(2)}, u32[]{:S(2)}) collective-permute-start(f32[128,256]{1,0:T(8,128)S(1)} %add.198), channel_id=1, source_target_pairs={{0,32},{1,33},{2,34},{3,35},{4,36},{5,37},{6,38},{7,39},{8,40},{9,... | collective-permute-start | bytes 393224 | tf_op jit(solution)/shard_map/diag_x/ppermute | solution.py:27
  153.4 3.4 %collective-permute-done.33 = f32[128,256]{1,0:T(8,128)S(1)} collective-permute-done((f32[128,256]{1,0:T(8,128)S(1)}, f32[128,256]{1,0:T(8,128)S(1)}, u32[]{:S(2)}, u32[]{:S(2)}) %collective-permute-start.33) | collective-permute-done | bytes 131104 | tf_op jit(solution)/shard_map/diag_x/ppermute | solution.py:27
  165.9 17.7 %collective-permute-start.38 = (f32[3,256,256]{2,1,0:T(8,128)S(1)}, f32[3,256,256]{2,1,0:T(8,128)S(1)}, u32[]{:S(2)}, u32[]{:S(2)}) collective-permute-start(f32[3,256,256]{2,1,0:T(8,128)S(1)} %pad_maximum_fusion), channel_id=1, source_target_pairs={{0,8},{1,9},{2,10},{3,11},{4,12},{5,13},{6,14},{7,15},{8,0},{9,1},... | collective-permute-start | bytes 2359304 | tf_op jit(solution)/shard_map/diag_back/ppermute | solution.py:27
  (121 shorter events, 53.5 us)
Async XLA Ops:
  0.7 75.0 %collective-permute-start = (bf16[4,16,256,256]{3,2,1,0:T(8,128)(2,1)}, bf16[4,16,256,256]{3,2,1,0:T(8,128)(2,1)}, u32[]{:S(2)}, u32[]{:S(2)}) collective-permute-start(bf16[4,16,256,256]{3,2,1,0:T(8,128)(2,1)} %near.3), channel_id=1, source_target_pairs={{0,8},{1,9},{2,10},{3,11},{4,12},{5,13},{6,14},{7,15},{8,0},{9,1},... | collective-permute-start | bytes 25165832 | tf_op jit(solution)/shard_map/swap/ppermute | solution.py:27
  8.0 18.2 %collective-permute-start.11 = (bf16[2,256,128]{2,1,0:T(8,128)(2,1)S(1)}, bf16[2,256,128]{2,1,0:T(8,128)(2,1)S(1)}, u32[]{:S(2)}, u32[]{:S(2)}) collective-permute-start(bf16[2,256,128]{2,1,0:T(8,128)(2,1)S(1)} %get-tuple-element.62), channel_id=1, source_target_pairs={{0,0},{1,8},{2,48},{3,56},{4,128},{5,136},{6,176},{7,184},{8,72},{... | collective-permute-start | bytes 393224 | tf_op jit(solution)/shard_map/spread/ppermute | solution.py:27
  25.0 10.6 %collective-permute-start.4 = (bf16[2,256,128]{2,1,0:T(8,128)(2,1)S(1)}, bf16[2,256,128]{2,1,0:T(8,128)(2,1)}, u32[]{:S(2)}, u32[]{:S(2)}) collective-permute-start(bf16[2,256,128]{2,1,0:T(8,128)(2,1)S(1)} %collective-permute-done.1), channel_id=1, source_target_pairs={{0,192},{1,193},{2,194},{3,195},{4,196},{5,197},{6,198},{7,199},{8... | collective-permute-start | bytes 393224 | tf_op jit(solution)/shard_map/gather0/ppermute | solution.py:27
  26.2 14.8 %collective-permute-start.12 = (bf16[2,256,128]{2,1,0:T(8,128)(2,1)S(1)}, bf16[2,256,128]{2,1,0:T(8,128)(2,1)S(1)}, u32[]{:S(2)}, u32[]{:S(2)}) collective-permute-start(bf16[2,256,128]{2,1,0:T(8,128)(2,1)S(1)} %collective-permute-done.11), channel_id=1, source_target_pairs={{0,64},{1,65},{2,66},{3,67},{4,68},{5,69},{6,70},{7,71},{8,72},{9,... | collective-permute-start | bytes 393224 | tf_op jit(solution)/shard_map/gather1/ppermute | solution.py:27
  36.7 16.2 %collective-permute-start.5 = (bf16[2,4,256,128]{3,2,0,1:T(8,128)(2,1)S(1)}, bf16[2,4,256,128]{3,2,0,1:T(8,128)(2,1)}, u32[]{:S(2)}, u32[]{:S(2)}) collective-permute-start(bf16[2,4,256,128]{3,2,0,1:T(8,128)(2,1)S(1)} %pad_maximum_fusion.1), channel_id=1, source_target_pairs={{0,16},{1,17},{2,18},{3,19},{4,20},{5,21},{6,22},{7,23},{8,24},{9,... | collective-permute-start | bytes 1572872 | tf_op jit(solution)/shard_map/gather0/ppermute | solution.py:27
  37.1 11.2 %collective-permute-start.13 = (bf16[2,256,128]{2,1,0:T(8,128)(2,1)S(1)}, bf16[2,256,128]{2,1,0:T(8,128)(2,1)S(1)}, u32[]{:S(2)}, u32[]{:S(2)}) collective-permute-start(bf16[2,256,128]{2,1,0:T(8,128)(2,1)S(1)} %collective-permute-done.11), channel_id=1, source_target_pairs={{0,128},{1,129},{2,130},{3,131},{4,132},{5,133},{6,134},{7,135},{8... | collective-permute-start | bytes 393224 | tf_op jit(solution)/shard_map/gather1/ppermute | solution.py:27
  39.8 11.4 %collective-permute-start.14 = (bf16[2,256,128]{2,1,0:T(8,128)(2,1)S(1)}, bf16[2,256,128]{2,1,0:T(8,128)(2,1)S(1)}, u32[]{:S(2)}, u32[]{:S(2)}) collective-permute-start(bf16[2,256,128]{2,1,0:T(8,128)(2,1)S(1)} %collective-permute-done.11), channel_id=1, source_target_pairs={{0,192},{1,193},{2,194},{3,195},{4,196},{5,197},{6,198},{7,199},{8... | collective-permute-start | bytes 393224 | tf_op jit(solution)/shard_map/gather1/ppermute | solution.py:27
  41.0 13.5 %collective-permute-start.6 = (bf16[2,4,256,128]{3,2,0,1:T(8,128)(2,1)S(1)}, bf16[2,4,256,128]{3,2,0,1:T(8,128)(2,1)}, u32[]{:S(2)}, u32[]{:S(2)}) collective-permute-start(bf16[2,4,256,128]{3,2,0,1:T(8,128)(2,1)S(1)} %pad_maximum_fusion.1), channel_id=1, source_target_pairs={{0,48},{1,49},{2,50},{3,51},{4,52},{5,53},{6,54},{7,55},{8,56},{9,... | collective-permute-start | bytes 1572872 | tf_op jit(solution)/shard_map/gather0/ppermute | solution.py:27
  48.2 27.5 %collective-permute-start.9 = (bf16[2,4,256,256]{3,2,1,0:T(8,128)(2,1)}, bf16[2,4,256,256]{3,2,1,0:T(8,128)(2,1)S(1)}, u32[]{:S(2)}, u32[]{:S(2)}) collective-permute-start(bf16[2,4,256,256]{3,2,1,0:T(8,128)(2,1)} %get-tuple-element.48), channel_id=1, source_target_pairs={{0,8},{1,9},{2,10},{3,11},{4,12},{5,13},{6,14},{7,15},{8,0},{9,1},... | collective-permute-start | bytes 3145736 | tf_op jit(solution)/shard_map/swap/ppermute | solution.py:27
  56.2 12.8 %collective-permute-start.15 = (bf16[2,4,256,128]{3,2,1,0:T(8,128)(2,1)S(1)}, bf16[2,4,256,128]{3,2,1,0:T(8,128)(2,1)S(1)}, u32[]{:S(2)}, u32[]{:S(2)}) collective-permute-start(bf16[2,4,256,128]{3,2,1,0:T(8,128)(2,1)S(1)} %pad_maximum_fusion.2.p0), channel_id=1, source_target_pairs={{0,16},{1,17},{2,18},{3,19},{4,20},{5,21},{6,22},{7,23},{8,24},{9,... | collective-permute-start | bytes 1572872 | tf_op jit(solution)/shard_map/gather1/ppermute | solution.py:27
  58.9 12.4 %collective-permute-start.16 = (bf16[2,4,256,128]{3,2,1,0:T(8,128)(2,1)S(1)}, bf16[2,4,256,128]{3,2,1,0:T(8,128)(2,1)}, u32[]{:S(2)}, u32[]{:S(2)}) collective-permute-start(bf16[2,4,256,128]{3,2,1,0:T(8,128)(2,1)S(1)} %pad_maximum_fusion.2.p0), channel_id=1, source_target_pairs={{0,48},{1,49},{2,50},{3,51},{4,52},{5,53},{6,54},{7,55},{8,56},{9,... | collective-permute-start | bytes 1572872 | tf_op jit(solution)/shard_map/gather1/ppermute | solution.py:27
  61.3 13.3 %collective-permute-start.7 = (bf16[4,256,128]{2,1,0:T(8,128)(2,1)}, bf16[4,256,128]{2,1,0:T(8,128)(2,1)S(1)}, u32[]{:S(2)}, u32[]{:S(2)}) collective-permute-start(bf16[4,256,128]{2,1,0:T(8,128)(2,1)} %slice_bitcast_fusion.3), channel_id=1, source_target_pairs={{0,16},{1,17},{2,18},{3,19},{4,20},{5,21},{6,22},{7,23},{8,24},{9,... | collective-permute-start | bytes 786440 | tf_op jit(solution)/shard_map/gather0/ppermute | solution.py:27
  71.2 22.5 %collective-permute-start.17 = (bf16[4,256,128]{2,1,0:T(8,128)(2,1)S(1)}, bf16[4,256,128]{2,1,0:T(8,128)(2,1)S(1)}, u32[]{:S(2)}, u32[]{:S(2)}) collective-permute-start(bf16[4,256,128]{2,1,0:T(8,128)(2,1)S(1)} %slice_bitcast_fusion.1), channel_id=1, source_target_pairs={{0,16},{1,17},{2,18},{3,19},{4,20},{5,21},{6,22},{7,23},{8,24},{9,... | collective-permute-start | bytes 786440 | tf_op jit(solution)/shard_map/gather1/ppermute | solution.py:27
  74.6 19.1 %collective-permute-start.18 = (bf16[4,256,128]{2,1,0:T(8,128)(2,1)S(1)}, bf16[4,256,128]{2,1,0:T(8,128)(2,1)S(1)}, u32[]{:S(2)}, u32[]{:S(2)}) collective-permute-start(bf16[4,256,128]{2,1,0:T(8,128)(2,1)S(1)} %slice_bitcast_fusion), channel_id=1, source_target_pairs={{0,48},{1,49},{2,50},{3,51},{4,52},{5,53},{6,54},{7,55},{8,56},{9,... | collective-permute-start | bytes 786440 | tf_op jit(solution)/shard_map/gather1/ppermute | solution.py:27
  90.4 19.7 %collective-permute-start.20 = (s16[2,2,272,128]{3,2,1,0:T(8,128)(2,1)S(1)}, s16[2,2,272,128]{3,2,1,0:T(8,128)(2,1)S(1)}, u32[]{:S(2)}, u32[]{:S(2)}) collective-permute-start(s16[2,2,272,128]{3,2,1,0:T(8,128)(2,1)S(1)} %get-tuple-element.34), channel_id=1, source_target_pairs={{0,3},{1,2},{2,1},{3,0},{4,7},{5,6},{6,5},{7,4},{8,11},{9,10},{10,... | collective-permute-start | bytes 835592 | tf_op jit(solution)/shard_map/column0/ppermute | solution.py:27
  92.6 17.5 %collective-permute-start.19 = (s16[2,2,272,128]{3,2,1,0:T(8,128)(2,1)S(1)}, s16[2,2,272,128]{3,2,1,0:T(8,128)(2,1)S(1)}, u32[]{:S(2)}, u32[]{:S(2)}) collective-permute-start(s16[2,2,272,128]{3,2,1,0:T(8,128)(2,1)S(1)} %get-tuple-element.32), channel_id=1, source_target_pairs={{0,2},{1,3},{2,0},{3,1},{4,6},{5,7},{6,4},{7,5},{8,10},{9,11},{10,... | collective-permute-start | bytes 835592 | tf_op jit(solution)/shard_map/column0/ppermute | solution.py:27
  93.3 16.9 %collective-permute-start.10 = (s16[2,2,272,128]{3,2,1,0:T(8,128)(2,1)S(1)}, s16[2,2,272,128]{3,2,1,0:T(8,128)(2,1)S(1)}, u32[]{:S(2)}, u32[]{:S(2)}) collective-permute-start(s16[2,2,272,128]{3,2,1,0:T(8,128)(2,1)S(1)} %get-tuple-element.26), channel_id=1, source_target_pairs={{0,1},{1,0},{2,3},{3,2},{4,5},{5,4},{6,7},{7,6},{8,9},{9,8},{10,11... | collective-permute-start | bytes 835592 | tf_op jit(solution)/shard_map/column0/ppermute | solution.py:27
  114.5 11.5 %collective-permute-start.22 = (s16[2,2,272,128]{3,2,1,0:T(8,128)(2,1)}, s16[2,2,272,128]{3,2,1,0:T(8,128)(2,1)S(1)}, u32[]{:S(2)}, u32[]{:S(2)}) collective-permute-start(s16[2,2,272,128]{3,2,1,0:T(8,128)(2,1)} %get-tuple-element.39), channel_id=1, source_target_pairs={{0,2},{1,3},{2,0},{3,1},{4,6},{5,7},{6,4},{7,5},{8,10},{9,11},{10,... | collective-permute-start | bytes 835592 | tf_op jit(solution)/shard_map/column1/ppermute | solution.py:27
  117.7 12.2 %collective-permute-start.23 = (s16[2,2,272,128]{3,2,1,0:T(8,128)(2,1)S(1)}, s16[2,2,272,128]{3,2,1,0:T(8,128)(2,1)S(1)}, u32[]{:S(2)}, u32[]{:S(2)}) collective-permute-start(s16[2,2,272,128]{3,2,1,0:T(8,128)(2,1)S(1)} %get-tuple-element.40), channel_id=1, source_target_pairs={{0,3},{1,2},{2,1},{3,0},{4,7},{5,6},{6,5},{7,4},{8,11},{9,10},{10,... | collective-permute-start | bytes 835592 | tf_op jit(solution)/shard_map/column1/ppermute | solution.py:27
  119.0 20.0 %collective-permute-start.28 = (f32[128,256]{1,0:T(8,128)S(1)}, f32[128,256]{1,0:T(8,128)S(1)}, u32[]{:S(2)}, u32[]{:S(2)}) collective-permute-start(f32[128,256]{1,0:T(8,128)S(1)} %fusion.2), channel_id=1, source_target_pairs={{0,64},{1,65},{2,66},{3,67},{4,68},{5,69},{6,70},{7,71},{8,72},{9,... | collective-permute-start | bytes 393224 | tf_op jit(solution)/shard_map/diag_z/ppermute | solution.py:27
  122.8 16.3 %collective-permute-start.29 = (f32[128,256]{1,0:T(8,128)S(1)}, f32[128,256]{1,0:T(8,128)S(1)}, u32[]{:S(2)}, u32[]{:S(2)}) collective-permute-start(f32[128,256]{1,0:T(8,128)S(1)} %fusion.2), channel_id=1, source_target_pairs={{0,128},{1,129},{2,130},{3,131},{4,132},{5,133},{6,134},{7,135},{8... | collective-permute-start | bytes 393224 | tf_op jit(solution)/shard_map/diag_z/ppermute | solution.py:27
  122.8 16.3 %collective-permute-start.30 = (f32[128,256]{1,0:T(8,128)S(1)}, f32[128,256]{1,0:T(8,128)S(1)}, u32[]{:S(2)}, u32[]{:S(2)}) collective-permute-start(f32[128,256]{1,0:T(8,128)S(1)} %fusion.2), channel_id=1, source_target_pairs={{0,192},{1,193},{2,194},{3,195},{4,196},{5,197},{6,198},{7,199},{8... | collective-permute-start | bytes 393224 | tf_op jit(solution)/shard_map/diag_z/ppermute | solution.py:27
  131.3 22.1 %collective-permute-start.24 = (s16[2,272,256]{2,1,0:T(8,128)(2,1)S(1)}, s16[2,272,256]{2,1,0:T(8,128)(2,1)S(1)}, u32[]{:S(2)}, u32[]{:S(2)}) collective-permute-start(s16[2,272,256]{2,1,0:T(8,128)(2,1)S(1)} %pad_add_fusion), channel_id=1, source_target_pairs={{0,4},{1,5},{2,6},{3,7},{4,0},{5,1},{6,2},{7,3},{8,12},{9,13},{10,... | collective-permute-start | bytes 835592 | tf_op jit(solution)/shard_map/total1/ppermute | solution.py:27
  165.9 19.6 %collective-permute-start.38 = (f32[3,256,256]{2,1,0:T(8,128)S(1)}, f32[3,256,256]{2,1,0:T(8,128)S(1)}, u32[]{:S(2)}, u32[]{:S(2)}) collective-permute-start(f32[3,256,256]{2,1,0:T(8,128)S(1)} %pad_maximum_fusion), channel_id=1, source_target_pairs={{0,8},{1,9},{2,10},{3,11},{4,12},{5,13},{6,14},{7,15},{8,0},{9,1},... | collective-permute-start | bytes 2359304 | tf_op jit(solution)/shard_map/diag_back/ppermute | solution.py:27
  (24 other events, 434.0 us)

commit v3 on v2

v3 whole, which is shorter than its diff:
```python
import jax
import jax.numpy as jnp
from jax import lax
from jax.experimental import pallas as pl
from jax.experimental.pallas import tpu as pltpu
from jax.sharding import PartitionSpec as P

F32 = jnp.float32
BF16 = jnp.bfloat16
CODE = jnp.int16
AXES = ("row", "col")


def split_id(dev):
    row, col = dev // 8, dev % 8
    return row // 8, (row // 2) % 4, row % 2, col // 4, col % 4


def join_id(zl, x, core, zh, y):
    return ((zl * 4 + x) * 2 + core) * 8 + zh * 4 + y


def send(value, where):
    pairs = [(dev, join_id(*where(*split_id(dev)))) for dev in range(256)]
    return lax.ppermute(value, AXES, pairs)


def to_core(value):
    return send(value, lambda zl, x, core, zh, y: (zl, x, core ^ 1, zh, y))


def to_x(value, k):
    return send(value, lambda zl, x, core, zh, y: (zl, x ^ k, core, zh, y))


def along_x(value, k):
    return send(value, lambda zl, x, core, zh, y: (zl, (x + k) % 4, core, zh, y))


def to_zl(value, k):
    return send(value, lambda zl, x, core, zh, y: (zl ^ k, x, core, zh, y))


def to_y(value, k):
    return send(value, lambda zl, x, core, zh, y: (zl, x, core, zh, y ^ k))


def to_zh(value):
    return send(value, lambda zl, x, core, zh, y: (zl, x, core, zh ^ 1, y))


def plane_spot(zl, x, core, zh, y):
    h, bit = x % 2, y // 2
    x_to = (x + (2 * h - 1) * bit) % 4
    z_to = 2 * (zh ^ (zl // 2) ^ (zl % 2)) + (core ^ (zl // 2))
    return z_to, x_to, core ^ (y % 2), zl // 2, 2 * (zl % 2) + x // 2


def to_plane(value):
    return send(value, plane_spot)


def chunk_spot(zl, x, zh, y):
    u = (x - 2 * (y % 2)) % 4
    h = jnp.where((u == 1) | (u == 2), 1, 0)
    bit = jnp.where(u >= 2, 1, 0)
    return 8 * h + 4 * ((zl % 2) ^ zh) + 2 * ((zl // 2) ^ zh ^ (y // 2)) + bit


def encode(value):
    peak = jnp.max(jnp.abs(value), axis=0, keepdims=True)
    power = jnp.floor(jnp.log2(jnp.maximum(peak, 1e-30))) + 1.0
    scaled = jnp.round(value * jnp.exp2(15.0 - power))
    code = jnp.clip(scaled, -32767.0, 32767.0).astype(jnp.int32).astype(CODE)
    mark = jnp.broadcast_to(power, (16, value.shape[1])).astype(jnp.int32).astype(CODE)
    return code, mark


def decode(code, mark):
    return code.astype(jnp.int32).astype(F32) * jnp.exp2(mark.astype(jnp.int32).astype(F32) - 15.0)


def first_kernel(scal, near, far, a0, b0, a1, b1, a2, b2, acc_ref, wide):
    step = pl.program_id(0)

    @pl.when(step == 0)
    def _():
        for k, group in enumerate(((a0, a1, a2), (b0, b1, b2))):
            for m, piece in enumerate(group):
                for z in range(4):
                    at = (4 * m + z) * 256
                    live = scal[34 + 2 * scal[4 * m + z] + k] > 0
                    value = jnp.where(live, piece[z], jnp.zeros((256, 256), BF16))
                    wide[at : at + 256, k * 256 : (k + 1) * 256] = value

    def work(blocks):
        acc = jnp.zeros((256, 512), F32)
        for pos in range(12):
            acc += jnp.dot(
                blocks[0, scal[pos]],
                wide[pos * 256 : (pos + 1) * 256, :],
                preferred_element_type=F32,
            )
        acc_ref[0] = acc

    @pl.when(step < 4)
    def _():
        work(near)

    @pl.when(step >= 4)
    def _():
        work(far)


def second_kernel(
    scal, acc_in, near, far, a3, b3, left_near, left_far, own, q1, q2, q3, diag_ref, wide
):
    step = pl.program_id(0)

    @pl.when(step == 0)
    def _():
        diag_ref[...] = jnp.zeros_like(diag_ref)
        for k, piece in enumerate((a3, b3)):
            for z in range(4):
                live = scal[34 + 2 * scal[12 + z] + k] > 0
                value = jnp.where(live, piece[z], jnp.zeros((256, 256), BF16))
                wide[z * 256 : (z + 1) * 256, k * 256 : (k + 1) * 256] = value

    half = lax.rem(step, 4) // 2
    zrel = half ^ scal[33]
    side = step // 4

    def work(blocks, left):
        acc = acc_in[0]
        for z in range(4):
            acc += jnp.dot(
                blocks[0, scal[12 + z] & 7],
                wide[z * 256 : (z + 1) * 256, :],
                preferred_element_type=F32,
            )
        for k in range(2):
            live = (-scal[16 + 2 * step + k]).astype(F32)
            term = acc[:, k * 256 : (k + 1) * 256] * live
            high = term.astype(BF16)
            rest = (term - high.astype(F32)).astype(BF16)
            both = jnp.concatenate([high, rest], axis=1)
            both = jnp.dot(left[k, 0], both, preferred_element_type=F32)
            diag_ref[k] += both[:, :256] + both[:, 256:]
            to = (2 * lax.rem(step, 2) + k) ^ scal[32]

            @pl.when(to == 0)
            def _():
                own[zrel, side] = term

            @pl.when(to != 0)
            def _():
                code, mark = encode(term)
                for m, ref in ((1, q1), (2, q2), (3, q3)):

                    @pl.when(to == m)
                    def _():
                        ref[zrel, side, 0:256] = code
                        ref[zrel, side, 256:272] = mark

    @pl.when(step < 4)
    def _():
        work(near, left_near)

    @pl.when(step >= 4)
    def _():
        work(far, left_far)


def early(i):
    return jnp.minimum(i, 3)


def late(i):
    return jnp.maximum(i - 4, 0)


def full(shape):
    return pl.BlockSpec(shape, lambda i, s: (0,) * len(shape))


PARAMS = pltpu.CompilerParams(dimension_semantics=("arbitrary",), vmem_limit_bytes=48 * 2**20)


def first_products(scal, near, far, pieces):
    return pl.pallas_call(
        first_kernel,
        grid_spec=pltpu.PrefetchScalarGridSpec(
            num_scalar_prefetch=1,
            grid=(8,),
            in_specs=[
                pl.BlockSpec((1, 16, 256, 256), lambda i, s: (early(i), 0, 0, 0)),
                pl.BlockSpec((1, 16, 256, 256), lambda i, s: (late(i), 0, 0, 0)),
            ]
            + [full(p.shape) for p in pieces],
            out_specs=pl.BlockSpec((1, 256, 512), lambda i, s: (i, 0, 0)),
            scratch_shapes=[pltpu.VMEM((3072, 512), BF16)],
        ),
        out_shape=jax.ShapeDtypeStruct((8, 256, 512), F32),
        cost_estimate=pl.CostEstimate(
            flops=2 * 2048 * 3072 * 512, transcendentals=0, bytes_accessed=24 * 2**20
        ),
        compiler_params=PARAMS,
    )(scal, near, far, *pieces)


def second_products(scal, acc, near, far, pieces, left_near, left_far):
    return pl.pallas_call(
        second_kernel,
        grid_spec=pltpu.PrefetchScalarGridSpec(
            num_scalar_prefetch=1,
            grid=(8,),
            in_specs=[
                pl.BlockSpec((1, 256, 512), lambda i, s: (i, 0, 0)),
                pl.BlockSpec((1, 8, 256, 256), lambda i, s: (early(i), s[12] // 8, 0, 0)),
                pl.BlockSpec((1, 8, 256, 256), lambda i, s: (late(i), s[12] // 8, 0, 0)),
            ]
            + [full(p.shape) for p in pieces]
            + [
                pl.BlockSpec((2, 1, 256, 256), lambda i, s: (0, early(i), 0, 0)),
                pl.BlockSpec((2, 1, 256, 256), lambda i, s: (0, late(i), 0, 0)),
            ],
            out_specs=[
                full((2, 2, 256, 256)),
                full((2, 2, 272, 256)),
                full((2, 2, 272, 256)),
                full((2, 2, 272, 256)),
                full((2, 256, 256)),
            ],
            scratch_shapes=[pltpu.VMEM((1024, 512), BF16)],
        ),
        out_shape=[jax.ShapeDtypeStruct((2, 2, 256, 256), F32)]
        + [jax.ShapeDtypeStruct((2, 2, 272, 256), CODE)] * 3
        + [jax.ShapeDtypeStruct((2, 256, 256), F32)],
        cost_estimate=pl.CostEstimate(
            flops=2 * 2048 * 1024 * 512, transcendentals=0, bytes_accessed=16 * 2**20
        ),
        compiler_params=PARAMS,
    )(scal, acc, near, far, *pieces, left_near, left_far)


def total_kernel(own, q1, q2, q3, keep, give):
    for z in range(2):
        for side in range(2):
            value = own[z, side]
            for ref in (q1, q2, q3):
                value += decode(ref[z, side, 0:256], ref[z, side, 256:257])
            if z == 0:
                keep[side] = value
            else:
                code, mark = encode(value)
                give[side, 0:256] = code
                give[side, 256:272] = mark


def totals(own, others):
    return pl.pallas_call(
        total_kernel,
        out_shape=[
            jax.ShapeDtypeStruct((2, 256, 256), F32),
            jax.ShapeDtypeStruct((2, 272, 256), CODE),
        ],
        compiler_params=pltpu.CompilerParams(vmem_limit_bytes=32 * 2**20),
    )(own, *others)


def products(scal, near, far, pieces, left_near, left_far):
    early = lambda i: jnp.minimum(i, 3)
    late = lambda i: jnp.maximum(i - 4, 0)
    full = lambda shape: pl.BlockSpec(shape, lambda i, s: (0,) * len(shape))
    return pl.pallas_call(
        product_kernel,
        grid_spec=pltpu.PrefetchScalarGridSpec(
            num_scalar_prefetch=1,
            grid=(8,),
            in_specs=[
                pl.BlockSpec((1, 16, 256, 256), lambda i, s: (early(i), 0, 0, 0)),
                pl.BlockSpec((1, 16, 256, 256), lambda i, s: (late(i), 0, 0, 0)),
            ]
            + [full(p.shape) for p in pieces]
            + [
                pl.BlockSpec((2, 1, 256, 256), lambda i, s: (0, early(i), 0, 0)),
                pl.BlockSpec((2, 1, 256, 256), lambda i, s: (0, late(i), 0, 0)),
            ],
            out_specs=[
                full((2, 2, 256, 256)),
                full((2, 2, 272, 256)),
                full((2, 2, 272, 256)),
                full((2, 2, 272, 256)),
                full((2, 256, 256)),
            ],
            scratch_shapes=[pltpu.VMEM((4096, 2 * 256), BF16)],
        ),
        out_shape=[jax.ShapeDtypeStruct((2, 2, 256, 256), F32)]
        + [jax.ShapeDtypeStruct((2, 2, 272, 256), CODE)] * 3
        + [jax.ShapeDtypeStruct((2, 256, 256), F32)],
        cost_estimate=pl.CostEstimate(
            flops=2 * 2048 * 4096 * 2 * 256, transcendentals=0, bytes_accessed=24 * 2**20
        ),
        compiler_params=pltpu.CompilerParams(
            dimension_semantics=("arbitrary",), vmem_limit_bytes=48 * 2**20
        ),
    )(scal, near, far, *pieces, left_near, left_far)


def body(ancestors, panel_one, present_one, dinv_one, panel_two, present_two, dinv_two):
    row = lax.axis_index("row")
    col = lax.axis_index("col")
    zl, x, core = row // 8, (row // 2) % 4, row % 2
    zh, y = col // 4, col % 4
    first = core == 0
    tie = lambda *values: lax.optimization_barrier(values)

    with jax.named_scope("spread"):
        take = lambda value: lax.dynamic_index_in_dim(value, 2 * zh + y // 2, 1, keepdims=False)
        own = to_plane(jnp.where(core == y % 2, take(panel_one), take(panel_two)))

    with jax.named_scope("swap"):
        other_blocks = to_core(ancestors)
        held_one, held_two, own = tie(panel_one, panel_two, own)
        mine = jnp.swapaxes(jnp.where(first, held_one, held_two), 2, 3)
        theirs = to_core(jnp.swapaxes(jnp.where(first, held_two, held_one), 2, 3))

    present = jnp.where(first, present_one, present_two)
    x_from = ((x + jnp.array([0, 3, 1, 2], jnp.int32)) % 4)[:, None]
    z_from = (zl ^ jnp.arange(4, dtype=jnp.int32))[None, :]
    spots = chunk_spot(z_from, x_from, zh, y)
    live_near = lax.dynamic_slice_in_dim(present, 4 * row, 4, 1)
    live_far = lax.dynamic_slice_in_dim(present, 4 * (row ^ 1), 4, 1)
    scal = jnp.concatenate(
        [
            spots.reshape(16),
            jnp.transpose(live_near).reshape(8),
            jnp.transpose(live_far).reshape(8),
            jnp.stack([y, zh]),
            jnp.transpose(lax.dynamic_slice_in_dim(present, 16 * col, 16, 1)).reshape(32),
        ]
    ).astype(jnp.int32)

    with jax.named_scope("gather"):
        parts = [own] + [to_zl(own, k) for k in (1, 2, 3)]
        a0, b0 = [jnp.stack([part[k] for part in parts]) for k in range(2)]
        a0, b0, other_blocks, theirs = tie(a0, b0, other_blocks, theirs)
        a1, b2 = along_x(a0, 1), along_x(b0, -1)
        b1, a2 = along_x(b0, 1), along_x(a0, -1)
        a3, b3 = along_x(a1, 1), along_x(b2, -1)
    with jax.named_scope("product"):
        acc = first_products(scal, ancestors, other_blocks, [a0, b0, a1, b1, a2, b2])
        out = second_products(scal, acc, ancestors, other_blocks, [a3, b3], mine, theirs)

    def shares(value, spot, move):
        at = lambda k: lax.dynamic_index_in_dim(value, spot ^ k, 0, keepdims=False)
        one, two, three = [move(at(k), k) for k in (1, 2, 3)]
        return (at(0) + one) + (two + three)

    def collect(value, spot, move):
        stack = jnp.stack([value] + [move(value, k) for k in (1, 2, 3)])
        return jnp.stack(
            [lax.dynamic_index_in_dim(stack, spot ^ k, 0, keepdims=False) for k in range(4)]
        )

    with jax.named_scope("diag"):
        piece = shares(out[4].reshape(4, 128, 256), y, to_y)
        piece = shares(piece.reshape(4, 32, 256), x, to_x)
        one, two, three = [to_zl(piece, k) for k in (1, 2, 3)]
        piece = (piece + one) + (two + three)
        piece = piece + to_zh(piece)
    with jax.named_scope("column"):
        keep, give = totals(out[0], [to_y(out[m], m) for m in (1, 2, 3)])
        got = to_zh(give)
        block = keep + decode(got[:, :256], got[:, 256:257])
    with jax.named_scope("back"):
        piece = tie(piece, keep)[0]
        part = collect(piece, x, to_x).reshape(128, 256)
        whole = collect(part, y, to_y).reshape(2, 256, 256)
        near, far = block[0], to_core(block[1])
        whole = tie(whole, far)[0]
        partner = to_core(whole)
    return (
        jnp.where(first, near, far)[None],
        dinv_one.astype(F32) - jnp.where(first, whole, partner),
        jnp.where(first, far, near)[None],
        dinv_two.astype(F32) - jnp.where(first, partner, whole),
    )


def solution(mesh):
    in_specs = (
        P("row", "col", None, None),
        P(None, "row", None, None),
        P(),
        P(),
        P(None, "row", None, None),
        P(),
        P(),
    )
    out_specs = (P(("row", "col"), None, None), P(), P(("row", "col"), None, None), P())
    return jax.shard_map(body, mesh=mesh, in_specs=in_specs, out_specs=out_specs, check_vma=False)
```

time: 189 us -> 177 us (0.937)
  other arithmetic: 9.73 us -> 5.26 us
  local copies, waits for them, and re-layouts: 13.8 us -> 9.38 us
  Pallas kernels: 30.9 us -> 28 us
    squeeze x5 -> x3, local copies, waits for them, and re-layouts: 4.37 us -> 0.06 us  [the longest x2 0.04 us: shares(): at = lambda k: lax.dynamic_index_in_dim(value, spot ^ k, 0, keepdims=False)]
    unnamed x21 -> x15, local copies, waits for them, and re-layouts: 5.48 us -> 2.46 us
    optimization_barrier x0 -> x2, local copies, waits for them, and re-layouts: none -> 2.95 us  [body(): tie = lambda *values: lax.optimization_barrier(values)]
    slice x2 -> x4, local copies, waits for them, and re-layouts: 0.07 us -> 2.98 us  [body(): a0, b0 = [jnp.stack([part[k] for part in parts]) for k in range(2)]]
    pallas_call x4 -> x3, Pallas kernels: 30.9 us -> 28 us  [the longest x1 14.6 us: first_products(): pl.pallas_call(first_kernel, grid_spec=pltpu.PrefetchScalarGridSpec(num_s...]
    ppermute x2 -> x0, local copies, waits for them, and re-layouts: 2.15 us -> none  [send(): return lax.ppermute(value, AXES, pairs)]
    another operation x4 -> x5, other arithmetic: 2.14 us -> 0.23 us  [the longest x1 0.13 us: body(): a0, b0 = [jnp.stack([part[k] for part in parts]) for k in range(2)]]
    ppermute x39 -> x34, starting transfers between devices: 86.3 us -> 85.1 us  [send(): return lax.ppermute(value, AXES, pairs)]
  transfers between devices with their start and end apart: 39 -> 34, of which waited for: 16 -> 11; matrix products, arithmetic and copies ran while one was open for 10% -> 6% of each run, Pallas kernels for 16% -> 8%
where the time goes in v3:
time: 177 us; the launch traced here: 174 us
  starting transfers between devices  85.1 us (48%)
  waiting for transfers between devices  44.8 us (25%)
  Pallas kernels  28 us (16%)
  local copies, waits for them, and re-layouts  9.38 us (5%)
  other arithmetic  5.26 us (3%)
    ppermute x34, starting transfers between devices, send(): return lax.ppermute(value, AXES, pairs)  85.1 us
    ppermute x34, waiting for transfers between devices, send(): return lax.ppermute(value, AXES, pairs)  44.8 us
    pallas_call x1, Pallas kernels, first_products(): pl.pallas_call(first_kernel, grid_spec=pltpu.PrefetchScalarGridSpec(num_s...  14.6 us
    pallas_call x1, Pallas kernels, second_products(): pl.pallas_call(second_kernel, grid_spec=pltpu.PrefetchScalarGridSpec(num_...  12.6 us
  transfers between devices with their start and end apart: 34, of which 11 were waited for; matrix products, arithmetic and copies ran while one was open for 6% of the time, Pallas kernels for 8%

profile of v3, /device:TPU:1, one launch (start us, length us, event | category | flops | bytes accessed | tf_op | source)
XLA Modules:
  0.0 173.6 jit_solution(9398667719635811087)
XLA Ops:
  0.7 3.3 %collective-permute-start.4 = (bf16[4,16,256,256]{3,2,1,0:T(8,128)(2,1)}, bf16[4,16,256,256]{3,2,1,0:T(8,128)(2,1)}, u32[]{:S(2)}, u32[]{:S(2)}) collective-permute-start(bf16[4,16,256,256]{3,2,1,0:T(8,128)(2,1)} %near.3), channel_id=1, source_target_pairs={{0,8},{1,9},{2,10},{3,11},{4,12},{5,13},{6,14},{7,15},{8,0},{9,1},... | collective-permute-start | bytes 25165832 | tf_op jit(solution)/shard_map/swap/ppermute | solution.py:25
  7.7 5.0 %collective-permute-done = bf16[2,256,256]{2,1,0:T(8,128)(2,1)S(1)} collective-permute-done((bf16[2,256,256]{2,1,0:T(8,128)(2,1)S(1)}, bf16[2,256,256]{2,1,0:T(8,128)(2,1)S(1)}, u32[]{:S(2)}, u32[]{:S(2)}) %collective-permute-start) | collective-permute-done | bytes 262176 | tf_op jit(solution)/shard_map/spread/ppermute | solution.py:25
  12.7 5.1 %collective-permute-start.1 = (bf16[2,256,256]{2,1,0:T(8,128)(2,1)S(1)}, bf16[2,256,256]{2,1,0:T(8,128)(2,1)}, u32[]{:S(2)}, u32[]{:S(2)}) collective-permute-start(bf16[2,256,256]{2,1,0:T(8,128)(2,1)S(1)} %collective-permute-done), channel_id=1, source_target_pairs={{0,64},{1,65},{2,66},{3,67},{4,68},{5,69},{6,70},{7,71},{8,72},{9,... | collective-permute-start | bytes 786440 | tf_op jit(solution)/shard_map/gather/ppermute | solution.py:25
  17.8 5.5 %collective-permute-start.2 = (bf16[2,256,256]{2,1,0:T(8,128)(2,1)S(1)}, bf16[2,256,256]{2,1,0:T(8,128)(2,1)}, u32[]{:S(2)}, u32[]{:S(2)}) collective-permute-start(bf16[2,256,256]{2,1,0:T(8,128)(2,1)S(1)} %collective-permute-done), channel_id=1, source_target_pairs={{0,128},{1,129},{2,130},{3,131},{4,132},{5,133},{6,134},{7,135},{8... | collective-permute-start | bytes 786440 | tf_op jit(solution)/shard_map/gather/ppermute | solution.py:25
  30.0 12.1 %collective-permute-done.3 = bf16[2,256,256]{2,1,0:T(8,128)(2,1)} collective-permute-done((bf16[2,256,256]{2,1,0:T(8,128)(2,1)S(1)}, bf16[2,256,256]{2,1,0:T(8,128)(2,1)}, u32[]{:S(2)}, u32[]{:S(2)}) %collective-permute-start.3) | collective-permute-done | bytes 262176 | tf_op jit(solution)/shard_map/gather/ppermute | solution.py:25
  44.5 3.6 %collective-permute-start.8 = (bf16[4,256,256]{2,1,0:T(8,128)(2,1)S(1)}, bf16[4,256,256]{2,1,0:T(8,128)(2,1)S(1)}, u32[]{:S(2)}, u32[]{:S(2)}) collective-permute-start(bf16[4,256,256]{2,1,0:T(8,128)(2,1)S(1)} %get-tuple-element.24.a0), channel_id=1, source_target_pairs={{0,48},{1,49},{2,50},{3,51},{4,52},{5,53},{6,54},{7,55},{8,56},{9,... | collective-permute-start | bytes 1572872 | tf_op jit(solution)/shard_map/gather/ppermute | solution.py:25
  48.1 2.7 %collective-permute-start.9 = (bf16[4,256,256]{2,1,0:T(8,128)(2,1)S(1)}, bf16[4,256,256]{2,1,0:T(8,128)(2,1)}, u32[]{:S(2)}, u32[]{:S(2)}) collective-permute-start(bf16[4,256,256]{2,1,0:T(8,128)(2,1)S(1)} %get-tuple-element.25.b0), channel_id=1, source_target_pairs={{0,48},{1,49},{2,50},{3,51},{4,52},{5,53},{6,54},{7,55},{8,56},{9,... | collective-permute-start | bytes 1572872 | tf_op jit(solution)/shard_map/gather/ppermute | solution.py:25
  51.8 5.8 %collective-permute-done.6.a1 = bf16[4,256,256]{2,1,0:T(8,128)(2,1)S(1)} collective-permute-done((bf16[4,256,256]{2,1,0:T(8,128)(2,1)S(1)}, bf16[4,256,256]{2,1,0:T(8,128)(2,1)S(1)}, u32[]{:S(2)}, u32[]{:S(2)}) %collective-permute-start.6) | collective-permute-done | bytes 524320 | tf_op jit(solution)/shard_map/gather/ppermute | solution.py:25
  57.6 10.3 %collective-permute-done.9.b2 = bf16[4,256,256]{2,1,0:T(8,128)(2,1)} collective-permute-done((bf16[4,256,256]{2,1,0:T(8,128)(2,1)S(1)}, bf16[4,256,256]{2,1,0:T(8,128)(2,1)}, u32[]{:S(2)}, u32[]{:S(2)}) %collective-permute-start.9) | collective-permute-done | bytes 524320 | tf_op jit(solution)/shard_map/gather/ppermute | solution.py:25
  67.9 3.5 %collective-permute-start.11 = (bf16[4,256,256]{2,1,0:T(8,128)(2,1)}, bf16[4,256,256]{2,1,0:T(8,128)(2,1)S(1)}, u32[]{:S(2)}, u32[]{:S(2)}) collective-permute-start(bf16[4,256,256]{2,1,0:T(8,128)(2,1)} %collective-permute-done.9.b2), channel_id=1, source_target_pairs={{0,48},{1,49},{2,50},{3,51},{4,52},{5,53},{6,54},{7,55},{8,56},{9,... | collective-permute-start | bytes 1572872 | tf_op jit(solution)/shard_map/gather/ppermute | solution.py:25
  71.4 14.6 %product.2.acc_in = f32[8,256,512]{2,1,0:T(8,128)} custom-call(s32[66]{0:T(128)S(1)} %concatenate.3.scal, bf16[4,16,256,256]{3,2,1,0:T(8,128)(2,1)} %near.3, bf16[4,16,256,256]{3,2,1,0:T(8,128)(2,1)} %collective-permute-done.4.far, bf16[4,256,256]{2,1,0:T(8,128)(2,1)S(1)} %get-tuple-element.24.a0, bf16[4,256,256]{2,1,0:T(8,128)(2,1)S(1)} %get-tuple-element.25.b0, ...), custom_call_target="tpu_custom_call" | custom-call | flops 6442450944 | bytes 25165824 | tf_op jit(solution)/shard_map/product/pallas_call | solution.py:190
  86.0 12.6 %product.3 = (f32[2,2,256,256]{3,2,1,0:T(8,128)S(1)}, s16[2,2,272,256]{3,2,1,0:T(8,128)(2,1)S(1)}, s16[2,2,272,256]{3,2,1,0:T(8,128)(2,1)S(1)}, s16[2,2,272,256]{3,2,1,0:T(8,128)(2,1)S(1)}, f32[2,256,256]{2,1,0:T(8,128)S(1)}) custom-call(s32[66]{0:T(128)S(1)} %concatenate.3.scal, f32[8,256,512]{2,1,0:T(8,128)} %product.2.acc_in, ...), custom_call_target="tpu_custom_call" | custom-call | flops 2147483648 | bytes 16777216 | tf_op jit(solution)/shard_map/product/pallas_call | solution.py:212
  101.1 4.8 %collective-permute-start.17 = (f32[128,256]{1,0:T(8,128)S(1)}, f32[128,256]{1,0:T(8,128)S(1)}, u32[]{:S(2)}, u32[]{:S(2)}) collective-permute-start(f32[128,256]{1,0:T(8,128)S(1)} %get-tuple-element.50), channel_id=1, source_target_pairs={{0,1},{1,0},{2,3},{3,2},{4,5},{5,4},{6,7},{7,6},{8,9},{9,8},{10,11... | collective-permute-start | bytes 393224 | tf_op jit(solution)/shard_map/diag/ppermute | solution.py:25
  106.0 2.5 %collective-permute-start.19 = (f32[128,256]{1,0:T(8,128)S(1)}, f32[128,256]{1,0:T(8,128)S(1)}, u32[]{:S(2)}, u32[]{:S(2)}) collective-permute-start(f32[128,256]{1,0:T(8,128)S(1)} %get-tuple-element.48), channel_id=1, source_target_pairs={{0,3},{1,2},{2,1},{3,0},{4,7},{5,6},{6,5},{7,4},{8,11},{9,10},{10,... | collective-permute-start | bytes 393224 | tf_op jit(solution)/shard_map/diag/ppermute | solution.py:25
  108.5 2.9 %collective-permute-done.18 = f32[128,256]{1,0:T(8,128)S(1)} collective-permute-done((f32[128,256]{1,0:T(8,128)S(1)}, f32[128,256]{1,0:T(8,128)S(1)}, u32[]{:S(2)}, u32[]{:S(2)}) %collective-permute-start.18) | collective-permute-done | bytes 131104 | tf_op jit(solution)/shard_map/diag/ppermute | solution.py:25
  116.7 4.1 %collective-permute-start.13 = (s16[2,2,272,256]{3,2,1,0:T(8,128)(2,1)}, s16[2,2,272,256]{3,2,1,0:T(8,128)(2,1)S(1)}, u32[]{:S(2)}, u32[]{:S(2)}) collective-permute-start(s16[2,2,272,256]{3,2,1,0:T(8,128)(2,1)} %copy-done.1), channel_id=1, source_target_pairs={{0,2},{1,3},{2,0},{3,1},{4,6},{5,7},{6,4},{7,5},{8,10},{9,11},{10,... | collective-permute-start | bytes 1671176 | tf_op jit(solution)/shard_map/column/ppermute | solution.py:25
  120.8 5.0 %collective-permute-start.23 = (f32[32,256]{1,0:T(8,128)S(1)}, f32[32,256]{1,0:T(8,128)S(1)}, u32[]{:S(2)}, u32[]{:S(2)}) collective-permute-start(f32[32,256]{1,0:T(8,128)S(1)} %fusion.2), channel_id=1, source_target_pairs={{0,64},{1,65},{2,66},{3,67},{4,68},{5,69},{6,70},{7,71},{8,72},{9,... | collective-permute-start | bytes 98312 | tf_op jit(solution)/shard_map/diag/ppermute | solution.py:25
  125.8 2.2 %collective-permute-start.24 = (f32[32,256]{1,0:T(8,128)S(1)}, f32[32,256]{1,0:T(8,128)S(1)}, u32[]{:S(2)}, u32[]{:S(2)}) collective-permute-start(f32[32,256]{1,0:T(8,128)S(1)} %fusion.2), channel_id=1, source_target_pairs={{0,128},{1,129},{2,130},{3,131},{4,132},{5,133},{6,134},{7,135},{8... | collective-permute-start | bytes 98312 | tf_op jit(solution)/shard_map/diag/ppermute | solution.py:25
  128.0 2.7 %collective-permute-start.25 = (f32[32,256]{1,0:T(8,128)S(1)}, f32[32,256]{1,0:T(8,128)S(1)}, u32[]{:S(2)}, u32[]{:S(2)}) collective-permute-start(f32[32,256]{1,0:T(8,128)S(1)} %fusion.2), channel_id=1, source_target_pairs={{0,192},{1,193},{2,194},{3,195},{4,196},{5,197},{6,198},{7,199},{8... | collective-permute-start | bytes 98312 | tf_op jit(solution)/shard_map/diag/ppermute | solution.py:25
  132.6 6.4 %collective-permute-start.26 = (f32[32,256]{1,0:T(8,128)S(1)}, f32[32,256]{1,0:T(8,128)S(1)}, u32[]{:S(2)}, u32[]{:S(2)}) collective-permute-start(f32[32,256]{1,0:T(8,128)S(1)} %add_add_fusion), channel_id=1, source_target_pairs={{0,4},{1,5},{2,6},{3,7},{4,0},{5,1},{6,2},{7,3},{8,12},{9,13},{10,... | collective-permute-start | bytes 98312 | tf_op jit(solution)/shard_map/diag/ppermute | solution.py:25
  140.5 2.6 %collective-permute-done.13.q2 = s16[2,2,272,256]{3,2,1,0:T(8,128)(2,1)S(1)} collective-permute-done((s16[2,2,272,256]{3,2,1,0:T(8,128)(2,1)}, s16[2,2,272,256]{3,2,1,0:T(8,128)(2,1)S(1)}, u32[]{:S(2)}, u32[]{:S(2)}) %collective-permute-start.13) | collective-permute-done | bytes 557088 | tf_op jit(solution)/shard_map/column/ppermute | solution.py:25
  144.8 3.0 %collective-permute-start.29 = (f32[32,256]{1,0:T(8,128)S(1)}, f32[32,256]{1,0:T(8,128)S(1)}, u32[]{:S(2)}, u32[]{:S(2)}) collective-permute-start(f32[32,256]{1,0:T(8,128)S(1)} %add.217), channel_id=1, source_target_pairs={{0,48},{1,49},{2,50},{3,51},{4,52},{5,53},{6,54},{7,55},{8,56},{9,... | collective-permute-start | bytes 98312 | tf_op jit(solution)/shard_map/back/ppermute | solution.py:25
  147.8 5.7 %collective-permute-start.15 = (s16[2,272,256]{2,1,0:T(8,128)(2,1)S(1)}, s16[2,272,256]{2,1,0:T(8,128)(2,1)S(1)}, u32[]{:S(2)}, u32[]{:S(2)}) collective-permute-start(s16[2,272,256]{2,1,0:T(8,128)(2,1)S(1)} %get-tuple-element.32), channel_id=1, source_target_pairs={{0,4},{1,5},{2,6},{3,7},{4,0},{5,1},{6,2},{7,3},{8,12},{9,13},{10,... | collective-permute-start | bytes 835592 | tf_op jit(solution)/shard_map/column/ppermute | solution.py:25
  157.7 9.8 %collective-permute-start.16 = (f32[256,256]{1,0:T(8,128)S(1)}, f32[256,256]{1,0:T(8,128)S(1)}, u32[]{:S(2)}, u32[]{:S(2)}) collective-permute-start(f32[256,256]{1,0:T(8,128)S(1)} %slice_bitcast_fusion), channel_id=1, source_target_pairs={{0,8},{1,9},{2,10},{3,11},{4,12},{5,13},{6,14},{7,15},{8,0},{9,1},... | collective-permute-start | bytes 786440 | tf_op jit(solution)/shard_map/back/ppermute | solution.py:25
  (103 shorter events, 36.8 us)
Async XLA Ops:
  0.7 42.6 %collective-permute-start.4 = (bf16[4,16,256,256]{3,2,1,0:T(8,128)(2,1)}, bf16[4,16,256,256]{3,2,1,0:T(8,128)(2,1)}, u32[]{:S(2)}, u32[]{:S(2)}) collective-permute-start(bf16[4,16,256,256]{3,2,1,0:T(8,128)(2,1)} %near.3), channel_id=1, source_target_pairs={{0,8},{1,9},{2,10},{3,11},{4,12},{5,13},{6,14},{7,15},{8,0},{9,1},... | collective-permute-start | bytes 25165832 | tf_op jit(solution)/shard_map/swap/ppermute | solution.py:25
  12.7 15.3 %collective-permute-start.1 = (bf16[2,256,256]{2,1,0:T(8,128)(2,1)S(1)}, bf16[2,256,256]{2,1,0:T(8,128)(2,1)}, u32[]{:S(2)}, u32[]{:S(2)}) collective-permute-start(bf16[2,256,256]{2,1,0:T(8,128)(2,1)S(1)} %collective-permute-done), channel_id=1, source_target_pairs={{0,64},{1,65},{2,66},{3,67},{4,68},{5,69},{6,70},{7,71},{8,72},{9,... | collective-permute-start | bytes 786440 | tf_op jit(solution)/shard_map/gather/ppermute | solution.py:25
  17.8 11.2 %collective-permute-start.2 = (bf16[2,256,256]{2,1,0:T(8,128)(2,1)S(1)}, bf16[2,256,256]{2,1,0:T(8,128)(2,1)}, u32[]{:S(2)}, u32[]{:S(2)}) collective-permute-start(bf16[2,256,256]{2,1,0:T(8,128)(2,1)S(1)} %collective-permute-done), channel_id=1, source_target_pairs={{0,128},{1,129},{2,130},{3,131},{4,132},{5,133},{6,134},{7,135},{8... | collective-permute-start | bytes 786440 | tf_op jit(solution)/shard_map/gather/ppermute | solution.py:25
  23.3 18.8 %collective-permute-start.3 = (bf16[2,256,256]{2,1,0:T(8,128)(2,1)S(1)}, bf16[2,256,256]{2,1,0:T(8,128)(2,1)}, u32[]{:S(2)}, u32[]{:S(2)}) collective-permute-start(bf16[2,256,256]{2,1,0:T(8,128)(2,1)S(1)} %collective-permute-done), channel_id=1, source_target_pairs={{0,192},{1,193},{2,194},{3,195},{4,196},{5,197},{6,198},{7,199},{8... | collective-permute-start | bytes 786440 | tf_op jit(solution)/shard_map/gather/ppermute | solution.py:25
  27.1 16.1 %collective-permute-start.5 = (bf16[2,4,256,256]{3,2,1,0:T(8,128)(2,1)S(1)}, bf16[2,4,256,256]{3,2,1,0:T(8,128)(2,1)S(1)}, u32[]{:S(2)}, u32[]{:S(2)}) collective-permute-start(bf16[2,4,256,256]{3,2,1,0:T(8,128)(2,1)S(1)} %get-tuple-element.39), channel_id=1, source_target_pairs={{0,8},{1,9},{2,10},{3,11},{4,12},{5,13},{6,14},{7,15},{8,0},{9,1},... | collective-permute-start | bytes 3145736 | tf_op jit(solution)/shard_map/swap/ppermute | solution.py:25
  43.2 14.3 %collective-permute-start.6 = (bf16[4,256,256]{2,1,0:T(8,128)(2,1)S(1)}, bf16[4,256,256]{2,1,0:T(8,128)(2,1)S(1)}, u32[]{:S(2)}, u32[]{:S(2)}) collective-permute-start(bf16[4,256,256]{2,1,0:T(8,128)(2,1)S(1)} %get-tuple-element.24.a0), channel_id=1, source_target_pairs={{0,16},{1,17},{2,18},{3,19},{4,20},{5,21},{6,22},{7,23},{8,24},{9,... | collective-permute-start | bytes 1572872 | tf_op jit(solution)/shard_map/gather/ppermute | solution.py:25
  44.5 26.9 %collective-permute-start.8 = (bf16[4,256,256]{2,1,0:T(8,128)(2,1)S(1)}, bf16[4,256,256]{2,1,0:T(8,128)(2,1)S(1)}, u32[]{:S(2)}, u32[]{:S(2)}) collective-permute-start(bf16[4,256,256]{2,1,0:T(8,128)(2,1)S(1)} %get-tuple-element.24.a0), channel_id=1, source_target_pairs={{0,48},{1,49},{2,50},{3,51},{4,52},{5,53},{6,54},{7,55},{8,56},{9,... | collective-permute-start | bytes 1572872 | tf_op jit(solution)/shard_map/gather/ppermute | solution.py:25
  48.1 23.2 %collective-permute-start.7 = (bf16[4,256,256]{2,1,0:T(8,128)(2,1)S(1)}, bf16[4,256,256]{2,1,0:T(8,128)(2,1)}, u32[]{:S(2)}, u32[]{:S(2)}) collective-permute-start(bf16[4,256,256]{2,1,0:T(8,128)(2,1)S(1)} %get-tuple-element.25.b0), channel_id=1, source_target_pairs={{0,16},{1,17},{2,18},{3,19},{4,20},{5,21},{6,22},{7,23},{8,24},{9,... | collective-permute-start | bytes 1572872 | tf_op jit(solution)/shard_map/gather/ppermute | solution.py:25
  48.1 19.7 %collective-permute-start.9 = (bf16[4,256,256]{2,1,0:T(8,128)(2,1)S(1)}, bf16[4,256,256]{2,1,0:T(8,128)(2,1)}, u32[]{:S(2)}, u32[]{:S(2)}) collective-permute-start(bf16[4,256,256]{2,1,0:T(8,128)(2,1)S(1)} %get-tuple-element.25.b0), channel_id=1, source_target_pairs={{0,48},{1,49},{2,50},{3,51},{4,52},{5,53},{6,54},{7,55},{8,56},{9,... | collective-permute-start | bytes 1572872 | tf_op jit(solution)/shard_map/gather/ppermute | solution.py:25
  57.6 28.4 %collective-permute-start.10 = (bf16[4,256,256]{2,1,0:T(8,128)(2,1)S(1)}, bf16[4,256,256]{2,1,0:T(8,128)(2,1)S(1)}, u32[]{:S(2)}, u32[]{:S(2)}) collective-permute-start(bf16[4,256,256]{2,1,0:T(8,128)(2,1)S(1)} %collective-permute-done.6.a1), channel_id=1, source_target_pairs={{0,16},{1,17},{2,18},{3,19},{4,20},{5,21},{6,22},{7,23},{8,24},{9,... | collective-permute-start | bytes 1572872 | tf_op jit(solution)/shard_map/gather/ppermute | solution.py:25
  67.9 18.1 %collective-permute-start.11 = (bf16[4,256,256]{2,1,0:T(8,128)(2,1)}, bf16[4,256,256]{2,1,0:T(8,128)(2,1)S(1)}, u32[]{:S(2)}, u32[]{:S(2)}) collective-permute-start(bf16[4,256,256]{2,1,0:T(8,128)(2,1)} %collective-permute-done.9.b2), channel_id=1, source_target_pairs={{0,48},{1,49},{2,50},{3,51},{4,52},{5,53},{6,54},{7,55},{8,56},{9,... | collective-permute-start | bytes 1572872 | tf_op jit(solution)/shard_map/gather/ppermute | solution.py:25
  112.5 8.3 %collective-permute-start.20 = (f32[32,256]{1,0:T(8,128)S(1)}, f32[32,256]{1,0:T(8,128)S(1)}, u32[]{:S(2)}, u32[]{:S(2)}) collective-permute-start(f32[32,256]{1,0:T(8,128)S(1)} %get-tuple-element.65), channel_id=1, source_target_pairs={{0,16},{1,17},{2,18},{3,19},{4,20},{5,21},{6,22},{7,23},{8,24},{9,... | collective-permute-start | bytes 98312 | tf_op jit(solution)/shard_map/diag/ppermute | solution.py:25
  112.6 8.2 %collective-permute-start.21 = (f32[32,256]{1,0:T(8,128)S(1)}, f32[32,256]{1,0:T(8,128)S(1)}, u32[]{:S(2)}, u32[]{:S(2)}) collective-permute-start(f32[32,256]{1,0:T(8,128)S(1)} %get-tuple-element.64), channel_id=1, source_target_pairs={{0,32},{1,33},{2,34},{3,35},{4,36},{5,37},{6,38},{7,39},{8,40},{9,... | collective-permute-start | bytes 98312 | tf_op jit(solution)/shard_map/diag/ppermute | solution.py:25
  116.4 24.1 %collective-permute-start.12 = (s16[2,2,272,256]{3,2,1,0:T(8,128)(2,1)}, s16[2,2,272,256]{3,2,1,0:T(8,128)(2,1)S(1)}, u32[]{:S(2)}, u32[]{:S(2)}) collective-permute-start(s16[2,2,272,256]{3,2,1,0:T(8,128)(2,1)} %copy-done.2), channel_id=1, source_target_pairs={{0,1},{1,0},{2,3},{3,2},{4,5},{5,4},{6,7},{7,6},{8,9},{9,8},{10,11... | collective-permute-start | bytes 1671176 | tf_op jit(solution)/shard_map/column/ppermute | solution.py:25
  116.7 26.4 %collective-permute-start.13 = (s16[2,2,272,256]{3,2,1,0:T(8,128)(2,1)}, s16[2,2,272,256]{3,2,1,0:T(8,128)(2,1)S(1)}, u32[]{:S(2)}, u32[]{:S(2)}) collective-permute-start(s16[2,2,272,256]{3,2,1,0:T(8,128)(2,1)} %copy-done.1), channel_id=1, source_target_pairs={{0,2},{1,3},{2,0},{3,1},{4,6},{5,7},{6,4},{7,5},{8,10},{9,11},{10,... | collective-permute-start | bytes 1671176 | tf_op jit(solution)/shard_map/column/ppermute | solution.py:25
  120.8 22.3 %collective-permute-start.14 = (s16[2,2,272,256]{3,2,1,0:T(8,128)(2,1)}, s16[2,2,272,256]{3,2,1,0:T(8,128)(2,1)S(1)}, u32[]{:S(2)}, u32[]{:S(2)}) collective-permute-start(s16[2,2,272,256]{3,2,1,0:T(8,128)(2,1)} %copy-done), channel_id=1, source_target_pairs={{0,3},{1,2},{2,1},{3,0},{4,7},{5,6},{6,5},{7,4},{8,11},{9,10},{10,... | collective-permute-start | bytes 1671176 | tf_op jit(solution)/shard_map/column/ppermute | solution.py:25
  143.8 9.7 %collective-permute-start.27 = (f32[32,256]{1,0:T(8,128)S(1)}, f32[32,256]{1,0:T(8,128)S(1)}, u32[]{:S(2)}, u32[]{:S(2)}) collective-permute-start(f32[32,256]{1,0:T(8,128)S(1)} %add.217), channel_id=1, source_target_pairs={{0,16},{1,17},{2,18},{3,19},{4,20},{5,21},{6,22},{7,23},{8,24},{9,... | collective-permute-start | bytes 98312 | tf_op jit(solution)/shard_map/back/ppermute | solution.py:25
  143.9 9.6 %collective-permute-start.28 = (f32[32,256]{1,0:T(8,128)S(1)}, f32[32,256]{1,0:T(8,128)S(1)}, u32[]{:S(2)}, u32[]{:S(2)}) collective-permute-start(f32[32,256]{1,0:T(8,128)S(1)} %add.217), channel_id=1, source_target_pairs={{0,32},{1,33},{2,34},{3,35},{4,36},{5,37},{6,38},{7,39},{8,40},{9,... | collective-permute-start | bytes 98312 | tf_op jit(solution)/shard_map/back/ppermute | solution.py:25
  144.8 8.7 %collective-permute-start.29 = (f32[32,256]{1,0:T(8,128)S(1)}, f32[32,256]{1,0:T(8,128)S(1)}, u32[]{:S(2)}, u32[]{:S(2)}) collective-permute-start(f32[32,256]{1,0:T(8,128)S(1)} %add.217), channel_id=1, source_target_pairs={{0,48},{1,49},{2,50},{3,51},{4,52},{5,53},{6,54},{7,55},{8,56},{9,... | collective-permute-start | bytes 98312 | tf_op jit(solution)/shard_map/back/ppermute | solution.py:25
  147.8 9.8 %collective-permute-start.15 = (s16[2,272,256]{2,1,0:T(8,128)(2,1)S(1)}, s16[2,272,256]{2,1,0:T(8,128)(2,1)S(1)}, u32[]{:S(2)}, u32[]{:S(2)}) collective-permute-start(s16[2,272,256]{2,1,0:T(8,128)(2,1)S(1)} %get-tuple-element.32), channel_id=1, source_target_pairs={{0,4},{1,5},{2,6},{3,7},{4,0},{5,1},{6,2},{7,3},{8,12},{9,13},{10,... | collective-permute-start | bytes 835592 | tf_op jit(solution)/shard_map/column/ppermute | solution.py:25
  153.6 13.9 %collective-permute-start.30 = (f32[128,256]{1,0:T(8,128)S(1)}, f32[128,256]{1,0:T(8,128)S(1)}, u32[]{:S(2)}, u32[]{:S(2)}) collective-permute-start(f32[128,256]{1,0:T(8,128)S(1)} %bitcast.73), channel_id=1, source_target_pairs={{0,1},{1,0},{2,3},{3,2},{4,5},{5,4},{6,7},{7,6},{8,9},{9,8},{10,11... | collective-permute-start | bytes 393224 | tf_op jit(solution)/shard_map/back/ppermute | solution.py:25
  153.7 13.8 %collective-permute-start.31 = (f32[128,256]{1,0:T(8,128)S(1)}, f32[128,256]{1,0:T(8,128)S(1)}, u32[]{:S(2)}, u32[]{:S(2)}) collective-permute-start(f32[128,256]{1,0:T(8,128)S(1)} %bitcast.74), channel_id=1, source_target_pairs={{0,2},{1,3},{2,0},{3,1},{4,6},{5,7},{6,4},{7,5},{8,10},{9,11},{10,... | collective-permute-start | bytes 393224 | tf_op jit(solution)/shard_map/back/ppermute | solution.py:25
  155.8 11.7 %collective-permute-start.32 = (f32[128,256]{1,0:T(8,128)S(1)}, f32[128,256]{1,0:T(8,128)S(1)}, u32[]{:S(2)}, u32[]{:S(2)}) collective-permute-start(f32[128,256]{1,0:T(8,128)S(1)} %bitcast.75), channel_id=1, source_target_pairs={{0,3},{1,2},{2,1},{3,0},{4,7},{5,6},{6,5},{7,4},{8,11},{9,10},{10,... | collective-permute-start | bytes 393224 | tf_op jit(solution)/shard_map/back/ppermute | solution.py:25
  157.7 11.0 %collective-permute-start.16 = (f32[256,256]{1,0:T(8,128)S(1)}, f32[256,256]{1,0:T(8,128)S(1)}, u32[]{:S(2)}, u32[]{:S(2)}) collective-permute-start(f32[256,256]{1,0:T(8,128)S(1)} %slice_bitcast_fusion), channel_id=1, source_target_pairs={{0,8},{1,9},{2,10},{3,11},{4,12},{5,13},{6,14},{7,15},{8,0},{9,1},... | collective-permute-start | bytes 786440 | tf_op jit(solution)/shard_map/back/ppermute | solution.py:25
  (17 other events, 239.4 us)

commit v4 on v3

--- a/solution.py
+++ b/solution.py
@@ -93,7 +93,7 @@
                     value = jnp.where(live, piece[z], jnp.zeros((256, 256), BF16))
                     wide[at : at + 256, k * 256 : (k + 1) * 256] = value
 
-    def work(blocks):
+    for side, blocks in enumerate((near, far)):
         acc = jnp.zeros((256, 512), F32)
         for pos in range(12):
             acc += jnp.dot(
@@ -101,15 +101,7 @@
                 wide[pos * 256 : (pos + 1) * 256, :],
                 preferred_element_type=F32,
             )
-        acc_ref[0] = acc
-
-    @pl.when(step < 4)
-    def _():
-        work(near)
-
-    @pl.when(step >= 4)
-    def _():
-        work(far)
+        acc_ref[side, 0] = acc
 
 
 def second_kernel(
@@ -126,12 +118,9 @@
                 value = jnp.where(live, piece[z], jnp.zeros((256, 256), BF16))
                 wide[z * 256 : (z + 1) * 256, k * 256 : (k + 1) * 256] = value
 
-    half = lax.rem(step, 4) // 2
-    zrel = half ^ scal[33]
-    side = step // 4
-
-    def work(blocks, left):
-        acc = acc_in[0]
+    zrel = (step // 2) ^ scal[33]
+    for side, (blocks, left) in enumerate(((near, left_near), (far, left_far))):
+        acc = acc_in[side, 0]
         for z in range(4):
             acc += jnp.dot(
                 blocks[0, scal[12 + z] & 7],
@@ -139,44 +128,26 @@
                 preferred_element_type=F32,
             )
         for k in range(2):
-            live = (-scal[16 + 2 * step + k]).astype(F32)
+            live = (-scal[16 + 8 * side + 2 * step + k]).astype(F32)
             term = acc[:, k * 256 : (k + 1) * 256] * live
             high = term.astype(BF16)
             rest = (term - high.astype(F32)).astype(BF16)
             both = jnp.concatenate([high, rest], axis=1)
             both = jnp.dot(left[k, 0], both, preferred_element_type=F32)
             diag_ref[k] += both[:, :256] + both[:, 256:]
+            code, mark = encode(term)
             to = (2 * lax.rem(step, 2) + k) ^ scal[32]
 
             @pl.when(to == 0)
             def _():
                 own[zrel, side] = term
 
-            @pl.when(to != 0)
-            def _():
-                code, mark = encode(term)
-                for m, ref in ((1, q1), (2, q2), (3, q3)):
-
-                    @pl.when(to == m)
-                    def _():
-                        ref[zrel, side, 0:256] = code
-                        ref[zrel, side, 256:272] = mark
-
-    @pl.when(step < 4)
-    def _():
-        work(near, left_near)
-
-    @pl.when(step >= 4)
-    def _():
-        work(far, left_far)
-
-
-def early(i):
-    return jnp.minimum(i, 3)
-
-
-def late(i):
-    return jnp.maximum(i - 4, 0)
+            for m, ref in ((1, q1), (2, q2), (3, q3)):
+
+                @pl.when(to == m)
+                def _():
+                    ref[zrel, side, 0:256] = code
+                    ref[zrel, side, 256:272] = mark
 
 
 def full(shape):
@@ -191,16 +162,16 @@
         first_kernel,
         grid_spec=pltpu.PrefetchScalarGridSpec(
             num_scalar_prefetch=1,
-            grid=(8,),
+            grid=(4,),
             in_specs=[
-                pl.BlockSpec((1, 16, 256, 256), lambda i, s: (early(i), 0, 0, 0)),
-                pl.BlockSpec((1, 16, 256, 256), lambda i, s: (late(i), 0, 0, 0)),
+                pl.BlockSpec((1, 16, 256, 256), lambda i, s: (i, 0, 0, 0)),
+                pl.BlockSpec((1, 16, 256, 256), lambda i, s: (i, 0, 0, 0)),
             ]
             + [full(p.shape) for p in pieces],
-            out_specs=pl.BlockSpec((1, 256, 512), lambda i, s: (i, 0, 0)),
+            out_specs=pl.BlockSpec((2, 1, 256, 512), lambda i, s: (0, i, 0, 0)),
             scratch_shapes=[pltpu.VMEM((3072, 512), BF16)],
         ),
-        out_shape=jax.ShapeDtypeStruct((8, 256, 512), F32),
+        out_shape=jax.ShapeDtypeStruct((2, 4, 256, 512), F32),
         cost_estimate=pl.CostEstimate(
             flops=2 * 2048 * 3072 * 512, transcendentals=0, bytes_accessed=24 * 2**20
         ),
@@ -213,16 +184,16 @@
         second_kernel,
         grid_spec=pltpu.PrefetchScalarGridSpec(
             num_scalar_prefetch=1,
-            grid=(8,),
+            grid=(4,),
             in_specs=[
-                pl.BlockSpec((1, 256, 512), lambda i, s: (i, 0, 0)),
-                pl.BlockSpec((1, 8, 256, 256), lambda i, s: (early(i), s[12] // 8, 0, 0)),
-                pl.BlockSpec((1, 8, 256, 256), lambda i, s: (late(i), s[12] // 8, 0, 0)),
+                pl.BlockSpec((2, 1, 256, 512), lambda i, s: (0, i, 0, 0)),
+                pl.BlockSpec((1, 8, 256, 256), lambda i, s: (i, s[12] // 8, 0, 0)),
+                pl.BlockSpec((1, 8, 256, 256), lambda i, s: (i, s[12] // 8, 0, 0)),
             ]
             + [full(p.shape) for p in pieces]
             + [
-                pl.BlockSpec((2, 1, 256, 256), lambda i, s: (0, early(i), 0, 0)),
-                pl.BlockSpec((2, 1, 256, 256), lambda i, s: (0, late(i), 0, 0)),
+                pl.BlockSpec((2, 1, 256, 256), lambda i, s: (0, i, 0, 0)),
+                pl.BlockSpec((2, 1, 256, 256), lambda i, s: (0, i, 0, 0)),
             ],
             out_specs=[
                 full((2, 2, 256, 256)),
@@ -276,15 +247,15 @@
         product_kernel,
         grid_spec=pltpu.PrefetchScalarGridSpec(
             num_scalar_prefetch=1,
-            grid=(8,),
+            grid=(4,),
             in_specs=[
-                pl.BlockSpec((1, 16, 256, 256), lambda i, s: (early(i), 0, 0, 0)),
-                pl.BlockSpec((1, 16, 256, 256), lambda i, s: (late(i), 0, 0, 0)),
+                pl.BlockSpec((1, 16, 256, 256), lambda i, s: (i, 0, 0, 0)),
+                pl.BlockSpec((1, 16, 256, 256), lambda i, s: (i, 0, 0, 0)),
             ]
             + [full(p.shape) for p in pieces]
             + [
-                pl.BlockSpec((2, 1, 256, 256), lambda i, s: (0, early(i), 0, 0)),
-                pl.BlockSpec((2, 1, 256, 256), lambda i, s: (0, late(i), 0, 0)),
+                pl.BlockSpec((2, 1, 256, 256), lambda i, s: (0, i, 0, 0)),
+                pl.BlockSpec((2, 1, 256, 256), lambda i, s: (0, i, 0, 0)),
             ],
             out_specs=[
                 full((2, 2, 256, 256)),
@@ -368,9 +339,11 @@
         piece = shares(piece.reshape(4, 32, 256), x, to_x)
         one, two, three = [to_zl(piece, k) for k in (1, 2, 3)]
         piece = (piece + one) + (two + three)
+    with jax.named_scope("column"):
+        got = [to_y(out[m], m) for m in (1, 2, 3)]
+        piece, got[0] = tie(piece, got[0])
         piece = piece + to_zh(piece)
-    with jax.named_scope("column"):
-        keep, give = totals(out[0], [to_y(out[m], m) for m in (1, 2, 3)])
+        keep, give = totals(out[0], got)
         got = to_zh(give)
         block = keep + decode(got[:, :256], got[:, 256:257])
     with jax.named_scope("back"):

time: 177 us -> 172 us (0.972)
  Pallas kernels: 28 us -> 23.3 us
  starting transfers between devices: 85.1 us -> 82.6 us
  waiting for transfers between devices: 44.8 us -> 47.3 us
    pallas_call x1, Pallas kernels: 12.6 us -> 10.1 us  [second_products(): pl.pallas_call(second_kernel, grid_spec=pltpu.PrefetchScalarGridSpec(num_...]
    ppermute x34, starting transfers between devices: 85.1 us -> 82.6 us  [send(): return lax.ppermute(value, AXES, pairs)]
    ppermute x34, waiting for transfers between devices: 44.8 us -> 47.3 us  [send(): return lax.ppermute(value, AXES, pairs)]
    pallas_call x1, Pallas kernels: 14.6 us -> 12.4 us  [first_products(): pl.pallas_call(first_kernel, grid_spec=pltpu.PrefetchScalarGridSpec(num_s...]
where the time goes in v4:
time: 172 us; the launch traced here: 169 us
  starting transfers between devices  82.6 us (48%)
  waiting for transfers between devices  47.3 us (28%)
  Pallas kernels  23.3 us (14%)
  local copies, waits for them, and re-layouts  9.38 us (5%)
  other arithmetic  5.27 us (3%)
    ppermute x34, starting transfers between devices, send(): return lax.ppermute(value, AXES, pairs)  82.6 us
    ppermute x34, waiting for transfers between devices, send(): return lax.ppermute(value, AXES, pairs)  47.3 us
    pallas_call x1, Pallas kernels, first_products(): pl.pallas_call(first_kernel, grid_spec=pltpu.PrefetchScalarGridSpec(num_s...  12.4 us
    pallas_call x1, Pallas kernels, second_products(): pl.pallas_call(second_kernel, grid_spec=pltpu.PrefetchScalarGridSpec(num_...  10.1 us
  transfers between devices with their start and end apart: 34, of which 11 were waited for; matrix products, arithmetic and copies ran while one was open for 6% of the time, Pallas kernels for 8%

profile of v4, /device:TPU:1, one launch (start us, length us, event | category | flops | bytes accessed | tf_op | source)
XLA Modules:
  0.0 168.8 jit_solution(7425086591895729861)
XLA Ops:
  0.7 3.3 %collective-permute-start.4 = (bf16[4,16,256,256]{3,2,1,0:T(8,128)(2,1)}, bf16[4,16,256,256]{3,2,1,0:T(8,128)(2,1)}, u32[]{:S(2)}, u32[]{:S(2)}) collective-permute-start(bf16[4,16,256,256]{3,2,1,0:T(8,128)(2,1)} %near.3), channel_id=1, source_target_pairs={{0,8},{1,9},{2,10},{3,11},{4,12},{5,13},{6,14},{7,15},{8,0},{9,1},... | collective-permute-start | bytes 25165832 | tf_op jit(solution)/shard_map/swap/ppermute | solution.py:25
  7.7 5.0 %collective-permute-done = bf16[2,256,256]{2,1,0:T(8,128)(2,1)S(1)} collective-permute-done((bf16[2,256,256]{2,1,0:T(8,128)(2,1)S(1)}, bf16[2,256,256]{2,1,0:T(8,128)(2,1)S(1)}, u32[]{:S(2)}, u32[]{:S(2)}) %collective-permute-start) | collective-permute-done | bytes 262176 | tf_op jit(solution)/shard_map/spread/ppermute | solution.py:25
  12.7 5.1 %collective-permute-start.1 = (bf16[2,256,256]{2,1,0:T(8,128)(2,1)S(1)}, bf16[2,256,256]{2,1,0:T(8,128)(2,1)}, u32[]{:S(2)}, u32[]{:S(2)}) collective-permute-start(bf16[2,256,256]{2,1,0:T(8,128)(2,1)S(1)} %collective-permute-done), channel_id=1, source_target_pairs={{0,64},{1,65},{2,66},{3,67},{4,68},{5,69},{6,70},{7,71},{8,72},{9,... | collective-permute-start | bytes 786440 | tf_op jit(solution)/shard_map/gather/ppermute | solution.py:25
  17.8 5.5 %collective-permute-start.2 = (bf16[2,256,256]{2,1,0:T(8,128)(2,1)S(1)}, bf16[2,256,256]{2,1,0:T(8,128)(2,1)}, u32[]{:S(2)}, u32[]{:S(2)}) collective-permute-start(bf16[2,256,256]{2,1,0:T(8,128)(2,1)S(1)} %collective-permute-done), channel_id=1, source_target_pairs={{0,128},{1,129},{2,130},{3,131},{4,132},{5,133},{6,134},{7,135},{8... | collective-permute-start | bytes 786440 | tf_op jit(solution)/shard_map/gather/ppermute | solution.py:25
  30.0 12.1 %collective-permute-done.3 = bf16[2,256,256]{2,1,0:T(8,128)(2,1)} collective-permute-done((bf16[2,256,256]{2,1,0:T(8,128)(2,1)S(1)}, bf16[2,256,256]{2,1,0:T(8,128)(2,1)}, u32[]{:S(2)}, u32[]{:S(2)}) %collective-permute-start.3) | collective-permute-done | bytes 262176 | tf_op jit(solution)/shard_map/gather/ppermute | solution.py:25
  44.5 3.6 %collective-permute-start.8 = (bf16[4,256,256]{2,1,0:T(8,128)(2,1)S(1)}, bf16[4,256,256]{2,1,0:T(8,128)(2,1)S(1)}, u32[]{:S(2)}, u32[]{:S(2)}) collective-permute-start(bf16[4,256,256]{2,1,0:T(8,128)(2,1)S(1)} %get-tuple-element.26.a0), channel_id=1, source_target_pairs={{0,48},{1,49},{2,50},{3,51},{4,52},{5,53},{6,54},{7,55},{8,56},{9,... | collective-permute-start | bytes 1572872 | tf_op jit(solution)/shard_map/gather/ppermute | solution.py:25
  48.1 2.7 %collective-permute-start.9 = (bf16[4,256,256]{2,1,0:T(8,128)(2,1)S(1)}, bf16[4,256,256]{2,1,0:T(8,128)(2,1)}, u32[]{:S(2)}, u32[]{:S(2)}) collective-permute-start(bf16[4,256,256]{2,1,0:T(8,128)(2,1)S(1)} %get-tuple-element.27.b0), channel_id=1, source_target_pairs={{0,48},{1,49},{2,50},{3,51},{4,52},{5,53},{6,54},{7,55},{8,56},{9,... | collective-permute-start | bytes 1572872 | tf_op jit(solution)/shard_map/gather/ppermute | solution.py:25
  51.8 5.8 %collective-permute-done.6.a1 = bf16[4,256,256]{2,1,0:T(8,128)(2,1)S(1)} collective-permute-done((bf16[4,256,256]{2,1,0:T(8,128)(2,1)S(1)}, bf16[4,256,256]{2,1,0:T(8,128)(2,1)S(1)}, u32[]{:S(2)}, u32[]{:S(2)}) %collective-permute-start.6) | collective-permute-done | bytes 524320 | tf_op jit(solution)/shard_map/gather/ppermute | solution.py:25
  57.6 10.3 %collective-permute-done.9.b2 = bf16[4,256,256]{2,1,0:T(8,128)(2,1)} collective-permute-done((bf16[4,256,256]{2,1,0:T(8,128)(2,1)S(1)}, bf16[4,256,256]{2,1,0:T(8,128)(2,1)}, u32[]{:S(2)}, u32[]{:S(2)}) %collective-permute-start.9) | collective-permute-done | bytes 524320 | tf_op jit(solution)/shard_map/gather/ppermute | solution.py:25
  67.9 3.5 %collective-permute-start.11 = (bf16[4,256,256]{2,1,0:T(8,128)(2,1)}, bf16[4,256,256]{2,1,0:T(8,128)(2,1)S(1)}, u32[]{:S(2)}, u32[]{:S(2)}) collective-permute-start(bf16[4,256,256]{2,1,0:T(8,128)(2,1)} %collective-permute-done.9.b2), channel_id=1, source_target_pairs={{0,48},{1,49},{2,50},{3,51},{4,52},{5,53},{6,54},{7,55},{8,56},{9,... | collective-permute-start | bytes 1572872 | tf_op jit(solution)/shard_map/gather/ppermute | solution.py:25
  71.4 12.4 %product.2.acc_in = f32[2,4,256,512]{3,2,1,0:T(8,128)} custom-call(s32[66]{0:T(128)S(1)} %concatenate.3.scal, bf16[4,16,256,256]{3,2,1,0:T(8,128)(2,1)} %near.3, bf16[4,16,256,256]{3,2,1,0:T(8,128)(2,1)} %collective-permute-done.4.far, bf16[4,256,256]{2,1,0:T(8,128)(2,1)S(1)} %get-tuple-element.26.a0, bf16[4,256,256]{2,1,0:T(8,128)(2,1)S(1)} %get-tuple-element.27.b0, ...), custom_call_target="tpu_custom_call" | custom-call | flops 6442450944 | bytes 25165824 | tf_op jit(solution)/shard_map/product/pallas_call | solution.py:161
  83.8 10.1 %product.3 = (f32[2,2,256,256]{3,2,1,0:T(8,128)S(1)}, s16[2,2,272,256]{3,2,1,0:T(8,128)(2,1)S(1)}, s16[2,2,272,256]{3,2,1,0:T(8,128)(2,1)S(1)}, s16[2,2,272,256]{3,2,1,0:T(8,128)(2,1)S(1)}, f32[2,256,256]{2,1,0:T(8,128)S(1)}) custom-call(s32[66]{0:T(128)S(1)} %concatenate.3.scal, f32[2,4,256,512]{3,2,1,0:T(8,128)} %product.2.acc_in, ...), custom_call_target="tpu_custom_call" | custom-call | flops 2147483648 | bytes 16777216 | tf_op jit(solution)/shard_map/product/pallas_call | solution.py:183
  96.4 4.6 %collective-permute-start.12 = (f32[128,256]{1,0:T(8,128)S(1)}, f32[128,256]{1,0:T(8,128)S(1)}, u32[]{:S(2)}, u32[]{:S(2)}) collective-permute-start(f32[128,256]{1,0:T(8,128)S(1)} %get-tuple-element.54), channel_id=1, source_target_pairs={{0,1},{1,0},{2,3},{3,2},{4,5},{5,4},{6,7},{7,6},{8,9},{9,8},{10,11... | collective-permute-start | bytes 393224 | tf_op jit(solution)/shard_map/diag/ppermute | solution.py:25
  101.0 2.7 %collective-permute-start.14 = (f32[128,256]{1,0:T(8,128)S(1)}, f32[128,256]{1,0:T(8,128)S(1)}, u32[]{:S(2)}, u32[]{:S(2)}) collective-permute-start(f32[128,256]{1,0:T(8,128)S(1)} %get-tuple-element.52), channel_id=1, source_target_pairs={{0,3},{1,2},{2,1},{3,0},{4,7},{5,6},{6,5},{7,4},{8,11},{9,10},{10,... | collective-permute-start | bytes 393224 | tf_op jit(solution)/shard_map/diag/ppermute | solution.py:25
  103.7 2.8 %collective-permute-done.13 = f32[128,256]{1,0:T(8,128)S(1)} collective-permute-done((f32[128,256]{1,0:T(8,128)S(1)}, f32[128,256]{1,0:T(8,128)S(1)}, u32[]{:S(2)}, u32[]{:S(2)}) %collective-permute-start.13) | collective-permute-done | bytes 131104 | tf_op jit(solution)/shard_map/diag/ppermute | solution.py:25
  111.8 4.2 %collective-permute-start.22 = (s16[2,2,272,256]{3,2,1,0:T(8,128)(2,1)}, s16[2,2,272,256]{3,2,1,0:T(8,128)(2,1)S(1)}, u32[]{:S(2)}, u32[]{:S(2)}) collective-permute-start(s16[2,2,272,256]{3,2,1,0:T(8,128)(2,1)} %copy-done.1), channel_id=1, source_target_pairs={{0,2},{1,3},{2,0},{3,1},{4,6},{5,7},{6,4},{7,5},{8,10},{9,11},{10,... | collective-permute-start | bytes 1671176 | tf_op jit(solution)/shard_map/column/ppermute | solution.py:25
  116.1 4.9 %collective-permute-start.18 = (f32[32,256]{1,0:T(8,128)S(1)}, f32[32,256]{1,0:T(8,128)S(1)}, u32[]{:S(2)}, u32[]{:S(2)}) collective-permute-start(f32[32,256]{1,0:T(8,128)S(1)} %fusion.2), channel_id=1, source_target_pairs={{0,64},{1,65},{2,66},{3,67},{4,68},{5,69},{6,70},{7,71},{8,72},{9,... | collective-permute-start | bytes 98312 | tf_op jit(solution)/shard_map/diag/ppermute | solution.py:25
  123.1 2.7 %collective-permute-start.20 = (f32[32,256]{1,0:T(8,128)S(1)}, f32[32,256]{1,0:T(8,128)S(1)}, u32[]{:S(2)}, u32[]{:S(2)}) collective-permute-start(f32[32,256]{1,0:T(8,128)S(1)} %fusion.2), channel_id=1, source_target_pairs={{0,192},{1,193},{2,194},{3,195},{4,196},{5,197},{6,198},{7,199},{8... | collective-permute-start | bytes 98312 | tf_op jit(solution)/shard_map/diag/ppermute | solution.py:25
  128.0 6.4 %collective-permute-start.26 = (f32[32,256]{1,0:T(8,128)S(1)}, f32[32,256]{1,0:T(8,128)S(1)}, u32[]{:S(2)}, u32[]{:S(2)}) collective-permute-start(f32[32,256]{1,0:T(8,128)S(1)} %add_add_fusion), channel_id=1, source_target_pairs={{0,4},{1,5},{2,6},{3,7},{4,0},{5,1},{6,2},{7,3},{8,12},{9,13},{10,... | collective-permute-start | bytes 98312 | tf_op jit(solution)/shard_map/column/ppermute | solution.py:25
  135.5 5.0 %collective-permute-done.23.q3 = s16[2,2,272,256]{3,2,1,0:T(8,128)(2,1)S(1)} collective-permute-done((s16[2,2,272,256]{3,2,1,0:T(8,128)(2,1)}, s16[2,2,272,256]{3,2,1,0:T(8,128)(2,1)S(1)}, u32[]{:S(2)}, u32[]{:S(2)}) %collective-permute-start.23) | collective-permute-done | bytes 557088 | tf_op jit(solution)/shard_map/column/ppermute | solution.py:25
  142.8 2.5 %collective-permute-start.29 = (f32[32,256]{1,0:T(8,128)S(1)}, f32[32,256]{1,0:T(8,128)S(1)}, u32[]{:S(2)}, u32[]{:S(2)}) collective-permute-start(f32[32,256]{1,0:T(8,128)S(1)} %add.217), channel_id=1, source_target_pairs={{0,48},{1,49},{2,50},{3,51},{4,52},{5,53},{6,54},{7,55},{8,56},{9,... | collective-permute-start | bytes 98312 | tf_op jit(solution)/shard_map/back/ppermute | solution.py:25
  145.3 5.5 %collective-permute-start.24 = (s16[2,272,256]{2,1,0:T(8,128)(2,1)S(1)}, s16[2,272,256]{2,1,0:T(8,128)(2,1)S(1)}, u32[]{:S(2)}, u32[]{:S(2)}) collective-permute-start(s16[2,272,256]{2,1,0:T(8,128)(2,1)S(1)} %get-tuple-element.36), channel_id=1, source_target_pairs={{0,4},{1,5},{2,6},{3,7},{4,0},{5,1},{6,2},{7,3},{8,12},{9,13},{10,... | collective-permute-start | bytes 835592 | tf_op jit(solution)/shard_map/column/ppermute | solution.py:25
  155.0 5.9 %collective-permute-start.25 = (f32[256,256]{1,0:T(8,128)S(1)}, f32[256,256]{1,0:T(8,128)S(1)}, u32[]{:S(2)}, u32[]{:S(2)}) collective-permute-start(f32[256,256]{1,0:T(8,128)S(1)} %slice_bitcast_fusion), channel_id=1, source_target_pairs={{0,8},{1,9},{2,10},{3,11},{4,12},{5,13},{6,14},{7,15},{8,0},{9,1},... | collective-permute-start | bytes 786440 | tf_op jit(solution)/shard_map/back/ppermute | solution.py:25
  162.0 3.2 %collective-permute-start.33 = (f32[2,256,256]{2,1,0:T(8,128)S(1)}, f32[2,256,256]{2,1,0:T(8,128)S(1)}, u32[]{:S(2)}, u32[]{:S(2)}) collective-permute-start(f32[2,256,256]{2,1,0:T(8,128)S(1)} %bitcast.69), channel_id=1, source_target_pairs={{0,8},{1,9},{2,10},{3,11},{4,12},{5,13},{6,14},{7,15},{8,0},{9,1},... | collective-permute-start | bytes 1572872 | tf_op jit(solution)/shard_map/back/ppermute | solution.py:25
  (103 shorter events, 38.0 us)
Async XLA Ops:
  0.7 42.6 %collective-permute-start.4 = (bf16[4,16,256,256]{3,2,1,0:T(8,128)(2,1)}, bf16[4,16,256,256]{3,2,1,0:T(8,128)(2,1)}, u32[]{:S(2)}, u32[]{:S(2)}) collective-permute-start(bf16[4,16,256,256]{3,2,1,0:T(8,128)(2,1)} %near.3), channel_id=1, source_target_pairs={{0,8},{1,9},{2,10},{3,11},{4,12},{5,13},{6,14},{7,15},{8,0},{9,1},... | collective-permute-start | bytes 25165832 | tf_op jit(solution)/shard_map/swap/ppermute | solution.py:25
  5.0 7.7 %collective-permute-start = (bf16[2,256,256]{2,1,0:T(8,128)(2,1)S(1)}, bf16[2,256,256]{2,1,0:T(8,128)(2,1)S(1)}, u32[]{:S(2)}, u32[]{:S(2)}) collective-permute-start(bf16[2,256,256]{2,1,0:T(8,128)(2,1)S(1)} %fusion), channel_id=1, source_target_pairs={{0,0},{1,8},{2,48},{3,56},{4,128},{5,136},{6,176},{7,184},{8,72},{... | collective-permute-start | bytes 786440 | tf_op jit(solution)/shard_map/spread/ppermute | solution.py:25
  12.7 15.3 %collective-permute-start.1 = (bf16[2,256,256]{2,1,0:T(8,128)(2,1)S(1)}, bf16[2,256,256]{2,1,0:T(8,128)(2,1)}, u32[]{:S(2)}, u32[]{:S(2)}) collective-permute-start(bf16[2,256,256]{2,1,0:T(8,128)(2,1)S(1)} %collective-permute-done), channel_id=1, source_target_pairs={{0,64},{1,65},{2,66},{3,67},{4,68},{5,69},{6,70},{7,71},{8,72},{9,... | collective-permute-start | bytes 786440 | tf_op jit(solution)/shard_map/gather/ppermute | solution.py:25
  17.8 11.2 %collective-permute-start.2 = (bf16[2,256,256]{2,1,0:T(8,128)(2,1)S(1)}, bf16[2,256,256]{2,1,0:T(8,128)(2,1)}, u32[]{:S(2)}, u32[]{:S(2)}) collective-permute-start(bf16[2,256,256]{2,1,0:T(8,128)(2,1)S(1)} %collective-permute-done), channel_id=1, source_target_pairs={{0,128},{1,129},{2,130},{3,131},{4,132},{5,133},{6,134},{7,135},{8... | collective-permute-start | bytes 786440 | tf_op jit(solution)/shard_map/gather/ppermute | solution.py:25
  23.3 18.8 %collective-permute-start.3 = (bf16[2,256,256]{2,1,0:T(8,128)(2,1)S(1)}, bf16[2,256,256]{2,1,0:T(8,128)(2,1)}, u32[]{:S(2)}, u32[]{:S(2)}) collective-permute-start(bf16[2,256,256]{2,1,0:T(8,128)(2,1)S(1)} %collective-permute-done), channel_id=1, source_target_pairs={{0,192},{1,193},{2,194},{3,195},{4,196},{5,197},{6,198},{7,199},{8... | collective-permute-start | bytes 786440 | tf_op jit(solution)/shard_map/gather/ppermute | solution.py:25
  27.1 16.1 %collective-permute-start.5 = (bf16[2,4,256,256]{3,2,1,0:T(8,128)(2,1)S(1)}, bf16[2,4,256,256]{3,2,1,0:T(8,128)(2,1)S(1)}, u32[]{:S(2)}, u32[]{:S(2)}) collective-permute-start(bf16[2,4,256,256]{3,2,1,0:T(8,128)(2,1)S(1)} %get-tuple-element.43), channel_id=1, source_target_pairs={{0,8},{1,9},{2,10},{3,11},{4,12},{5,13},{6,14},{7,15},{8,0},{9,1},... | collective-permute-start | bytes 3145736 | tf_op jit(solution)/shard_map/swap/ppermute | solution.py:25
  43.2 14.3 %collective-permute-start.6 = (bf16[4,256,256]{2,1,0:T(8,128)(2,1)S(1)}, bf16[4,256,256]{2,1,0:T(8,128)(2,1)S(1)}, u32[]{:S(2)}, u32[]{:S(2)}) collective-permute-start(bf16[4,256,256]{2,1,0:T(8,128)(2,1)S(1)} %get-tuple-element.26.a0), channel_id=1, source_target_pairs={{0,16},{1,17},{2,18},{3,19},{4,20},{5,21},{6,22},{7,23},{8,24},{9,... | collective-permute-start | bytes 1572872 | tf_op jit(solution)/shard_map/gather/ppermute | solution.py:25
  44.5 26.9 %collective-permute-start.8 = (bf16[4,256,256]{2,1,0:T(8,128)(2,1)S(1)}, bf16[4,256,256]{2,1,0:T(8,128)(2,1)S(1)}, u32[]{:S(2)}, u32[]{:S(2)}) collective-permute-start(bf16[4,256,256]{2,1,0:T(8,128)(2,1)S(1)} %get-tuple-element.26.a0), channel_id=1, source_target_pairs={{0,48},{1,49},{2,50},{3,51},{4,52},{5,53},{6,54},{7,55},{8,56},{9,... | collective-permute-start | bytes 1572872 | tf_op jit(solution)/shard_map/gather/ppermute | solution.py:25
  48.1 23.2 %collective-permute-start.7 = (bf16[4,256,256]{2,1,0:T(8,128)(2,1)S(1)}, bf16[4,256,256]{2,1,0:T(8,128)(2,1)}, u32[]{:S(2)}, u32[]{:S(2)}) collective-permute-start(bf16[4,256,256]{2,1,0:T(8,128)(2,1)S(1)} %get-tuple-element.27.b0), channel_id=1, source_target_pairs={{0,16},{1,17},{2,18},{3,19},{4,20},{5,21},{6,22},{7,23},{8,24},{9,... | collective-permute-start | bytes 1572872 | tf_op jit(solution)/shard_map/gather/ppermute | solution.py:25
  48.1 19.7 %collective-permute-start.9 = (bf16[4,256,256]{2,1,0:T(8,128)(2,1)S(1)}, bf16[4,256,256]{2,1,0:T(8,128)(2,1)}, u32[]{:S(2)}, u32[]{:S(2)}) collective-permute-start(bf16[4,256,256]{2,1,0:T(8,128)(2,1)S(1)} %get-tuple-element.27.b0), channel_id=1, source_target_pairs={{0,48},{1,49},{2,50},{3,51},{4,52},{5,53},{6,54},{7,55},{8,56},{9,... | collective-permute-start | bytes 1572872 | tf_op jit(solution)/shard_map/gather/ppermute | solution.py:25
  57.6 26.3 %collective-permute-start.10 = (bf16[4,256,256]{2,1,0:T(8,128)(2,1)S(1)}, bf16[4,256,256]{2,1,0:T(8,128)(2,1)S(1)}, u32[]{:S(2)}, u32[]{:S(2)}) collective-permute-start(bf16[4,256,256]{2,1,0:T(8,128)(2,1)S(1)} %collective-permute-done.6.a1), channel_id=1, source_target_pairs={{0,16},{1,17},{2,18},{3,19},{4,20},{5,21},{6,22},{7,23},{8,24},{9,... | collective-permute-start | bytes 1572872 | tf_op jit(solution)/shard_map/gather/ppermute | solution.py:25
  67.9 16.0 %collective-permute-start.11 = (bf16[4,256,256]{2,1,0:T(8,128)(2,1)}, bf16[4,256,256]{2,1,0:T(8,128)(2,1)S(1)}, u32[]{:S(2)}, u32[]{:S(2)}) collective-permute-start(bf16[4,256,256]{2,1,0:T(8,128)(2,1)} %collective-permute-done.9.b2), channel_id=1, source_target_pairs={{0,48},{1,49},{2,50},{3,51},{4,52},{5,53},{6,54},{7,55},{8,56},{9,... | collective-permute-start | bytes 1572872 | tf_op jit(solution)/shard_map/gather/ppermute | solution.py:25
  107.8 8.2 %collective-permute-start.15 = (f32[32,256]{1,0:T(8,128)S(1)}, f32[32,256]{1,0:T(8,128)S(1)}, u32[]{:S(2)}, u32[]{:S(2)}) collective-permute-start(f32[32,256]{1,0:T(8,128)S(1)} %get-tuple-element.69), channel_id=1, source_target_pairs={{0,16},{1,17},{2,18},{3,19},{4,20},{5,21},{6,22},{7,23},{8,24},{9,... | collective-permute-start | bytes 98312 | tf_op jit(solution)/shard_map/diag/ppermute | solution.py:25
  107.9 20.1 %collective-permute-start.21 = (s16[2,2,272,256]{3,2,1,0:T(8,128)(2,1)}, s16[2,2,272,256]{3,2,1,0:T(8,128)(2,1)S(1)}, u32[]{:S(2)}, u32[]{:S(2)}) collective-permute-start(s16[2,2,272,256]{3,2,1,0:T(8,128)(2,1)} %copy-done.2), channel_id=1, source_target_pairs={{0,1},{1,0},{2,3},{3,2},{4,5},{5,4},{6,7},{7,6},{8,9},{9,8},{10,11... | collective-permute-start | bytes 1671176 | tf_op jit(solution)/shard_map/column/ppermute | solution.py:25
  108.0 8.0 %collective-permute-start.16 = (f32[32,256]{1,0:T(8,128)S(1)}, f32[32,256]{1,0:T(8,128)S(1)}, u32[]{:S(2)}, u32[]{:S(2)}) collective-permute-start(f32[32,256]{1,0:T(8,128)S(1)} %get-tuple-element.68), channel_id=1, source_target_pairs={{0,32},{1,33},{2,34},{3,35},{4,36},{5,37},{6,38},{7,39},{8,40},{9,... | collective-permute-start | bytes 98312 | tf_op jit(solution)/shard_map/diag/ppermute | solution.py:25
  111.8 23.7 %collective-permute-start.22 = (s16[2,2,272,256]{3,2,1,0:T(8,128)(2,1)}, s16[2,2,272,256]{3,2,1,0:T(8,128)(2,1)S(1)}, u32[]{:S(2)}, u32[]{:S(2)}) collective-permute-start(s16[2,2,272,256]{3,2,1,0:T(8,128)(2,1)} %copy-done.1), channel_id=1, source_target_pairs={{0,2},{1,3},{2,0},{3,1},{4,6},{5,7},{6,4},{7,5},{8,10},{9,11},{10,... | collective-permute-start | bytes 1671176 | tf_op jit(solution)/shard_map/column/ppermute | solution.py:25
  116.0 24.5 %collective-permute-start.23 = (s16[2,2,272,256]{3,2,1,0:T(8,128)(2,1)}, s16[2,2,272,256]{3,2,1,0:T(8,128)(2,1)S(1)}, u32[]{:S(2)}, u32[]{:S(2)}) collective-permute-start(s16[2,2,272,256]{3,2,1,0:T(8,128)(2,1)} %copy-done), channel_id=1, source_target_pairs={{0,3},{1,2},{2,1},{3,0},{4,7},{5,6},{6,5},{7,4},{8,11},{9,10},{10,... | collective-permute-start | bytes 1671176 | tf_op jit(solution)/shard_map/column/ppermute | solution.py:25
  128.0 13.3 %collective-permute-start.26 = (f32[32,256]{1,0:T(8,128)S(1)}, f32[32,256]{1,0:T(8,128)S(1)}, u32[]{:S(2)}, u32[]{:S(2)}) collective-permute-start(f32[32,256]{1,0:T(8,128)S(1)} %add_add_fusion), channel_id=1, source_target_pairs={{0,4},{1,5},{2,6},{3,7},{4,0},{5,1},{6,2},{7,3},{8,12},{9,13},{10,... | collective-permute-start | bytes 98312 | tf_op jit(solution)/shard_map/column/ppermute | solution.py:25
  141.3 9.4 %collective-permute-start.27 = (f32[32,256]{1,0:T(8,128)S(1)}, f32[32,256]{1,0:T(8,128)S(1)}, u32[]{:S(2)}, u32[]{:S(2)}) collective-permute-start(f32[32,256]{1,0:T(8,128)S(1)} %add.217), channel_id=1, source_target_pairs={{0,16},{1,17},{2,18},{3,19},{4,20},{5,21},{6,22},{7,23},{8,24},{9,... | collective-permute-start | bytes 98312 | tf_op jit(solution)/shard_map/back/ppermute | solution.py:25
  141.4 9.4 %collective-permute-start.28 = (f32[32,256]{1,0:T(8,128)S(1)}, f32[32,256]{1,0:T(8,128)S(1)}, u32[]{:S(2)}, u32[]{:S(2)}) collective-permute-start(f32[32,256]{1,0:T(8,128)S(1)} %add.217), channel_id=1, source_target_pairs={{0,32},{1,33},{2,34},{3,35},{4,36},{5,37},{6,38},{7,39},{8,40},{9,... | collective-permute-start | bytes 98312 | tf_op jit(solution)/shard_map/back/ppermute | solution.py:25
  142.8 8.0 %collective-permute-start.29 = (f32[32,256]{1,0:T(8,128)S(1)}, f32[32,256]{1,0:T(8,128)S(1)}, u32[]{:S(2)}, u32[]{:S(2)}) collective-permute-start(f32[32,256]{1,0:T(8,128)S(1)} %add.217), channel_id=1, source_target_pairs={{0,48},{1,49},{2,50},{3,51},{4,52},{5,53},{6,54},{7,55},{8,56},{9,... | collective-permute-start | bytes 98312 | tf_op jit(solution)/shard_map/back/ppermute | solution.py:25
  145.3 9.5 %collective-permute-start.24 = (s16[2,272,256]{2,1,0:T(8,128)(2,1)S(1)}, s16[2,272,256]{2,1,0:T(8,128)(2,1)S(1)}, u32[]{:S(2)}, u32[]{:S(2)}) collective-permute-start(s16[2,272,256]{2,1,0:T(8,128)(2,1)S(1)} %get-tuple-element.36), channel_id=1, source_target_pairs={{0,4},{1,5},{2,6},{3,7},{4,0},{5,1},{6,2},{7,3},{8,12},{9,13},{10,... | collective-permute-start | bytes 835592 | tf_op jit(solution)/shard_map/column/ppermute | solution.py:25
  150.9 10.0 %collective-permute-start.30 = (f32[128,256]{1,0:T(8,128)S(1)}, f32[128,256]{1,0:T(8,128)S(1)}, u32[]{:S(2)}, u32[]{:S(2)}) collective-permute-start(f32[128,256]{1,0:T(8,128)S(1)} %bitcast.73), channel_id=1, source_target_pairs={{0,1},{1,0},{2,3},{3,2},{4,5},{5,4},{6,7},{7,6},{8,9},{9,8},{10,11... | collective-permute-start | bytes 393224 | tf_op jit(solution)/shard_map/back/ppermute | solution.py:25
  151.0 9.9 %collective-permute-start.31 = (f32[128,256]{1,0:T(8,128)S(1)}, f32[128,256]{1,0:T(8,128)S(1)}, u32[]{:S(2)}, u32[]{:S(2)}) collective-permute-start(f32[128,256]{1,0:T(8,128)S(1)} %bitcast.74), channel_id=1, source_target_pairs={{0,2},{1,3},{2,0},{3,1},{4,6},{5,7},{6,4},{7,5},{8,10},{9,11},{10,... | collective-permute-start | bytes 393224 | tf_op jit(solution)/shard_map/back/ppermute | solution.py:25
  (17 other events, 240.5 us)

commit v5 on v4

--- a/solution.py
+++ b/solution.py
@@ -56,8 +56,12 @@
     return z_to, x_to, core ^ (y % 2), zl // 2, 2 * (zl % 2) + x // 2
 
 
-def to_plane(value):
-    return send(value, plane_spot)
+def to_plane(value, flip):
+    def where(*place):
+        zl, *rest = plane_spot(*place)
+        return zl ^ flip, *rest
+
+    return send(value, where)
 
 
 def chunk_spot(zl, x, zh, y):
@@ -288,17 +292,17 @@
 
     with jax.named_scope("spread"):
         take = lambda value: lax.dynamic_index_in_dim(value, 2 * zh + y // 2, 1, keepdims=False)
-        own = to_plane(jnp.where(core == y % 2, take(panel_one), take(panel_two)))
+        own = jnp.where(core == y % 2, take(panel_one), take(panel_two))
+        own = [to_plane(own, 0), to_plane(own, 2)]
 
     with jax.named_scope("swap"):
         other_blocks = to_core(ancestors)
-        held_one, held_two, own = tie(panel_one, panel_two, own)
-        mine = jnp.swapaxes(jnp.where(first, held_one, held_two), 2, 3)
-        theirs = to_core(jnp.swapaxes(jnp.where(first, held_two, held_one), 2, 3))
+        mine = jnp.swapaxes(jnp.where(first, panel_one, panel_two), 2, 3)
+        theirs = to_core(jnp.swapaxes(jnp.where(first, panel_two, panel_one), 2, 3))
 
     present = jnp.where(first, present_one, present_two)
     x_from = ((x + jnp.array([0, 3, 1, 2], jnp.int32)) % 4)[:, None]
-    z_from = (zl ^ jnp.arange(4, dtype=jnp.int32))[None, :]
+    z_from = (zl ^ jnp.array([0, 2, 1, 2 ^ 1], jnp.int32))[None, :]
     spots = chunk_spot(z_from, x_from, zh, y)
     live_near = lax.dynamic_slice_in_dim(present, 4 * row, 4, 1)
     live_far = lax.dynamic_slice_in_dim(present, 4 * (row ^ 1), 4, 1)
@@ -313,7 +317,7 @@
     ).astype(jnp.int32)
 
     with jax.named_scope("gather"):
-        parts = [own] + [to_zl(own, k) for k in (1, 2, 3)]
+        parts = own + [to_zl(part, 1) for part in own]
         a0, b0 = [jnp.stack([part[k] for part in parts]) for k in range(2)]
         a0, b0, other_blocks, theirs = tie(a0, b0, other_blocks, theirs)
         a1, b2 = along_x(a0, 1), along_x(b0, -1)

time: 172 us -> 169 us (0.983); the launches traced: 169 us -> 169 us
  starting transfers between devices: 82.6 us -> 76.3 us
  waiting for transfers between devices: 47.3 us -> 53.3 us
    ppermute x34, starting transfers between devices: 82.6 us -> 76.3 us  [send(): return lax.ppermute(value, AXES, pairs)]
    ppermute x34, waiting for transfers between devices: 47.3 us -> 53.3 us  [send(): return lax.ppermute(value, AXES, pairs)]
    unnamed x15 -> x21, local copies, waits for them, and re-layouts: 2.46 us -> 6.39 us
    optimization_barrier x2 -> x0, local copies, waits for them, and re-layouts: 2.95 us -> none  [body(): tie = lambda *values: lax.optimization_barrier(values)]
    slice x4, local copies, waits for them, and re-layouts: 2.98 us -> 1.05 us  [body(): a0, b0 = [jnp.stack([part[k] for part in parts]) for k in range(2)]]
  transfers between devices with their start and end apart: 34 -> 34, of which waited for: 11 -> 11; matrix products, arithmetic and copies ran while one was open for 6% -> 5% of each run, Pallas kernels for 8% -> 8%
where the time goes in v5:
time: 169 us
  starting transfers between devices  76.3 us (45%)
  waiting for transfers between devices  53.3 us (32%)
  Pallas kernels  23.2 us (14%)
  local copies, waits for them, and re-layouts  8.42 us (5%)
  other arithmetic  6.26 us (4%)
    ppermute x34, starting transfers between devices, send(): return lax.ppermute(value, AXES, pairs)  76.3 us
    ppermute x34, waiting for transfers between devices, send(): return lax.ppermute(value, AXES, pairs)  53.3 us
    pallas_call x1, Pallas kernels, first_products(): pl.pallas_call(first_kernel, grid_spec=pltpu.PrefetchScalarGridSpec(num_s...  12.4 us
    pallas_call x1, Pallas kernels, second_products(): pl.pallas_call(second_kernel, grid_spec=pltpu.PrefetchScalarGridSpec(num_...  10 us
    unnamed x21, local copies, waits for them, and re-layouts  6.39 us
  transfers between devices with their start and end apart: 34, of which 11 were waited for; matrix products, arithmetic and copies ran while one was open for 5% of the time, Pallas kernels for 8%

profile of v5, /device:TPU:1, one launch (start us, length us, event | category | flops | bytes accessed | tf_op | source)
XLA Modules:
  0.0 168.5 jit_solution(16292995290619916524)
XLA Ops:
  0.7 3.3 %collective-permute-start.4 = (bf16[4,16,256,256]{3,2,1,0:T(8,128)(2,1)}, bf16[4,16,256,256]{3,2,1,0:T(8,128)(2,1)}, u32[]{:S(2)}, u32[]{:S(2)}) collective-permute-start(bf16[4,16,256,256]{3,2,1,0:T(8,128)(2,1)} %near.3), channel_id=1, source_target_pairs={{0,8},{1,9},{2,10},{3,11},{4,12},{5,13},{6,14},{7,15},{8,0},{9,1},... | collective-permute-start | bytes 25165832 | tf_op jit(solution)/shard_map/swap/ppermute | solution.py:25
  7.7 10.0 %collective-permute-start.1 = (bf16[2,256,256]{2,1,0:T(8,128)(2,1)}, bf16[2,256,256]{2,1,0:T(8,128)(2,1)S(1)}, u32[]{:S(2)}, u32[]{:S(2)}) collective-permute-start(bf16[2,256,256]{2,1,0:T(8,128)(2,1)} %fusion), channel_id=1, source_target_pairs={{0,128},{1,136},{2,176},{3,184},{4,0},{5,8},{6,48},{7,56},{8,200},... | collective-permute-start | bytes 786440 | tf_op jit(solution)/shard_map/spread/ppermute | solution.py:25
  21.8 2.7 %collective-permute-start.2 = (bf16[2,256,256]{2,1,0:T(8,128)(2,1)}, bf16[2,256,256]{2,1,0:T(8,128)(2,1)S(1)}, u32[]{:S(2)}, u32[]{:S(2)}) collective-permute-start(bf16[2,256,256]{2,1,0:T(8,128)(2,1)} %collective-permute-done), channel_id=1, source_target_pairs={{0,64},{1,65},{2,66},{3,67},{4,68},{5,69},{6,70},{7,71},{8,72},{9,... | collective-permute-start | bytes 786440 | tf_op jit(solution)/shard_map/gather/ppermute | solution.py:25
  26.8 6.9 %collective-permute-done.2 = bf16[2,256,256]{2,1,0:T(8,128)(2,1)S(1)} collective-permute-done((bf16[2,256,256]{2,1,0:T(8,128)(2,1)}, bf16[2,256,256]{2,1,0:T(8,128)(2,1)S(1)}, u32[]{:S(2)}, u32[]{:S(2)}) %collective-permute-start.2) | collective-permute-done | bytes 262176 | tf_op jit(solution)/shard_map/gather/ppermute | solution.py:25
  33.7 5.4 %collective-permute-done.3 = bf16[2,256,256]{2,1,0:T(8,128)(2,1)S(1)} collective-permute-done((bf16[2,256,256]{2,1,0:T(8,128)(2,1)S(1)}, bf16[2,256,256]{2,1,0:T(8,128)(2,1)S(1)}, u32[]{:S(2)}, u32[]{:S(2)}) %collective-permute-start.3) | collective-permute-done | bytes 262176 | tf_op jit(solution)/shard_map/gather/ppermute | solution.py:25
  40.3 6.1 %collective-permute-start.8 = (bf16[4,256,256]{2,1,0:T(8,128)(2,1)S(1)}, bf16[4,256,256]{2,1,0:T(8,128)(2,1)S(1)}, u32[]{:S(2)}, u32[]{:S(2)}) collective-permute-start(bf16[4,256,256]{2,1,0:T(8,128)(2,1)S(1)} %get-tuple-element.20.a0), channel_id=1, source_target_pairs={{0,48},{1,49},{2,50},{3,51},{4,52},{5,53},{6,54},{7,55},{8,56},{9,... | collective-permute-start | bytes 1572872 | tf_op jit(solution)/shard_map/gather/ppermute | solution.py:25
  46.4 2.7 %collective-permute-start.9 = (bf16[4,256,256]{2,1,0:T(8,128)(2,1)S(1)}, bf16[4,256,256]{2,1,0:T(8,128)(2,1)}, u32[]{:S(2)}, u32[]{:S(2)}) collective-permute-start(bf16[4,256,256]{2,1,0:T(8,128)(2,1)S(1)} %get-tuple-element.21.b0), channel_id=1, source_target_pairs={{0,48},{1,49},{2,50},{3,51},{4,52},{5,53},{6,54},{7,55},{8,56},{9,... | collective-permute-start | bytes 1572872 | tf_op jit(solution)/shard_map/gather/ppermute | solution.py:25
  50.0 7.8 %collective-permute-done.6.a1 = bf16[4,256,256]{2,1,0:T(8,128)(2,1)S(1)} collective-permute-done((bf16[4,256,256]{2,1,0:T(8,128)(2,1)S(1)}, bf16[4,256,256]{2,1,0:T(8,128)(2,1)S(1)}, u32[]{:S(2)}, u32[]{:S(2)}) %collective-permute-start.6) | collective-permute-done | bytes 524320 | tf_op jit(solution)/shard_map/gather/ppermute | solution.py:25
  57.8 10.2 %collective-permute-done.9.b2 = bf16[4,256,256]{2,1,0:T(8,128)(2,1)} collective-permute-done((bf16[4,256,256]{2,1,0:T(8,128)(2,1)S(1)}, bf16[4,256,256]{2,1,0:T(8,128)(2,1)}, u32[]{:S(2)}, u32[]{:S(2)}) %collective-permute-start.9) | collective-permute-done | bytes 524320 | tf_op jit(solution)/shard_map/gather/ppermute | solution.py:25
  68.0 3.5 %collective-permute-start.11 = (bf16[4,256,256]{2,1,0:T(8,128)(2,1)}, bf16[4,256,256]{2,1,0:T(8,128)(2,1)S(1)}, u32[]{:S(2)}, u32[]{:S(2)}) collective-permute-start(bf16[4,256,256]{2,1,0:T(8,128)(2,1)} %collective-permute-done.9.b2), channel_id=1, source_target_pairs={{0,48},{1,49},{2,50},{3,51},{4,52},{5,53},{6,54},{7,55},{8,56},{9,... | collective-permute-start | bytes 1572872 | tf_op jit(solution)/shard_map/gather/ppermute | solution.py:25
  71.5 12.4 %product.2.acc_in = f32[2,4,256,512]{3,2,1,0:T(8,128)} custom-call(s32[66]{0:T(128)S(1)} %concatenate.3.scal, bf16[4,16,256,256]{3,2,1,0:T(8,128)(2,1)} %near.3, bf16[4,16,256,256]{3,2,1,0:T(8,128)(2,1)} %collective-permute-done.4.far, bf16[4,256,256]{2,1,0:T(8,128)(2,1)S(1)} %get-tuple-element.20.a0, bf16[4,256,256]{2,1,0:T(8,128)(2,1)S(1)} %get-tuple-element.21.b0, ...), custom_call_target="tpu_custom_call" | custom-call | flops 6442450944 | bytes 25165824 | tf_op jit(solution)/shard_map/product/pallas_call | solution.py:165
  83.9 10.0 %product.3 = (f32[2,2,256,256]{3,2,1,0:T(8,128)S(1)}, s16[2,2,272,256]{3,2,1,0:T(8,128)(2,1)S(1)}, s16[2,2,272,256]{3,2,1,0:T(8,128)(2,1)S(1)}, s16[2,2,272,256]{3,2,1,0:T(8,128)(2,1)S(1)}, f32[2,256,256]{2,1,0:T(8,128)S(1)}) custom-call(s32[66]{0:T(128)S(1)} %concatenate.3.scal, f32[2,4,256,512]{3,2,1,0:T(8,128)} %product.2.acc_in, ...), custom_call_target="tpu_custom_call" | custom-call | flops 2147483648 | bytes 16777216 | tf_op jit(solution)/shard_map/product/pallas_call | solution.py:187
  96.8 3.6 %collective-permute-start.14 = (f32[128,256]{1,0:T(8,128)S(1)}, f32[128,256]{1,0:T(8,128)S(1)}, u32[]{:S(2)}, u32[]{:S(2)}) collective-permute-start(f32[128,256]{1,0:T(8,128)S(1)} %get-tuple-element.46), channel_id=1, source_target_pairs={{0,3},{1,2},{2,1},{3,0},{4,7},{5,6},{6,5},{7,4},{8,11},{9,10},{10,... | collective-permute-start | bytes 393224 | tf_op jit(solution)/shard_map/diag/ppermute | solution.py:25
  102.8 3.2 %collective-permute-done.14 = f32[128,256]{1,0:T(8,128)S(1)} collective-permute-done((f32[128,256]{1,0:T(8,128)S(1)}, f32[128,256]{1,0:T(8,128)S(1)}, u32[]{:S(2)}, u32[]{:S(2)}) %collective-permute-start.14) | collective-permute-done | bytes 131104 | tf_op jit(solution)/shard_map/diag/ppermute | solution.py:25
  106.4 3.6 %collective-permute-start.17 = (f32[32,256]{1,0:T(8,128)S(1)}, f32[32,256]{1,0:T(8,128)S(1)}, u32[]{:S(2)}, u32[]{:S(2)}) collective-permute-start(f32[32,256]{1,0:T(8,128)S(1)} %get-tuple-element.61), channel_id=1, source_target_pairs={{0,48},{1,49},{2,50},{3,51},{4,52},{5,53},{6,54},{7,55},{8,56},{9,... | collective-permute-start | bytes 98312 | tf_op jit(solution)/shard_map/diag/ppermute | solution.py:25
  111.1 2.8 %collective-permute-start.23 = (s16[2,2,272,256]{3,2,1,0:T(8,128)(2,1)}, s16[2,2,272,256]{3,2,1,0:T(8,128)(2,1)S(1)}, u32[]{:S(2)}, u32[]{:S(2)}) collective-permute-start(s16[2,2,272,256]{3,2,1,0:T(8,128)(2,1)} %copy-done), channel_id=1, source_target_pairs={{0,3},{1,2},{2,1},{3,0},{4,7},{5,6},{6,5},{7,4},{8,11},{9,10},{10,... | collective-permute-start | bytes 1671176 | tf_op jit(solution)/shard_map/column/ppermute | solution.py:25
  114.4 3.1 %collective-permute-start.19 = (f32[32,256]{1,0:T(8,128)S(1)}, f32[32,256]{1,0:T(8,128)S(1)}, u32[]{:S(2)}, u32[]{:S(2)}) collective-permute-start(f32[32,256]{1,0:T(8,128)S(1)} %fusion.2), channel_id=1, source_target_pairs={{0,128},{1,129},{2,130},{3,131},{4,132},{5,133},{6,134},{7,135},{8... | collective-permute-start | bytes 98312 | tf_op jit(solution)/shard_map/diag/ppermute | solution.py:25
  117.6 2.7 %collective-permute-start.20 = (f32[32,256]{1,0:T(8,128)S(1)}, f32[32,256]{1,0:T(8,128)S(1)}, u32[]{:S(2)}, u32[]{:S(2)}) collective-permute-start(f32[32,256]{1,0:T(8,128)S(1)} %fusion.2), channel_id=1, source_target_pairs={{0,192},{1,193},{2,194},{3,195},{4,196},{5,197},{6,198},{7,199},{8... | collective-permute-start | bytes 98312 | tf_op jit(solution)/shard_map/diag/ppermute | solution.py:25
  122.2 7.3 %collective-permute-start.26 = (f32[32,256]{1,0:T(8,128)S(1)}, f32[32,256]{1,0:T(8,128)S(1)}, u32[]{:S(2)}, u32[]{:S(2)}) collective-permute-start(f32[32,256]{1,0:T(8,128)S(1)} %add_add_fusion), channel_id=1, source_target_pairs={{0,4},{1,5},{2,6},{3,7},{4,0},{5,1},{6,2},{7,3},{8,12},{9,13},{10,... | collective-permute-start | bytes 98312 | tf_op jit(solution)/shard_map/column/ppermute | solution.py:25
  129.5 6.3 %collective-permute-done.23.q3 = s16[2,2,272,256]{3,2,1,0:T(8,128)(2,1)S(1)} collective-permute-done((s16[2,2,272,256]{3,2,1,0:T(8,128)(2,1)}, s16[2,2,272,256]{3,2,1,0:T(8,128)(2,1)S(1)}, u32[]{:S(2)}, u32[]{:S(2)}) %collective-permute-start.23) | collective-permute-done | bytes 557088 | tf_op jit(solution)/shard_map/column/ppermute | solution.py:25
  137.9 2.6 %collective-permute-start.29 = (f32[32,256]{1,0:T(8,128)S(1)}, f32[32,256]{1,0:T(8,128)S(1)}, u32[]{:S(2)}, u32[]{:S(2)}) collective-permute-start(f32[32,256]{1,0:T(8,128)S(1)} %add.209), channel_id=1, source_target_pairs={{0,48},{1,49},{2,50},{3,51},{4,52},{5,53},{6,54},{7,55},{8,56},{9,... | collective-permute-start | bytes 98312 | tf_op jit(solution)/shard_map/back/ppermute | solution.py:25
  140.6 8.9 %collective-permute-start.24 = (s16[2,272,256]{2,1,0:T(8,128)(2,1)S(1)}, s16[2,272,256]{2,1,0:T(8,128)(2,1)S(1)}, u32[]{:S(2)}, u32[]{:S(2)}) collective-permute-start(s16[2,272,256]{2,1,0:T(8,128)(2,1)S(1)} %get-tuple-element.30), channel_id=1, source_target_pairs={{0,4},{1,5},{2,6},{3,7},{4,0},{5,1},{6,2},{7,3},{8,12},{9,13},{10,... | collective-permute-start | bytes 835592 | tf_op jit(solution)/shard_map/column/ppermute | solution.py:25
  149.7 2.8 %collective-permute-start.31 = (f32[128,256]{1,0:T(8,128)S(1)}, f32[128,256]{1,0:T(8,128)S(1)}, u32[]{:S(2)}, u32[]{:S(2)}) collective-permute-start(f32[128,256]{1,0:T(8,128)S(1)} %bitcast.74), channel_id=1, source_target_pairs={{0,2},{1,3},{2,0},{3,1},{4,6},{5,7},{6,4},{7,5},{8,10},{9,11},{10,... | collective-permute-start | bytes 393224 | tf_op jit(solution)/shard_map/back/ppermute | solution.py:25
  153.5 7.4 %collective-permute-done.24 = s16[2,272,256]{2,1,0:T(8,128)(2,1)S(1)} collective-permute-done((s16[2,272,256]{2,1,0:T(8,128)(2,1)S(1)}, s16[2,272,256]{2,1,0:T(8,128)(2,1)S(1)}, u32[]{:S(2)}, u32[]{:S(2)}) %collective-permute-start.24) | collective-permute-done | bytes 278560 | tf_op jit(solution)/shard_map/column/ppermute | solution.py:25
  (106 shorter events, 32.1 us)
Async XLA Ops:
  0.7 38.7 %collective-permute-start.4 = (bf16[4,16,256,256]{3,2,1,0:T(8,128)(2,1)}, bf16[4,16,256,256]{3,2,1,0:T(8,128)(2,1)}, u32[]{:S(2)}, u32[]{:S(2)}) collective-permute-start(bf16[4,16,256,256]{3,2,1,0:T(8,128)(2,1)} %near.3), channel_id=1, source_target_pairs={{0,8},{1,9},{2,10},{3,11},{4,12},{5,13},{6,14},{7,15},{8,0},{9,1},... | collective-permute-start | bytes 25165832 | tf_op jit(solution)/shard_map/swap/ppermute | solution.py:25
  5.8 16.1 %collective-permute-start = (bf16[2,256,256]{2,1,0:T(8,128)(2,1)}, bf16[2,256,256]{2,1,0:T(8,128)(2,1)}, u32[]{:S(2)}, u32[]{:S(2)}) collective-permute-start(bf16[2,256,256]{2,1,0:T(8,128)(2,1)} %fusion), channel_id=1, source_target_pairs={{0,0},{1,8},{2,48},{3,56},{4,128},{5,136},{6,176},{7,184},{8,72},{... | collective-permute-start | bytes 786440 | tf_op jit(solution)/shard_map/spread/ppermute | solution.py:25
  7.7 17.8 %collective-permute-start.1 = (bf16[2,256,256]{2,1,0:T(8,128)(2,1)}, bf16[2,256,256]{2,1,0:T(8,128)(2,1)S(1)}, u32[]{:S(2)}, u32[]{:S(2)}) collective-permute-start(bf16[2,256,256]{2,1,0:T(8,128)(2,1)} %fusion), channel_id=1, source_target_pairs={{0,128},{1,136},{2,176},{3,184},{4,0},{5,8},{6,48},{7,56},{8,200},... | collective-permute-start | bytes 786440 | tf_op jit(solution)/shard_map/spread/ppermute | solution.py:25
  21.8 17.6 %collective-permute-start.5 = (bf16[2,4,256,256]{3,2,1,0:T(8,128)(2,1)}, bf16[2,4,256,256]{3,2,1,0:T(8,128)(2,1)S(1)}, u32[]{:S(2)}, u32[]{:S(2)}) collective-permute-start(bf16[2,4,256,256]{3,2,1,0:T(8,128)(2,1)} %get-tuple-element.37), channel_id=1, source_target_pairs={{0,8},{1,9},{2,10},{3,11},{4,12},{5,13},{6,14},{7,15},{8,0},{9,1},... | collective-permute-start | bytes 3145736 | tf_op jit(solution)/shard_map/swap/ppermute | solution.py:25
  21.8 11.9 %collective-permute-start.2 = (bf16[2,256,256]{2,1,0:T(8,128)(2,1)}, bf16[2,256,256]{2,1,0:T(8,128)(2,1)S(1)}, u32[]{:S(2)}, u32[]{:S(2)}) collective-permute-start(bf16[2,256,256]{2,1,0:T(8,128)(2,1)} %collective-permute-done), channel_id=1, source_target_pairs={{0,64},{1,65},{2,66},{3,67},{4,68},{5,69},{6,70},{7,71},{8,72},{9,... | collective-permute-start | bytes 786440 | tf_op jit(solution)/shard_map/gather/ppermute | solution.py:25
  25.5 13.7 %collective-permute-start.3 = (bf16[2,256,256]{2,1,0:T(8,128)(2,1)S(1)}, bf16[2,256,256]{2,1,0:T(8,128)(2,1)S(1)}, u32[]{:S(2)}, u32[]{:S(2)}) collective-permute-start(bf16[2,256,256]{2,1,0:T(8,128)(2,1)S(1)} %collective-permute-done.1), channel_id=1, source_target_pairs={{0,64},{1,65},{2,66},{3,67},{4,68},{5,69},{6,70},{7,71},{8,72},{9,... | collective-permute-start | bytes 786440 | tf_op jit(solution)/shard_map/gather/ppermute | solution.py:25
  40.3 17.5 %collective-permute-start.6 = (bf16[4,256,256]{2,1,0:T(8,128)(2,1)S(1)}, bf16[4,256,256]{2,1,0:T(8,128)(2,1)S(1)}, u32[]{:S(2)}, u32[]{:S(2)}) collective-permute-start(bf16[4,256,256]{2,1,0:T(8,128)(2,1)S(1)} %get-tuple-element.20.a0), channel_id=1, source_target_pairs={{0,16},{1,17},{2,18},{3,19},{4,20},{5,21},{6,22},{7,23},{8,24},{9,... | collective-permute-start | bytes 1572872 | tf_op jit(solution)/shard_map/gather/ppermute | solution.py:25
  40.3 31.2 %collective-permute-start.8 = (bf16[4,256,256]{2,1,0:T(8,128)(2,1)S(1)}, bf16[4,256,256]{2,1,0:T(8,128)(2,1)S(1)}, u32[]{:S(2)}, u32[]{:S(2)}) collective-permute-start(bf16[4,256,256]{2,1,0:T(8,128)(2,1)S(1)} %get-tuple-element.20.a0), channel_id=1, source_target_pairs={{0,48},{1,49},{2,50},{3,51},{4,52},{5,53},{6,54},{7,55},{8,56},{9,... | collective-permute-start | bytes 1572872 | tf_op jit(solution)/shard_map/gather/ppermute | solution.py:25
  46.4 25.1 %collective-permute-start.7 = (bf16[4,256,256]{2,1,0:T(8,128)(2,1)S(1)}, bf16[4,256,256]{2,1,0:T(8,128)(2,1)}, u32[]{:S(2)}, u32[]{:S(2)}) collective-permute-start(bf16[4,256,256]{2,1,0:T(8,128)(2,1)S(1)} %get-tuple-element.21.b0), channel_id=1, source_target_pairs={{0,16},{1,17},{2,18},{3,19},{4,20},{5,21},{6,22},{7,23},{8,24},{9,... | collective-permute-start | bytes 1572872 | tf_op jit(solution)/shard_map/gather/ppermute | solution.py:25
  46.4 21.6 %collective-permute-start.9 = (bf16[4,256,256]{2,1,0:T(8,128)(2,1)S(1)}, bf16[4,256,256]{2,1,0:T(8,128)(2,1)}, u32[]{:S(2)}, u32[]{:S(2)}) collective-permute-start(bf16[4,256,256]{2,1,0:T(8,128)(2,1)S(1)} %get-tuple-element.21.b0), channel_id=1, source_target_pairs={{0,48},{1,49},{2,50},{3,51},{4,52},{5,53},{6,54},{7,55},{8,56},{9,... | collective-permute-start | bytes 1572872 | tf_op jit(solution)/shard_map/gather/ppermute | solution.py:25
  57.8 26.1 %collective-permute-start.10 = (bf16[4,256,256]{2,1,0:T(8,128)(2,1)S(1)}, bf16[4,256,256]{2,1,0:T(8,128)(2,1)S(1)}, u32[]{:S(2)}, u32[]{:S(2)}) collective-permute-start(bf16[4,256,256]{2,1,0:T(8,128)(2,1)S(1)} %collective-permute-done.6.a1), channel_id=1, source_target_pairs={{0,16},{1,17},{2,18},{3,19},{4,20},{5,21},{6,22},{7,23},{8,24},{9,... | collective-permute-start | bytes 1572872 | tf_op jit(solution)/shard_map/gather/ppermute | solution.py:25
  68.0 16.0 %collective-permute-start.11 = (bf16[4,256,256]{2,1,0:T(8,128)(2,1)}, bf16[4,256,256]{2,1,0:T(8,128)(2,1)S(1)}, u32[]{:S(2)}, u32[]{:S(2)}) collective-permute-start(bf16[4,256,256]{2,1,0:T(8,128)(2,1)} %collective-permute-done.9.b2), channel_id=1, source_target_pairs={{0,48},{1,49},{2,50},{3,51},{4,52},{5,53},{6,54},{7,55},{8,56},{9,... | collective-permute-start | bytes 1572872 | tf_op jit(solution)/shard_map/gather/ppermute | solution.py:25
  96.8 9.2 %collective-permute-start.14 = (f32[128,256]{1,0:T(8,128)S(1)}, f32[128,256]{1,0:T(8,128)S(1)}, u32[]{:S(2)}, u32[]{:S(2)}) collective-permute-start(f32[128,256]{1,0:T(8,128)S(1)} %get-tuple-element.46), channel_id=1, source_target_pairs={{0,3},{1,2},{2,1},{3,0},{4,7},{5,6},{6,5},{7,4},{8,11},{9,10},{10,... | collective-permute-start | bytes 393224 | tf_op jit(solution)/shard_map/diag/ppermute | solution.py:25
  106.2 16.1 %collective-permute-start.21 = (s16[2,2,272,256]{3,2,1,0:T(8,128)(2,1)}, s16[2,2,272,256]{3,2,1,0:T(8,128)(2,1)S(1)}, u32[]{:S(2)}, u32[]{:S(2)}) collective-permute-start(s16[2,2,272,256]{3,2,1,0:T(8,128)(2,1)} %copy-done.2), channel_id=1, source_target_pairs={{0,1},{1,0},{2,3},{3,2},{4,5},{5,4},{6,7},{7,6},{8,9},{9,8},{10,11... | collective-permute-start | bytes 1671176 | tf_op jit(solution)/shard_map/column/ppermute | solution.py:25
  110.0 19.5 %collective-permute-start.22 = (s16[2,2,272,256]{3,2,1,0:T(8,128)(2,1)}, s16[2,2,272,256]{3,2,1,0:T(8,128)(2,1)S(1)}, u32[]{:S(2)}, u32[]{:S(2)}) collective-permute-start(s16[2,2,272,256]{3,2,1,0:T(8,128)(2,1)} %copy-done.1), channel_id=1, source_target_pairs={{0,2},{1,3},{2,0},{3,1},{4,6},{5,7},{6,4},{7,5},{8,10},{9,11},{10,... | collective-permute-start | bytes 1671176 | tf_op jit(solution)/shard_map/column/ppermute | solution.py:25
  111.1 24.7 %collective-permute-start.23 = (s16[2,2,272,256]{3,2,1,0:T(8,128)(2,1)}, s16[2,2,272,256]{3,2,1,0:T(8,128)(2,1)S(1)}, u32[]{:S(2)}, u32[]{:S(2)}) collective-permute-start(s16[2,2,272,256]{3,2,1,0:T(8,128)(2,1)} %copy-done), channel_id=1, source_target_pairs={{0,3},{1,2},{2,1},{3,0},{4,7},{5,6},{6,5},{7,4},{8,11},{9,10},{10,... | collective-permute-start | bytes 1671176 | tf_op jit(solution)/shard_map/column/ppermute | solution.py:25
  122.2 14.3 %collective-permute-start.26 = (f32[32,256]{1,0:T(8,128)S(1)}, f32[32,256]{1,0:T(8,128)S(1)}, u32[]{:S(2)}, u32[]{:S(2)}) collective-permute-start(f32[32,256]{1,0:T(8,128)S(1)} %add_add_fusion), channel_id=1, source_target_pairs={{0,4},{1,5},{2,6},{3,7},{4,0},{5,1},{6,2},{7,3},{8,12},{9,13},{10,... | collective-permute-start | bytes 98312 | tf_op jit(solution)/shard_map/column/ppermute | solution.py:25
  136.6 12.9 %collective-permute-start.27 = (f32[32,256]{1,0:T(8,128)S(1)}, f32[32,256]{1,0:T(8,128)S(1)}, u32[]{:S(2)}, u32[]{:S(2)}) collective-permute-start(f32[32,256]{1,0:T(8,128)S(1)} %add.209), channel_id=1, source_target_pairs={{0,16},{1,17},{2,18},{3,19},{4,20},{5,21},{6,22},{7,23},{8,24},{9,... | collective-permute-start | bytes 98312 | tf_op jit(solution)/shard_map/back/ppermute | solution.py:25
  136.7 12.8 %collective-permute-start.28 = (f32[32,256]{1,0:T(8,128)S(1)}, f32[32,256]{1,0:T(8,128)S(1)}, u32[]{:S(2)}, u32[]{:S(2)}) collective-permute-start(f32[32,256]{1,0:T(8,128)S(1)} %add.209), channel_id=1, source_target_pairs={{0,32},{1,33},{2,34},{3,35},{4,36},{5,37},{6,38},{7,39},{8,40},{9,... | collective-permute-start | bytes 98312 | tf_op jit(solution)/shard_map/back/ppermute | solution.py:25
  137.9 11.6 %collective-permute-start.29 = (f32[32,256]{1,0:T(8,128)S(1)}, f32[32,256]{1,0:T(8,128)S(1)}, u32[]{:S(2)}, u32[]{:S(2)}) collective-permute-start(f32[32,256]{1,0:T(8,128)S(1)} %add.209), channel_id=1, source_target_pairs={{0,48},{1,49},{2,50},{3,51},{4,52},{5,53},{6,54},{7,55},{8,56},{9,... | collective-permute-start | bytes 98312 | tf_op jit(solution)/shard_map/back/ppermute | solution.py:25
  140.6 20.3 %collective-permute-start.24 = (s16[2,272,256]{2,1,0:T(8,128)(2,1)S(1)}, s16[2,272,256]{2,1,0:T(8,128)(2,1)S(1)}, u32[]{:S(2)}, u32[]{:S(2)}) collective-permute-start(s16[2,272,256]{2,1,0:T(8,128)(2,1)S(1)} %get-tuple-element.30), channel_id=1, source_target_pairs={{0,4},{1,5},{2,6},{3,7},{4,0},{5,1},{6,2},{7,3},{8,12},{9,13},{10,... | collective-permute-start | bytes 835592 | tf_op jit(solution)/shard_map/column/ppermute | solution.py:25
  149.6 13.8 %collective-permute-start.30 = (f32[128,256]{1,0:T(8,128)S(1)}, f32[128,256]{1,0:T(8,128)S(1)}, u32[]{:S(2)}, u32[]{:S(2)}) collective-permute-start(f32[128,256]{1,0:T(8,128)S(1)} %bitcast.73), channel_id=1, source_target_pairs={{0,1},{1,0},{2,3},{3,2},{4,5},{5,4},{6,7},{7,6},{8,9},{9,8},{10,11... | collective-permute-start | bytes 393224 | tf_op jit(solution)/shard_map/back/ppermute | solution.py:25
  149.7 13.7 %collective-permute-start.31 = (f32[128,256]{1,0:T(8,128)S(1)}, f32[128,256]{1,0:T(8,128)S(1)}, u32[]{:S(2)}, u32[]{:S(2)}) collective-permute-start(f32[128,256]{1,0:T(8,128)S(1)} %bitcast.74), channel_id=1, source_target_pairs={{0,2},{1,3},{2,0},{3,1},{4,6},{5,7},{6,4},{7,5},{8,10},{9,11},{10,... | collective-permute-start | bytes 393224 | tf_op jit(solution)/shard_map/back/ppermute | solution.py:25
  152.5 11.0 %collective-permute-start.32 = (f32[128,256]{1,0:T(8,128)S(1)}, f32[128,256]{1,0:T(8,128)S(1)}, u32[]{:S(2)}, u32[]{:S(2)}) collective-permute-start(f32[128,256]{1,0:T(8,128)S(1)} %bitcast.75), channel_id=1, source_target_pairs={{0,3},{1,2},{2,1},{3,0},{4,7},{5,6},{6,5},{7,4},{8,11},{9,10},{10,... | collective-permute-start | bytes 393224 | tf_op jit(solution)/shard_map/back/ppermute | solution.py:25
  (19 other events, 262.8 us)

commit v6 on v5

--- a/solution.py
+++ b/solution.py
@@ -351,8 +351,8 @@
         got = to_zh(give)
         block = keep + decode(got[:, :256], got[:, 256:257])
     with jax.named_scope("back"):
-        piece = tie(piece, keep)[0]
         part = collect(piece, x, to_x).reshape(128, 256)
+        part = tie(part, keep)[0]
         whole = collect(part, y, to_y).reshape(2, 256, 256)
         near, far = block[0], to_core(block[1])
         whole = tie(whole, far)[0]

time: 169 us -> 163 us (0.964)
  starting transfers between devices: 76.3 us -> 73 us
  waiting for transfers between devices: 53.3 us -> 51.3 us
    ppermute x34, starting transfers between devices: 76.3 us -> 73 us  [send(): return lax.ppermute(value, AXES, pairs)]
    ppermute x34, waiting for transfers between devices: 53.3 us -> 51.3 us  [send(): return lax.ppermute(value, AXES, pairs)]
    unnamed x21 -> x23, local copies, waits for them, and re-layouts: 6.39 us -> 6.38 us
  transfers between devices with their start and end apart: 34 -> 34, of which waited for: 11 -> 13; matrix products, arithmetic and copies ran while one was open for 5% -> 6% of each run, Pallas kernels for 8% -> 8%
where the time goes in v6:
time: 163 us; the launch traced here: 162 us
  starting transfers between devices  73 us (45%)
  waiting for transfers between devices  51.3 us (31%)
  Pallas kernels  23.2 us (14%)
  local copies, waits for them, and re-layouts  8.41 us (5%)
  other arithmetic  5.32 us (3%)
    ppermute x34, starting transfers between devices, send(): return lax.ppermute(value, AXES, pairs)  73 us
    ppermute x34, waiting for transfers between devices, send(): return lax.ppermute(value, AXES, pairs)  51.3 us
    pallas_call x1, Pallas kernels, first_products(): pl.pallas_call(first_kernel, grid_spec=pltpu.PrefetchScalarGridSpec(num_s...  12.4 us
    pallas_call x1, Pallas kernels, second_products(): pl.pallas_call(second_kernel, grid_spec=pltpu.PrefetchScalarGridSpec(num_...  10.1 us
    unnamed x23, local copies, waits for them, and re-layouts  6.38 us
  transfers between devices with their start and end apart: 34, of which 13 were waited for; matrix products, arithmetic and copies ran while one was open for 6% of the time, Pallas kernels for 8%

profile of v6, /device:TPU:1, one launch (start us, length us, event | category | flops | bytes accessed | tf_op | source)
XLA Modules:
  0.0 162.3 jit_solution(17469476358904155551)
XLA Ops:
  0.7 3.3 %collective-permute-start.4 = (bf16[4,16,256,256]{3,2,1,0:T(8,128)(2,1)}, bf16[4,16,256,256]{3,2,1,0:T(8,128)(2,1)}, u32[]{:S(2)}, u32[]{:S(2)}) collective-permute-start(bf16[4,16,256,256]{3,2,1,0:T(8,128)(2,1)} %near.3), channel_id=1, source_target_pairs={{0,8},{1,9},{2,10},{3,11},{4,12},{5,13},{6,14},{7,15},{8,0},{9,1},... | collective-permute-start | bytes 25165832 | tf_op jit(solution)/shard_map/swap/ppermute | solution.py:25
  7.7 10.0 %collective-permute-start.1 = (bf16[2,256,256]{2,1,0:T(8,128)(2,1)}, bf16[2,256,256]{2,1,0:T(8,128)(2,1)S(1)}, u32[]{:S(2)}, u32[]{:S(2)}) collective-permute-start(bf16[2,256,256]{2,1,0:T(8,128)(2,1)} %fusion), channel_id=1, source_target_pairs={{0,128},{1,136},{2,176},{3,184},{4,0},{5,8},{6,48},{7,56},{8,200},... | collective-permute-start | bytes 786440 | tf_op jit(solution)/shard_map/spread/ppermute | solution.py:25
  21.8 2.7 %collective-permute-start.2 = (bf16[2,256,256]{2,1,0:T(8,128)(2,1)}, bf16[2,256,256]{2,1,0:T(8,128)(2,1)S(1)}, u32[]{:S(2)}, u32[]{:S(2)}) collective-permute-start(bf16[2,256,256]{2,1,0:T(8,128)(2,1)} %collective-permute-done), channel_id=1, source_target_pairs={{0,64},{1,65},{2,66},{3,67},{4,68},{5,69},{6,70},{7,71},{8,72},{9,... | collective-permute-start | bytes 786440 | tf_op jit(solution)/shard_map/gather/ppermute | solution.py:25
  26.8 6.9 %collective-permute-done.2 = bf16[2,256,256]{2,1,0:T(8,128)(2,1)S(1)} collective-permute-done((bf16[2,256,256]{2,1,0:T(8,128)(2,1)}, bf16[2,256,256]{2,1,0:T(8,128)(2,1)S(1)}, u32[]{:S(2)}, u32[]{:S(2)}) %collective-permute-start.2) | collective-permute-done | bytes 262176 | tf_op jit(solution)/shard_map/gather/ppermute | solution.py:25
  33.7 5.4 %collective-permute-done.3 = bf16[2,256,256]{2,1,0:T(8,128)(2,1)S(1)} collective-permute-done((bf16[2,256,256]{2,1,0:T(8,128)(2,1)S(1)}, bf16[2,256,256]{2,1,0:T(8,128)(2,1)S(1)}, u32[]{:S(2)}, u32[]{:S(2)}) %collective-permute-start.3) | collective-permute-done | bytes 262176 | tf_op jit(solution)/shard_map/gather/ppermute | solution.py:25
  40.3 6.1 %collective-permute-start.8 = (bf16[4,256,256]{2,1,0:T(8,128)(2,1)S(1)}, bf16[4,256,256]{2,1,0:T(8,128)(2,1)S(1)}, u32[]{:S(2)}, u32[]{:S(2)}) collective-permute-start(bf16[4,256,256]{2,1,0:T(8,128)(2,1)S(1)} %get-tuple-element.20.a0), channel_id=1, source_target_pairs={{0,48},{1,49},{2,50},{3,51},{4,52},{5,53},{6,54},{7,55},{8,56},{9,... | collective-permute-start | bytes 1572872 | tf_op jit(solution)/shard_map/gather/ppermute | solution.py:25
  46.4 2.7 %collective-permute-start.9 = (bf16[4,256,256]{2,1,0:T(8,128)(2,1)S(1)}, bf16[4,256,256]{2,1,0:T(8,128)(2,1)}, u32[]{:S(2)}, u32[]{:S(2)}) collective-permute-start(bf16[4,256,256]{2,1,0:T(8,128)(2,1)S(1)} %get-tuple-element.21.b0), channel_id=1, source_target_pairs={{0,48},{1,49},{2,50},{3,51},{4,52},{5,53},{6,54},{7,55},{8,56},{9,... | collective-permute-start | bytes 1572872 | tf_op jit(solution)/shard_map/gather/ppermute | solution.py:25
  50.0 7.8 %collective-permute-done.6.a1 = bf16[4,256,256]{2,1,0:T(8,128)(2,1)S(1)} collective-permute-done((bf16[4,256,256]{2,1,0:T(8,128)(2,1)S(1)}, bf16[4,256,256]{2,1,0:T(8,128)(2,1)S(1)}, u32[]{:S(2)}, u32[]{:S(2)}) %collective-permute-start.6) | collective-permute-done | bytes 524320 | tf_op jit(solution)/shard_map/gather/ppermute | solution.py:25
  57.8 10.2 %collective-permute-done.9.b2 = bf16[4,256,256]{2,1,0:T(8,128)(2,1)} collective-permute-done((bf16[4,256,256]{2,1,0:T(8,128)(2,1)S(1)}, bf16[4,256,256]{2,1,0:T(8,128)(2,1)}, u32[]{:S(2)}, u32[]{:S(2)}) %collective-permute-start.9) | collective-permute-done | bytes 524320 | tf_op jit(solution)/shard_map/gather/ppermute | solution.py:25
  68.0 3.5 %collective-permute-start.11 = (bf16[4,256,256]{2,1,0:T(8,128)(2,1)}, bf16[4,256,256]{2,1,0:T(8,128)(2,1)S(1)}, u32[]{:S(2)}, u32[]{:S(2)}) collective-permute-start(bf16[4,256,256]{2,1,0:T(8,128)(2,1)} %collective-permute-done.9.b2), channel_id=1, source_target_pairs={{0,48},{1,49},{2,50},{3,51},{4,52},{5,53},{6,54},{7,55},{8,56},{9,... | collective-permute-start | bytes 1572872 | tf_op jit(solution)/shard_map/gather/ppermute | solution.py:25
  71.5 12.4 %product.2.acc_in = f32[2,4,256,512]{3,2,1,0:T(8,128)} custom-call(s32[66]{0:T(128)S(1)} %concatenate.3.scal, bf16[4,16,256,256]{3,2,1,0:T(8,128)(2,1)} %near.3, bf16[4,16,256,256]{3,2,1,0:T(8,128)(2,1)} %collective-permute-done.4.far, bf16[4,256,256]{2,1,0:T(8,128)(2,1)S(1)} %get-tuple-element.20.a0, bf16[4,256,256]{2,1,0:T(8,128)(2,1)S(1)} %get-tuple-element.21.b0, ...), custom_call_target="tpu_custom_call" | custom-call | flops 6442450944 | bytes 25165824 | tf_op jit(solution)/shard_map/product/pallas_call | solution.py:165
  83.9 10.1 %product.3 = (f32[2,2,256,256]{3,2,1,0:T(8,128)S(1)}, s16[2,2,272,256]{3,2,1,0:T(8,128)(2,1)S(1)}, s16[2,2,272,256]{3,2,1,0:T(8,128)(2,1)S(1)}, s16[2,2,272,256]{3,2,1,0:T(8,128)(2,1)S(1)}, f32[2,256,256]{2,1,0:T(8,128)S(1)}) custom-call(s32[66]{0:T(128)S(1)} %concatenate.3.scal, f32[2,4,256,512]{3,2,1,0:T(8,128)} %product.2.acc_in, ...), custom_call_target="tpu_custom_call" | custom-call | flops 2147483648 | bytes 16777216 | tf_op jit(solution)/shard_map/product/pallas_call | solution.py:187
  96.8 3.6 %collective-permute-start.14 = (f32[128,256]{1,0:T(8,128)S(1)}, f32[128,256]{1,0:T(8,128)S(1)}, u32[]{:S(2)}, u32[]{:S(2)}) collective-permute-start(f32[128,256]{1,0:T(8,128)S(1)} %get-tuple-element.46), channel_id=1, source_target_pairs={{0,3},{1,2},{2,1},{3,0},{4,7},{5,6},{6,5},{7,4},{8,11},{9,10},{10,... | collective-permute-start | bytes 393224 | tf_op jit(solution)/shard_map/diag/ppermute | solution.py:25
  100.4 2.3 %collective-permute-done.13 = f32[128,256]{1,0:T(8,128)S(1)} collective-permute-done((f32[128,256]{1,0:T(8,128)S(1)}, f32[128,256]{1,0:T(8,128)S(1)}, u32[]{:S(2)}, u32[]{:S(2)}) %collective-permute-start.13) | collective-permute-done | bytes 131104 | tf_op jit(solution)/shard_map/diag/ppermute | solution.py:25
  102.7 2.3 %collective-permute-done.14 = f32[128,256]{1,0:T(8,128)S(1)} collective-permute-done((f32[128,256]{1,0:T(8,128)S(1)}, f32[128,256]{1,0:T(8,128)S(1)}, u32[]{:S(2)}, u32[]{:S(2)}) %collective-permute-start.14) | collective-permute-done | bytes 131104 | tf_op jit(solution)/shard_map/diag/ppermute | solution.py:25
  105.8 3.2 %collective-permute-start.17 = (f32[32,256]{1,0:T(8,128)S(1)}, f32[32,256]{1,0:T(8,128)S(1)}, u32[]{:S(2)}, u32[]{:S(2)}) collective-permute-start(f32[32,256]{1,0:T(8,128)S(1)} %get-tuple-element.61), channel_id=1, source_target_pairs={{0,48},{1,49},{2,50},{3,51},{4,52},{5,53},{6,54},{7,55},{8,56},{9,... | collective-permute-start | bytes 98312 | tf_op jit(solution)/shard_map/diag/ppermute | solution.py:25
  110.7 5.9 %collective-permute-start.19 = (f32[32,256]{1,0:T(8,128)S(1)}, f32[32,256]{1,0:T(8,128)S(1)}, u32[]{:S(2)}, u32[]{:S(2)}) collective-permute-start(f32[32,256]{1,0:T(8,128)S(1)} %fusion.2), channel_id=1, source_target_pairs={{0,128},{1,129},{2,130},{3,131},{4,132},{5,133},{6,134},{7,135},{8... | collective-permute-start | bytes 98312 | tf_op jit(solution)/shard_map/diag/ppermute | solution.py:25
  116.5 2.7 %collective-permute-start.20 = (f32[32,256]{1,0:T(8,128)S(1)}, f32[32,256]{1,0:T(8,128)S(1)}, u32[]{:S(2)}, u32[]{:S(2)}) collective-permute-start(f32[32,256]{1,0:T(8,128)S(1)} %fusion.2), channel_id=1, source_target_pairs={{0,192},{1,193},{2,194},{3,195},{4,196},{5,197},{6,198},{7,199},{8... | collective-permute-start | bytes 98312 | tf_op jit(solution)/shard_map/diag/ppermute | solution.py:25
  119.2 2.2 %collective-permute-done.20 = f32[32,256]{1,0:T(8,128)S(1)} collective-permute-done((f32[32,256]{1,0:T(8,128)S(1)}, f32[32,256]{1,0:T(8,128)S(1)}, u32[]{:S(2)}, u32[]{:S(2)}) %collective-permute-start.20) | collective-permute-done | bytes 32800 | tf_op jit(solution)/shard_map/diag/ppermute | solution.py:25
  121.4 5.5 %collective-permute-start.26 = (f32[32,256]{1,0:T(8,128)S(1)}, f32[32,256]{1,0:T(8,128)S(1)}, u32[]{:S(2)}, u32[]{:S(2)}) collective-permute-start(f32[32,256]{1,0:T(8,128)S(1)} %add_add_fusion), channel_id=1, source_target_pairs={{0,4},{1,5},{2,6},{3,7},{4,0},{5,1},{6,2},{7,3},{8,12},{9,13},{10,... | collective-permute-start | bytes 98312 | tf_op jit(solution)/shard_map/column/ppermute | solution.py:25
  128.8 3.2 %collective-permute-start.28 = (f32[32,256]{1,0:T(8,128)S(1)}, f32[32,256]{1,0:T(8,128)S(1)}, u32[]{:S(2)}, u32[]{:S(2)}) collective-permute-start(f32[32,256]{1,0:T(8,128)S(1)} %add.209), channel_id=1, source_target_pairs={{0,32},{1,33},{2,34},{3,35},{4,36},{5,37},{6,38},{7,39},{8,40},{9,... | collective-permute-start | bytes 98312 | tf_op jit(solution)/shard_map/back/ppermute | solution.py:25
  134.5 9.5 %collective-permute-start.24 = (s16[2,272,256]{2,1,0:T(8,128)(2,1)S(1)}, s16[2,272,256]{2,1,0:T(8,128)(2,1)S(1)}, u32[]{:S(2)}, u32[]{:S(2)}) collective-permute-start(s16[2,272,256]{2,1,0:T(8,128)(2,1)S(1)} %get-tuple-element.30), channel_id=1, source_target_pairs={{0,4},{1,5},{2,6},{3,7},{4,0},{5,1},{6,2},{7,3},{8,12},{9,13},{10,... | collective-permute-start | bytes 835592 | tf_op jit(solution)/shard_map/column/ppermute | solution.py:25
  144.2 2.3 %collective-permute-start.31 = (f32[128,256]{1,0:T(8,128)S(1)}, f32[128,256]{1,0:T(8,128)S(1)}, u32[]{:S(2)}, u32[]{:S(2)}) collective-permute-start(f32[128,256]{1,0:T(8,128)S(1)} %bitcast.74), channel_id=1, source_target_pairs={{0,2},{1,3},{2,0},{3,1},{4,6},{5,7},{6,4},{7,5},{8,10},{9,11},{10,... | collective-permute-start | bytes 393224 | tf_op jit(solution)/shard_map/back/ppermute | solution.py:25
  148.1 8.9 %collective-permute-done.24 = s16[2,272,256]{2,1,0:T(8,128)(2,1)S(1)} collective-permute-done((s16[2,272,256]{2,1,0:T(8,128)(2,1)S(1)}, s16[2,272,256]{2,1,0:T(8,128)(2,1)S(1)}, u32[]{:S(2)}, u32[]{:S(2)}) %collective-permute-start.24) | collective-permute-done | bytes 278560 | tf_op jit(solution)/shard_map/column/ppermute | solution.py:25
  (108 shorter events, 28.7 us)
Async XLA Ops:
  0.7 38.7 %collective-permute-start.4 = (bf16[4,16,256,256]{3,2,1,0:T(8,128)(2,1)}, bf16[4,16,256,256]{3,2,1,0:T(8,128)(2,1)}, u32[]{:S(2)}, u32[]{:S(2)}) collective-permute-start(bf16[4,16,256,256]{3,2,1,0:T(8,128)(2,1)} %near.3), channel_id=1, source_target_pairs={{0,8},{1,9},{2,10},{3,11},{4,12},{5,13},{6,14},{7,15},{8,0},{9,1},... | collective-permute-start | bytes 25165832 | tf_op jit(solution)/shard_map/swap/ppermute | solution.py:25
  5.8 16.1 %collective-permute-start = (bf16[2,256,256]{2,1,0:T(8,128)(2,1)}, bf16[2,256,256]{2,1,0:T(8,128)(2,1)}, u32[]{:S(2)}, u32[]{:S(2)}) collective-permute-start(bf16[2,256,256]{2,1,0:T(8,128)(2,1)} %fusion), channel_id=1, source_target_pairs={{0,0},{1,8},{2,48},{3,56},{4,128},{5,136},{6,176},{7,184},{8,72},{... | collective-permute-start | bytes 786440 | tf_op jit(solution)/shard_map/spread/ppermute | solution.py:25
  7.7 17.8 %collective-permute-start.1 = (bf16[2,256,256]{2,1,0:T(8,128)(2,1)}, bf16[2,256,256]{2,1,0:T(8,128)(2,1)S(1)}, u32[]{:S(2)}, u32[]{:S(2)}) collective-permute-start(bf16[2,256,256]{2,1,0:T(8,128)(2,1)} %fusion), channel_id=1, source_target_pairs={{0,128},{1,136},{2,176},{3,184},{4,0},{5,8},{6,48},{7,56},{8,200},... | collective-permute-start | bytes 786440 | tf_op jit(solution)/shard_map/spread/ppermute | solution.py:25
  21.8 17.6 %collective-permute-start.5 = (bf16[2,4,256,256]{3,2,1,0:T(8,128)(2,1)}, bf16[2,4,256,256]{3,2,1,0:T(8,128)(2,1)S(1)}, u32[]{:S(2)}, u32[]{:S(2)}) collective-permute-start(bf16[2,4,256,256]{3,2,1,0:T(8,128)(2,1)} %get-tuple-element.37), channel_id=1, source_target_pairs={{0,8},{1,9},{2,10},{3,11},{4,12},{5,13},{6,14},{7,15},{8,0},{9,1},... | collective-permute-start | bytes 3145736 | tf_op jit(solution)/shard_map/swap/ppermute | solution.py:25
  21.8 11.9 %collective-permute-start.2 = (bf16[2,256,256]{2,1,0:T(8,128)(2,1)}, bf16[2,256,256]{2,1,0:T(8,128)(2,1)S(1)}, u32[]{:S(2)}, u32[]{:S(2)}) collective-permute-start(bf16[2,256,256]{2,1,0:T(8,128)(2,1)} %collective-permute-done), channel_id=1, source_target_pairs={{0,64},{1,65},{2,66},{3,67},{4,68},{5,69},{6,70},{7,71},{8,72},{9,... | collective-permute-start | bytes 786440 | tf_op jit(solution)/shard_map/gather/ppermute | solution.py:25
  25.5 13.6 %collective-permute-start.3 = (bf16[2,256,256]{2,1,0:T(8,128)(2,1)S(1)}, bf16[2,256,256]{2,1,0:T(8,128)(2,1)S(1)}, u32[]{:S(2)}, u32[]{:S(2)}) collective-permute-start(bf16[2,256,256]{2,1,0:T(8,128)(2,1)S(1)} %collective-permute-done.1), channel_id=1, source_target_pairs={{0,64},{1,65},{2,66},{3,67},{4,68},{5,69},{6,70},{7,71},{8,72},{9,... | collective-permute-start | bytes 786440 | tf_op jit(solution)/shard_map/gather/ppermute | solution.py:25
  40.3 17.5 %collective-permute-start.6 = (bf16[4,256,256]{2,1,0:T(8,128)(2,1)S(1)}, bf16[4,256,256]{2,1,0:T(8,128)(2,1)S(1)}, u32[]{:S(2)}, u32[]{:S(2)}) collective-permute-start(bf16[4,256,256]{2,1,0:T(8,128)(2,1)S(1)} %get-tuple-element.20.a0), channel_id=1, source_target_pairs={{0,16},{1,17},{2,18},{3,19},{4,20},{5,21},{6,22},{7,23},{8,24},{9,... | collective-permute-start | bytes 1572872 | tf_op jit(solution)/shard_map/gather/ppermute | solution.py:25
  40.3 31.2 %collective-permute-start.8 = (bf16[4,256,256]{2,1,0:T(8,128)(2,1)S(1)}, bf16[4,256,256]{2,1,0:T(8,128)(2,1)S(1)}, u32[]{:S(2)}, u32[]{:S(2)}) collective-permute-start(bf16[4,256,256]{2,1,0:T(8,128)(2,1)S(1)} %get-tuple-element.20.a0), channel_id=1, source_target_pairs={{0,48},{1,49},{2,50},{3,51},{4,52},{5,53},{6,54},{7,55},{8,56},{9,... | collective-permute-start | bytes 1572872 | tf_op jit(solution)/shard_map/gather/ppermute | solution.py:25
  46.4 25.1 %collective-permute-start.7 = (bf16[4,256,256]{2,1,0:T(8,128)(2,1)S(1)}, bf16[4,256,256]{2,1,0:T(8,128)(2,1)}, u32[]{:S(2)}, u32[]{:S(2)}) collective-permute-start(bf16[4,256,256]{2,1,0:T(8,128)(2,1)S(1)} %get-tuple-element.21.b0), channel_id=1, source_target_pairs={{0,16},{1,17},{2,18},{3,19},{4,20},{5,21},{6,22},{7,23},{8,24},{9,... | collective-permute-start | bytes 1572872 | tf_op jit(solution)/shard_map/gather/ppermute | solution.py:25
  46.4 21.6 %collective-permute-start.9 = (bf16[4,256,256]{2,1,0:T(8,128)(2,1)S(1)}, bf16[4,256,256]{2,1,0:T(8,128)(2,1)}, u32[]{:S(2)}, u32[]{:S(2)}) collective-permute-start(bf16[4,256,256]{2,1,0:T(8,128)(2,1)S(1)} %get-tuple-element.21.b0), channel_id=1, source_target_pairs={{0,48},{1,49},{2,50},{3,51},{4,52},{5,53},{6,54},{7,55},{8,56},{9,... | collective-permute-start | bytes 1572872 | tf_op jit(solution)/shard_map/gather/ppermute | solution.py:25
  57.8 26.1 %collective-permute-start.10 = (bf16[4,256,256]{2,1,0:T(8,128)(2,1)S(1)}, bf16[4,256,256]{2,1,0:T(8,128)(2,1)S(1)}, u32[]{:S(2)}, u32[]{:S(2)}) collective-permute-start(bf16[4,256,256]{2,1,0:T(8,128)(2,1)S(1)} %collective-permute-done.6.a1), channel_id=1, source_target_pairs={{0,16},{1,17},{2,18},{3,19},{4,20},{5,21},{6,22},{7,23},{8,24},{9,... | collective-permute-start | bytes 1572872 | tf_op jit(solution)/shard_map/gather/ppermute | solution.py:25
  68.0 16.0 %collective-permute-start.11 = (bf16[4,256,256]{2,1,0:T(8,128)(2,1)}, bf16[4,256,256]{2,1,0:T(8,128)(2,1)S(1)}, u32[]{:S(2)}, u32[]{:S(2)}) collective-permute-start(bf16[4,256,256]{2,1,0:T(8,128)(2,1)} %collective-permute-done.9.b2), channel_id=1, source_target_pairs={{0,48},{1,49},{2,50},{3,51},{4,52},{5,53},{6,54},{7,55},{8,56},{9,... | collective-permute-start | bytes 1572872 | tf_op jit(solution)/shard_map/gather/ppermute | solution.py:25
  96.8 8.2 %collective-permute-start.14 = (f32[128,256]{1,0:T(8,128)S(1)}, f32[128,256]{1,0:T(8,128)S(1)}, u32[]{:S(2)}, u32[]{:S(2)}) collective-permute-start(f32[128,256]{1,0:T(8,128)S(1)} %get-tuple-element.46), channel_id=1, source_target_pairs={{0,3},{1,2},{2,1},{3,0},{4,7},{5,6},{6,5},{7,4},{8,11},{9,10},{10,... | collective-permute-start | bytes 393224 | tf_op jit(solution)/shard_map/diag/ppermute | solution.py:25
  100.4 21.0 %collective-permute-start.21 = (s16[2,2,272,256]{3,2,1,0:T(8,128)(2,1)}, s16[2,2,272,256]{3,2,1,0:T(8,128)(2,1)S(1)}, u32[]{:S(2)}, u32[]{:S(2)}) collective-permute-start(s16[2,2,272,256]{3,2,1,0:T(8,128)(2,1)} %copy-done.2), channel_id=1, source_target_pairs={{0,1},{1,0},{2,3},{3,2},{4,5},{5,4},{6,7},{7,6},{8,9},{9,8},{10,11... | collective-permute-start | bytes 1671176 | tf_op jit(solution)/shard_map/column/ppermute | solution.py:25
  109.0 23.1 %collective-permute-start.22 = (s16[2,2,272,256]{3,2,1,0:T(8,128)(2,1)}, s16[2,2,272,256]{3,2,1,0:T(8,128)(2,1)S(1)}, u32[]{:S(2)}, u32[]{:S(2)}) collective-permute-start(s16[2,2,272,256]{3,2,1,0:T(8,128)(2,1)} %copy-done.1), channel_id=1, source_target_pairs={{0,2},{1,3},{2,0},{3,1},{4,6},{5,7},{6,4},{7,5},{8,10},{9,11},{10,... | collective-permute-start | bytes 1671176 | tf_op jit(solution)/shard_map/column/ppermute | solution.py:25
  109.0 24.8 %collective-permute-start.23 = (s16[2,2,272,256]{3,2,1,0:T(8,128)(2,1)}, s16[2,2,272,256]{3,2,1,0:T(8,128)(2,1)S(1)}, u32[]{:S(2)}, u32[]{:S(2)}) collective-permute-start(s16[2,2,272,256]{3,2,1,0:T(8,128)(2,1)} %copy-done), channel_id=1, source_target_pairs={{0,3},{1,2},{2,1},{3,0},{4,7},{5,6},{6,5},{7,4},{8,11},{9,10},{10,... | collective-permute-start | bytes 1671176 | tf_op jit(solution)/shard_map/column/ppermute | solution.py:25
  110.7 8.6 %collective-permute-start.19 = (f32[32,256]{1,0:T(8,128)S(1)}, f32[32,256]{1,0:T(8,128)S(1)}, u32[]{:S(2)}, u32[]{:S(2)}) collective-permute-start(f32[32,256]{1,0:T(8,128)S(1)} %fusion.2), channel_id=1, source_target_pairs={{0,128},{1,129},{2,130},{3,131},{4,132},{5,133},{6,134},{7,135},{8... | collective-permute-start | bytes 98312 | tf_op jit(solution)/shard_map/diag/ppermute | solution.py:25
  128.2 15.8 %collective-permute-start.27 = (f32[32,256]{1,0:T(8,128)S(1)}, f32[32,256]{1,0:T(8,128)S(1)}, u32[]{:S(2)}, u32[]{:S(2)}) collective-permute-start(f32[32,256]{1,0:T(8,128)S(1)} %add.209), channel_id=1, source_target_pairs={{0,16},{1,17},{2,18},{3,19},{4,20},{5,21},{6,22},{7,23},{8,24},{9,... | collective-permute-start | bytes 98312 | tf_op jit(solution)/shard_map/back/ppermute | solution.py:25
  128.8 15.2 %collective-permute-start.28 = (f32[32,256]{1,0:T(8,128)S(1)}, f32[32,256]{1,0:T(8,128)S(1)}, u32[]{:S(2)}, u32[]{:S(2)}) collective-permute-start(f32[32,256]{1,0:T(8,128)S(1)} %add.209), channel_id=1, source_target_pairs={{0,32},{1,33},{2,34},{3,35},{4,36},{5,37},{6,38},{7,39},{8,40},{9,... | collective-permute-start | bytes 98312 | tf_op jit(solution)/shard_map/back/ppermute | solution.py:25
  132.0 12.1 %collective-permute-start.29 = (f32[32,256]{1,0:T(8,128)S(1)}, f32[32,256]{1,0:T(8,128)S(1)}, u32[]{:S(2)}, u32[]{:S(2)}) collective-permute-start(f32[32,256]{1,0:T(8,128)S(1)} %add.209), channel_id=1, source_target_pairs={{0,48},{1,49},{2,50},{3,51},{4,52},{5,53},{6,54},{7,55},{8,56},{9,... | collective-permute-start | bytes 98312 | tf_op jit(solution)/shard_map/back/ppermute | solution.py:25
  134.5 22.4 %collective-permute-start.24 = (s16[2,272,256]{2,1,0:T(8,128)(2,1)S(1)}, s16[2,272,256]{2,1,0:T(8,128)(2,1)S(1)}, u32[]{:S(2)}, u32[]{:S(2)}) collective-permute-start(s16[2,272,256]{2,1,0:T(8,128)(2,1)S(1)} %get-tuple-element.30), channel_id=1, source_target_pairs={{0,4},{1,5},{2,6},{3,7},{4,0},{5,1},{6,2},{7,3},{8,12},{9,13},{10,... | collective-permute-start | bytes 835592 | tf_op jit(solution)/shard_map/column/ppermute | solution.py:25
  144.1 14.0 %collective-permute-start.30 = (f32[128,256]{1,0:T(8,128)S(1)}, f32[128,256]{1,0:T(8,128)S(1)}, u32[]{:S(2)}, u32[]{:S(2)}) collective-permute-start(f32[128,256]{1,0:T(8,128)S(1)} %bitcast.73), channel_id=1, source_target_pairs={{0,1},{1,0},{2,3},{3,2},{4,5},{5,4},{6,7},{7,6},{8,9},{9,8},{10,11... | collective-permute-start | bytes 393224 | tf_op jit(solution)/shard_map/back/ppermute | solution.py:25
  144.2 13.9 %collective-permute-start.31 = (f32[128,256]{1,0:T(8,128)S(1)}, f32[128,256]{1,0:T(8,128)S(1)}, u32[]{:S(2)}, u32[]{:S(2)}) collective-permute-start(f32[128,256]{1,0:T(8,128)S(1)} %bitcast.74), channel_id=1, source_target_pairs={{0,2},{1,3},{2,0},{3,1},{4,6},{5,7},{6,4},{7,5},{8,10},{9,11},{10,... | collective-permute-start | bytes 393224 | tf_op jit(solution)/shard_map/back/ppermute | solution.py:25
  146.5 11.6 %collective-permute-start.32 = (f32[128,256]{1,0:T(8,128)S(1)}, f32[128,256]{1,0:T(8,128)S(1)}, u32[]{:S(2)}, u32[]{:S(2)}) collective-permute-start(f32[128,256]{1,0:T(8,128)S(1)} %bitcast.75), channel_id=1, source_target_pairs={{0,3},{1,2},{2,1},{3,0},{4,7},{5,6},{6,5},{7,4},{8,11},{9,10},{10,... | collective-permute-start | bytes 393224 | tf_op jit(solution)/shard_map/back/ppermute | solution.py:25
  (20 other events, 317.4 us)
